TPU v7x, 128 devices: a whole 4x4x4 slice. The times are simulated.
128 devices in a mesh: dp: 32 (over z, x, y_lo), tensor: 4 (over y_hi, core).
Axes of the slice: x: 4, y: 4 (y_hi: 2, y_lo: 2; y = y_hi * 2 + y_lo), z: 4, core: 2. Of those that a mesh axis runs over, the one named last changes fastest.
Arguments:
- acts: bfloat16 [16384, 4096], P(('dp', 'tensor')), may hold values from -6 to 6
- out_grad: bfloat16 [16384, 16384], P('dp', 'tensor'), may hold values from -0.09375 to 0.09375
- projector: bfloat16 [4096, 512], replicated, may hold values from -0.09375 to 0.09375
- weight: bfloat16 [4096, 16384], P('dp', 'tensor'), may hold values from -6 to 6
- first_moment: float32 [4, 4096, 512], P('tensor', 'dp'), may hold values from -4 to 4
- second_moment: float32 [4, 4096, 512], P('tensor', 'dp'), may hold values from 0.01 to 1
Outputs:
- new_weight: bfloat16 [4096, 16384], P('dp', 'tensor')
- new_first: float32 [4, 4096, 512], P('tensor', 'dp')
- new_second: float32 [4, 4096, 512], P('tensor', 'dp')
All inputs are finite; a program needn't handle non-finite values.
Results may differ from a plain program's by a relative error of at most 0.015.
Values may be sent and summed in bfloat16 or wider, within the bound.
A program may use at most 128 MiB of HBM per device.

v0:
```python
import jax
import jax.numpy as jnp
from jax import lax
from jax.sharding import PartitionSpec as P

beta_first = 0.9
beta_second = 0.95
adam_step = 10
epsilon = 1e-08
step_rate = 0.5


def adam_moments(lowgrad, first_moment, second_moment):
    new_first = beta_first * first_moment + (1.0 - beta_first) * lowgrad
    new_second = beta_second * second_moment + (1.0 - beta_second) * lowgrad * lowgrad
    corrected_first = new_first / (1.0 - beta_first**adam_step)
    corrected_second = new_second / (1.0 - beta_second**adam_step)
    direction = (corrected_first / (jnp.sqrt(corrected_second) + epsilon)).astype(jnp.bfloat16)
    return (new_first, new_second, direction)


def per_device(acts, out_grad, projector, weight, first_moment, second_moment):
    whole_acts = lax.all_gather(acts, "tensor", axis=0, tiled=True)
    owned_grad = lax.psum_scatter(
        lax.dot_general(
            out_grad, whole_acts, (((0,), (0,)), ((), ())), preferred_element_type=jnp.float32
        ).astype(jnp.bfloat16),
        "dp",
        scatter_dimension=0,
        tiled=True,
    ).astype(jnp.float32)
    lowgrad = jnp.dot(
        owned_grad,
        projector.astype(jnp.float32),
        precision=lax.Precision.HIGHEST,
        preferred_element_type=jnp.float32,
    )
    new_first, new_second, direction = adam_moments(lowgrad, first_moment[0], second_moment[0])
    owned_update = lax.dot_general(
        projector, direction, (((1,), (1,)), ((), ())), preferred_element_type=jnp.float32
    ).astype(jnp.bfloat16)
    update = lax.all_to_all(owned_update, "dp", split_axis=0, concat_axis=1, tiled=True)
    new_weight = (weight.astype(jnp.float32) - step_rate * update.astype(jnp.float32)).astype(
        jnp.bfloat16
    )
    return (new_weight, new_first[None], new_second[None])


def solution(mesh):
    return jax.shard_map(
        per_device,
        mesh=mesh,
        in_specs=(
            P(("dp", "tensor"), None),
            P("dp", "tensor"),
            P(),
            P("dp", "tensor"),
            P("tensor", "dp", None),
            P("tensor", "dp", None),
        ),
        out_specs=(P("dp", "tensor"), P("tensor", "dp", None), P("tensor", "dp", None)),
        check_vma=False,
    )
```

profile of v0, /device:TPU:0, one launch (start us, length us, event | category | flops | bytes accessed | tf_op | source)
XLA Modules:
  0.0 826.6 jit_solution(7803383295628024617)
XLA Ops:
  7.2 0.0 all-gather.2.cloned.1.call-start
  7.2 0.7 all-gather.2.cloned.1.call-update
  7.9 0.0 reduce-scatter.2.cloned.1.call-start
  7.9 42.8 %all-gather.2.cloned.1.call-done = bf16[512,4096]{1,0:T(8,128)(2,1)} async-done(((bf16[128,4096]{1,0:T(8,128)(2,1)}), bf16[512,4096]{1,0:T(8,128)(2,1)}) %all-gather.2.cloned.1.call-update) | async-done | bytes 4194320 | tf_op jit(solution)/shard_map/all_gather | solution.py:23
  50.7 24.1 %convolution_convert_fusion = bf16[4096,4096]{1,0:T(8,128)(2,1)} fusion(bf16[512,4096]{1,0:T(8,128)(2,1)} %param.7, bf16[512,4096]{1,0:T(8,128)(2,1)} %all-gather.2.cloned.1.call-done), kind=kOutput, calls=%fused_computation | convolution fusion | flops 17196646400 | bytes 41943040 | tf_op jit(solution)/shard_map/dot_general | solution.py:25
  74.8 0.0 reduce-scatter.2.cloned.1.call-update
  74.9 0.0 copy-start.1
  74.9 0.0 copy-start.2
  74.9 708.0 %reduce-scatter.2.cloned.1.call-done = bf16[128,4096]{1,0:T(8,128)(2,1)} async-done(((bf16[4096,4096]{1,0:T(8,128)(2,1)}), bf16[128,4096]{1,0:T(8,128)(2,1)}) %reduce-scatter.2.cloned.1.call-update) | async-done | bytes 1048592 | tf_op jit(solution)/shard_map/reduce_scatter | solution.py:24
  782.9 0.0 copy-start
  782.9 3.4 fusion.15
  786.2 0.0 copy-done.1
  786.3 0.0 copy-done.2
  786.3 0.3 copy-done
  786.6 1.4 fusion
  788.1 1.3 copy.14
  789.3 7.3 all-to-all-start
  796.6 0.9 fusion.6
  797.5 17.2 %all-to-all-done = bf16[32,128,128]{1,2,0:T(8,128)(2,1)S(1)} async-done(((bf16[32,128,128]{1,2,0:T(8,128)(2,1)}), bf16[32,128,128]{1,2,0:T(8,128)(2,1)S(1)}, u32[]{:S(2)}, u32[]{:S(2)}) %all-to-all-start) | async-done | bytes 1048608 | tf_op jit(solution)/shard_map/all_to_all | solution.py:42
  814.7 0.2 convert_multiply_fusion
  814.9 1.9 copy.11
  816.8 3.0 subtract_convert_fusion
Async XLA Ops:
  7.2 43.5 %all-gather.2.cloned.1.call-start = ((), (), s32[]{:S(2)}) async-start(), calls=%async_computation.2 | async-start | bytes 5242880 | tf_op jit(solution)/shard_map/all_gather | solution.py:23
  7.9 775.0 %reduce-scatter.2.cloned.1.call-start = ((), (), s32[]{:S(2)}) async-start(), calls=%async_computation.3 | async-start | bytes 34603008 | tf_op jit(solution)/shard_map/reduce_scatter | solution.py:24
  74.9 711.4 %copy-start.1 = (f32[1,128,512]{2,1,0:T(8,128)S(1)}, f32[1,128,512]{2,1,0:T(8,128)}, u32[]{:S(2)}) copy-start(f32[1,128,512]{2,1,0:T(8,128)} %param.10) | copy-start | bytes 786436
  74.9 711.4 %copy-start.2 = (f32[1,128,512]{2,1,0:T(8,128)S(1)}, f32[1,128,512]{2,1,0:T(8,128)}, u32[]{:S(2)}) copy-start(f32[1,128,512]{2,1,0:T(8,128)} %param.11) | copy-start | bytes 786436
  782.9 3.7 copy-start
  789.3 25.3 %all-to-all-start = ((bf16[32,128,128]{1,2,0:T(8,128)(2,1)}), bf16[32,128,128]{1,2,0:T(8,128)(2,1)S(1)}, u32[]{:S(2)}, u32[]{:S(2)}) async-start(bf16[32,128,128]{1,2,0:T(8,128)(2,1)} %bitcast.31), calls=%async_computation.1 | async-start | bytes 2097152 | tf_op jit(solution)/shard_map/all_to_all | solution.py:42
Sparse Core Ops, SparseCore 0:
  9.7 40.9 all-gather.1
  75.0 707.8 reduce-scatter.1
where the time goes:
time: 827 us
  waiting for transfers between devices  769 us (93%)
  matrix products  29 us (4%)
  between operations  14.1 us (2%)
    reduce_scatter x1, waiting for transfers between devices, per_device(): lax.psum_scatter(lax.dot_general(out_grad, whole_acts, (((0,), (0,)), (()...  708 us
    all_gather x1, waiting for transfers between devices, per_device(): whole_acts = lax.all_gather(acts, 'tensor', axis=0, tiled=True)  42.8 us
    dot_general x1, matrix products, per_device(): lax.dot_general(out_grad, whole_acts, (((0,), (0,)), ((), ())), preferred...  24.1 us
    all_to_all x1, waiting for transfers between devices, per_device(): lax.all_to_all(owned_update, 'dp', split_axis=0, concat_axis=1, tiled=True)  17.2 us
  transfers between devices with their start and end apart: 3, of which 3 were waited for; matrix products, arithmetic and copies ran while one was open for 0% of the time, Pallas kernels for 0%

commit v1 on v0

--- a/solution.py
+++ b/solution.py
@@ -20,21 +20,26 @@
 
 
 def per_device(acts, out_grad, projector, weight, first_moment, second_moment):
-    whole_acts = lax.all_gather(acts, "tensor", axis=0, tiled=True)
-    owned_grad = lax.psum_scatter(
-        lax.dot_general(
-            out_grad, whole_acts, (((0,), (0,)), ((), ())), preferred_element_type=jnp.float32
-        ).astype(jnp.bfloat16),
+    token_proj = jnp.dot(acts, projector, preferred_element_type=jnp.float32)
+    peers = lax.axis_size("tensor")
+    whole_proj = lax.all_to_all(
+        jnp.tile(token_proj, (peers, 1)), "tensor", split_axis=0, concat_axis=0, tiled=True
+    )
+    proj_hi = whole_proj.astype(jnp.bfloat16)
+    proj_lo = (whole_proj - proj_hi.astype(jnp.float32)).astype(jnp.bfloat16)
+    dims = (((0,), (0,)), ((), ()))
+    partial = lax.dot_general(
+        out_grad, proj_hi, dims, preferred_element_type=jnp.float32
+    ) + lax.dot_general(out_grad, proj_lo, dims, preferred_element_type=jnp.float32)
+    owners = lax.axis_size("dp")
+    blocks = lax.all_to_all(
+        partial.astype(jnp.bfloat16).reshape(owners, -1, partial.shape[1]),
         "dp",
-        scatter_dimension=0,
+        split_axis=0,
+        concat_axis=0,
         tiled=True,
-    ).astype(jnp.float32)
-    lowgrad = jnp.dot(
-        owned_grad,
-        projector.astype(jnp.float32),
-        precision=lax.Precision.HIGHEST,
-        preferred_element_type=jnp.float32,
     )
+    lowgrad = jnp.sum(blocks.astype(jnp.float32), axis=0)
     new_first, new_second, direction = adam_moments(lowgrad, first_moment[0], second_moment[0])
     owned_update = lax.dot_general(
         projector, direction, (((1,), (1,)), ((), ())), preferred_element_type=jnp.float32

time: 827 us -> 133 us (0.16)
  waiting for transfers between devices: 769 us -> 69.7 us
  blocking collectives: 0 us -> 20.3 us
  matrix products: 29 us -> 9.95 us
  between operations: 14.1 us -> 0.76 us
    reduce_scatter x1 -> x0, waiting for transfers between devices: 708 us -> none  [per_device(): lax.psum_scatter(lax.dot_general(out_grad, whole_acts, (((0,), (0,)), (()...]
    all_to_all x0 -> x1, waiting for transfers between devices: none -> 53.6 us  [per_device(): lax.all_to_all(partial.astype(jnp.bfloat16).reshape(owners, -1, partial.s...]
    all_gather x1 -> x0, waiting for transfers between devices: 42.8 us -> none  [per_device(): whole_acts = lax.all_gather(acts, 'tensor', axis=0, tiled=True)]
    all_to_all x0 -> x1, blocking collectives: none -> 20.3 us  [per_device(): lax.all_to_all(jnp.tile(token_proj, (peers, 1)), 'tensor', split_axis=0,...]
    dot_general x2 -> x3, matrix products: 27.5 us -> 8.36 us  [the longest x1 3.24 us: per_device(): token_proj = jnp.dot(acts, projector, preferred_element_type=jnp.float32)]
    all_to_all x0 -> x1, starting transfers between devices: none -> 8.54 us  [per_device(): lax.all_to_all(partial.astype(jnp.bfloat16).reshape(owners, -1, partial.s...]
  transfers between devices with their start and end apart: 3 -> 2, of which waited for: 3 -> 2; matrix products, arithmetic and copies ran while one was open for 0% -> 2% of each run, Pallas kernels for 0% -> 0%
where the time goes in v1:
time: 133 us
  waiting for transfers between devices  69.7 us (52%)
  blocking collectives  20.3 us (15%)
  starting transfers between devices  14.4 us (11%)
  local copies, waits for them, and re-layouts  10.1 us (8%)
  matrix products  9.95 us (7%)
  other arithmetic  7.59 us (6%)
    all_to_all x1, waiting for transfers between devices, per_device(): lax.all_to_all(partial.astype(jnp.bfloat16).reshape(owners, -1, partial.s...  53.6 us
    all_to_all x1, blocking collectives, per_device(): lax.all_to_all(jnp.tile(token_proj, (peers, 1)), 'tensor', split_axis=0,...  20.3 us
    all_to_all x1, waiting for transfers between devices, per_device(): lax.all_to_all(owned_update, 'dp', split_axis=0, concat_axis=1, tiled=True)  16.1 us
    all_to_all x1, starting transfers between devices, per_device(): lax.all_to_all(partial.astype(jnp.bfloat16).reshape(owners, -1, partial.s...  8.54 us
    all_to_all x1, starting transfers between devices, per_device(): lax.all_to_all(owned_update, 'dp', split_axis=0, concat_axis=1, tiled=True)  5.82 us
    unnamed x14, local copies, waits for them, and re-layouts  3.65 us
    dot_general x1, matrix products, per_device(): token_proj = jnp.dot(acts, projector, preferred_element_type=jnp.float32)  3.24 us
    reshape x1, local copies, waits for them, and re-layouts, per_device(): partial.astype(jnp.bfloat16).reshape(owners, -1, partial.shape[1])  3.15 us
  transfers between devices with their start and end apart: 2, of which 2 were waited for; matrix products, arithmetic and copies ran while one was open for 2% of the time, Pallas kernels for 0%

profile of v1, /device:TPU:0, one launch (start us, length us, event | category | flops | bytes accessed | tf_op | source)
XLA Modules:
  0.0 132.7 jit_solution(2327064367462858731)
XLA Ops:
  0.7 1.2 copy-done
  1.9 3.2 %fusion.27 = f32[128,512]{1,0:T(8,128)S(1)} fusion(bf16[128,4096]{1,0:T(8,128)(2,1)S(1)} %copy-done, bf16[4096,512]{1,0:T(8,128)(2,1)} %param.8), kind=kOutput, calls=%fused_computation.39 | convolution fusion | flops 536870912 | bytes 5505024 | tf_op jit(solution)/shard_map/dot_general | solution.py:23
  5.1 0.1 tile.2
  5.2 20.3 %all_to_all.27 = f32[4,128,512]{2,1,0:T(8,128)S(1)} all-to-all(f32[4,128,512]{2,1,0:T(8,128)S(1)} %tile.2), channel_id=1, replica_groups=mesh['dp'=32,'tensor'=4] {'tensor'}, dimensions={0} | all-to-all | bytes 2097152 | tf_op jit(solution)/shard_map/all_to_all | solution.py:25
  25.5 0.1 fusion.2
  25.6 2.4 %fusion.28 = f32[512,4096]{1,0:T(8,128)S(1)} fusion(bf16[512,512]{1,0:T(8,128)(2,1)S(1)} %get-tuple-element.7, bf16[512,4096]{1,0:T(8,128)(2,1)S(1)} %copy-done.1), kind=kOutput, calls=%fused_computation.40 | convolution fusion | flops 2147483648 | bytes 13107200 | tf_op jit(solution)/shard_map/dot_general | solution.py:31
  28.0 2.7 %fusion = bf16[64,32,8,128]{3,2,1,0:T(8,128)(2,1)S(1)} fusion(f32[512,4096]{1,0:T(8,128)S(1)} %fusion.28, bf16[512,512]{1,0:T(8,128)(2,1)S(1)} %get-tuple-element.6, bf16[512,4096]{1,0:T(8,128)(2,1)S(1)} %copy-done.1), kind=kOutput, calls=%fused_computation.4 | convolution fusion | flops 2151677952 | bytes 17301504 | tf_op jit(solution)/shard_map/dot_general | solution.py:33
  30.8 3.1 %copy.23 = bf16[64,32,8,128]{3,2,0,1:T(8,128)(2,1)} copy(bf16[64,32,8,128]{3,2,1,0:T(8,128)(2,1)S(1)} %fusion) | data formatting | bytes 8388608 | tf_op jit(solution)/shard_map/reshape | solution.py:36
  33.9 8.5 %all-to-all-start.1 = ((bf16[32,128,512]{1,2,0:T(8,128)(2,1)}), bf16[32,128,512]{1,2,0:T(8,128)(2,1)}, u32[]{:S(2)}, u32[]{:S(2)}) async-start(bf16[32,128,512]{1,2,0:T(8,128)(2,1)} %bitcast.47), calls=%async_computation.1 | async-start | bytes 8388608 | tf_op jit(solution)/shard_map/all_to_all | solution.py:35
  42.5 0.1 copy.10
  42.6 0.1 copy.13
  42.8 53.6 %all-to-all-done.1 = bf16[32,128,512]{1,2,0:T(8,128)(2,1)} async-done(((bf16[32,128,512]{1,2,0:T(8,128)(2,1)}), bf16[32,128,512]{1,2,0:T(8,128)(2,1)}, u32[]{:S(2)}, u32[]{:S(2)}) %all-to-all-start.1) | async-done | bytes 4194336 | tf_op jit(solution)/shard_map/all_to_all | solution.py:35
  96.4 2.9 %convert_reduce_fusion = f32[128,512]{0,1:T(8,128)S(1)} fusion(bf16[32,128,512]{1,2,0:T(8,128)(2,1)} %all-to-all-done.1), kind=kLoop, calls=%fused_computation | loop fusion | flops 4128768 | bytes 4456448 | tf_op jit(solution)/shard_map/reduce_sum | solution.py:42
  99.3 0.5 copy-done.2
  99.8 1.6 %fusion.1 = bf16[16,32,8,128]{3,2,1,0:T(8,128)(2,1)S(1)} fusion(bf16[4096,512]{1,0:T(8,128)(2,1)S(1)} %copy-done.2, f32[128,512]{0,1:T(8,128)S(1)} %convert_reduce_fusion, f32[1,128,512]{1,2,0:T(8,128)S(1)} %copy.13, f32[1,128,512]{1,2,0:T(8,128)S(1)} %copy.10), kind=kOutput, calls=%fused_computation.7 | convolution fusion | flops 538181632 | bytes 6029312 | tf_op jit(solution)/shard_map/dot_general | solution.py:44
  101.4 1.3 copy.24
  102.7 5.8 %all-to-all-start.2 = ((bf16[32,128,128]{1,2,0:T(8,128)(2,1)}), bf16[32,128,128]{1,2,0:T(8,128)(2,1)}, u32[]{:S(2)}, u32[]{:S(2)}) async-start(bf16[32,128,128]{1,2,0:T(8,128)(2,1)} %bitcast.46), calls=%async_computation.2 | async-start | bytes 2097152 | tf_op jit(solution)/shard_map/all_to_all | solution.py:47
  108.5 0.1 fusion.8
  108.6 0.8 copy.16
  109.5 0.8 copy.17
  110.3 16.1 %all-to-all-done.2 = bf16[32,128,128]{1,2,0:T(8,128)(2,1)} async-done(((bf16[32,128,128]{1,2,0:T(8,128)(2,1)}), bf16[32,128,128]{1,2,0:T(8,128)(2,1)}, u32[]{:S(2)}, u32[]{:S(2)}) %all-to-all-start.2) | async-done | bytes 1048608 | tf_op jit(solution)/shard_map/all_to_all | solution.py:47
  126.3 1.5 %convert_multiply_fusion = f32[32,128,128]{1,2,0:T(8,128)S(1)} fusion(bf16[32,128,128]{1,2,0:T(8,128)(2,1)} %all-to-all-done.2), kind=kLoop, calls=%fused_computation.6 | loop fusion | flops 1048576 | bytes 3145728 | tf_op jit(solution)/shard_map/mul | solution.py:48
  127.8 1.9 %copy.15 = f32[128,4096]{1,0:T(8,128)} copy(f32[128,4096]{0,1:T(8,128)S(1)} %bitcast.48) | data formatting | bytes 4194304 | tf_op jit(solution)/shard_map/mul | solution.py:48
  129.7 3.0 %subtract_convert_fusion = bf16[128,4096]{1,0:T(8,128)(2,1)} fusion(f32[128,4096]{1,0:T(8,128)} %copy.15, bf16[128,4096]{1,0:T(8,128)(2,1)} %param.9), kind=kLoop, calls=%fused_computation.5 | loop fusion | flops 1572864 | bytes 4194304 | tf_op jit(solution)/shard_map/convert_element_type | solution.py:48
  (8 shorter events, 0.0 us)
Async XLA Ops:
  0.6 1.2 copy-start
  0.6 25.0 %copy-start.1 = (bf16[512,4096]{1,0:T(8,128)(2,1)S(1)}, bf16[512,4096]{1,0:T(8,128)(2,1)}, u32[]{:S(2)}) copy-start(bf16[512,4096]{1,0:T(8,128)(2,1)} %param.7) | copy-start | bytes 12582916
  33.9 8.6 %copy-start.3 = (f32[1,128,512]{2,1,0:T(8,128)S(1)}, f32[1,128,512]{2,1,0:T(8,128)}, u32[]{:S(2)}) copy-start(f32[1,128,512]{2,1,0:T(8,128)} %param.10) | copy-start | bytes 786436
  33.9 8.7 %copy-start.4 = (f32[1,128,512]{2,1,0:T(8,128)S(1)}, f32[1,128,512]{2,1,0:T(8,128)}, u32[]{:S(2)}) copy-start(f32[1,128,512]{2,1,0:T(8,128)} %param.11) | copy-start | bytes 786436
  33.9 62.5 %all-to-all-start.1 = ((bf16[32,128,512]{1,2,0:T(8,128)(2,1)}), bf16[32,128,512]{1,2,0:T(8,128)(2,1)}, u32[]{:S(2)}, u32[]{:S(2)}) async-start(bf16[32,128,512]{1,2,0:T(8,128)(2,1)} %bitcast.47), calls=%async_computation.1 | async-start | bytes 8388608 | tf_op jit(solution)/shard_map/all_to_all | solution.py:35
  96.4 3.4 %copy-start.2 = (bf16[4096,512]{1,0:T(8,128)(2,1)S(1)}, bf16[4096,512]{1,0:T(8,128)(2,1)}, u32[]{:S(2)}) copy-start(bf16[4096,512]{1,0:T(8,128)(2,1)} %param.8) | copy-start | bytes 12582916
  102.7 23.6 %all-to-all-start.2 = ((bf16[32,128,128]{1,2,0:T(8,128)(2,1)}), bf16[32,128,128]{1,2,0:T(8,128)(2,1)}, u32[]{:S(2)}, u32[]{:S(2)}) async-start(bf16[32,128,128]{1,2,0:T(8,128)(2,1)} %bitcast.46), calls=%async_computation.2 | async-start | bytes 2097152 | tf_op jit(solution)/shard_map/all_to_all | solution.py:47

commit v2 on v1

--- a/solution.py
+++ b/solution.py
@@ -1,6 +1,10 @@
+import functools
+
 import jax
 import jax.numpy as jnp
 from jax import lax
+from jax.experimental import pallas as pl
+from jax.experimental.pallas import tpu as pltpu
 from jax.sharding import PartitionSpec as P
 
 beta_first = 0.9
@@ -8,6 +12,8 @@
 adam_step = 10
 epsilon = 1e-08
 step_rate = 0.5
+
+MESH_ID = pl.DeviceIdType.MESH
 
 
 def adam_moments(lowgrad, first_moment, second_moment):
@@ -17,6 +23,52 @@
     corrected_second = new_second / (1.0 - beta_second**adam_step)
     direction = (corrected_first / (jnp.sqrt(corrected_second) + epsilon)).astype(jnp.bfloat16)
     return (new_first, new_second, direction)
+
+
+def exchange_sum_kernel(n, part_ref, out_ref, recv, send_sem, recv_sem):
+    me = lax.axis_index("dp")
+    col = lax.axis_index("tensor")
+    barrier = pltpu.get_barrier_semaphore()
+    for k in range(1, n):
+        pl.semaphore_signal(
+            barrier, inc=1, device_id=(lax.rem(me + k, n), col), device_id_type=MESH_ID
+        )
+    pl.semaphore_wait(barrier, n - 1)
+    copies = []
+    for k in range(1, n):
+        dest = lax.rem(me + k, n)
+        copy = pltpu.make_async_remote_copy(
+            src_ref=part_ref.at[dest],
+            dst_ref=recv.at[k],
+            send_sem=send_sem.at[k],
+            recv_sem=recv_sem.at[k],
+            device_id=(dest, col),
+            device_id_type=MESH_ID,
+        )
+        copy.start()
+        copies.append(copy)
+    out_ref[...] = part_ref[me].astype(jnp.float32)
+    for k, copy in enumerate(copies, 1):
+        copy.wait()
+        out_ref[...] += recv[k].astype(jnp.float32)
+
+
+def exchange_sum(part):
+    n, rows, cols = part.shape
+    return pl.pallas_call(
+        functools.partial(exchange_sum_kernel, n),
+        out_shape=jax.ShapeDtypeStruct((rows, cols), jnp.float32),
+        in_specs=[pl.BlockSpec(memory_space=pltpu.VMEM)],
+        out_specs=pl.BlockSpec(memory_space=pltpu.VMEM),
+        scratch_shapes=[
+            pltpu.VMEM((n, rows, cols), part.dtype),
+            pltpu.SemaphoreType.DMA((n,)),
+            pltpu.SemaphoreType.DMA((n,)),
+        ],
+        compiler_params=pltpu.CompilerParams(
+            collective_id=0, has_side_effects=True, vmem_limit_bytes=48 * 1024 * 1024
+        ),
+    )(part)
 
 
 def per_device(acts, out_grad, projector, weight, first_moment, second_moment):
@@ -32,14 +84,7 @@
         out_grad, proj_hi, dims, preferred_element_type=jnp.float32
     ) + lax.dot_general(out_grad, proj_lo, dims, preferred_element_type=jnp.float32)
     owners = lax.axis_size("dp")
-    blocks = lax.all_to_all(
-        partial.astype(jnp.bfloat16).reshape(owners, -1, partial.shape[1]),
-        "dp",
-        split_axis=0,
-        concat_axis=0,
-        tiled=True,
-    )
-    lowgrad = jnp.sum(blocks.astype(jnp.float32), axis=0)
+    lowgrad = exchange_sum(partial.astype(jnp.bfloat16).reshape(owners, -1, partial.shape[1]))
     new_first, new_second, direction = adam_moments(lowgrad, first_moment[0], second_moment[0])
     owned_update = lax.dot_general(
         projector, direction, (((1,), (1,)), ((), ())), preferred_element_type=jnp.float32

time: 133 us -> 148 us (1.11)
  Pallas kernels: 0 us -> 75.4 us
  waiting for transfers between devices: 69.7 us -> 15.2 us
  starting transfers between devices: 14.4 us -> 5.17 us
  local copies, waits for them, and re-layouts: 10.1 us -> 13.2 us
  other arithmetic: 7.59 us -> 5.45 us
  matrix products: 9.95 us -> 11.7 us
    pallas_call x0 -> x1, Pallas kernels: none -> 75.4 us  [exchange_sum(): pl.pallas_call(functools.partial(exchange_sum_kernel, n), out_shape=jax.S...]
    all_to_all x1 -> x0, waiting for transfers between devices: 53.6 us -> none  [per_device(): lax.all_to_all(partial.astype(jnp.bfloat16).reshape(owners, -1, partial.s...]
    all_to_all x1 -> x0, starting transfers between devices: 8.54 us -> none  [per_device(): lax.all_to_all(partial.astype(jnp.bfloat16).reshape(owners, -1, partial.s...]
    convert_element_type x0 -> x1, local copies, waits for them, and re-layouts: none -> 6.54 us  [per_device(): partial.astype(jnp.bfloat16).reshape(owners, -1, partial.shape[1])]
    reshape x1 -> x0, local copies, waits for them, and re-layouts: 3.15 us -> none  [per_device(): partial.astype(jnp.bfloat16).reshape(owners, -1, partial.shape[1])]
    reduce_sum x1 -> x0, other arithmetic: 2.94 us -> none  [per_device(): lowgrad = jnp.sum(blocks.astype(jnp.float32), axis=0)]
    dot_general x1, matrix products: 2.73 us -> 4.62 us  [per_device(): lax.dot_general(out_grad, proj_lo, dims, preferred_element_type=jnp.float32)]
    unnamed x14 -> x12, local copies, waits for them, and re-layouts: 3.65 us -> 3.42 us
  transfers between devices with their start and end apart: 2 -> 1, of which waited for: 2 -> 1; matrix products, arithmetic and copies ran while one was open for 2% -> 1% of each run, Pallas kernels for 0% -> 0%
where the time goes in v2:
time: 148 us; the launch traced here: 147 us
  Pallas kernels  75.4 us (51%)
  blocking collectives  20.3 us (14%)
  waiting for transfers between devices  15.2 us (10%)
  local copies, waits for them, and re-layouts  13.2 us (9%)
  matrix products  11.7 us (8%)
  other arithmetic  5.45 us (4%)
  starting transfers between devices  5.17 us (3%)
    pallas_call x1, Pallas kernels, exchange_sum(): pl.pallas_call(functools.partial(exchange_sum_kernel, n), out_shape=jax.S...  75.4 us
    all_to_all x1, blocking collectives, per_device(): lax.all_to_all(jnp.tile(token_proj, (peers, 1)), 'tensor', split_axis=0,...  20.3 us
    all_to_all x1, waiting for transfers between devices, per_device(): lax.all_to_all(owned_update, 'dp', split_axis=0, concat_axis=1, tiled=True)  15.2 us
    convert_element_type x1, local copies, waits for them, and re-layouts, per_device(): partial.astype(jnp.bfloat16).reshape(owners, -1, partial.shape[1])  6.54 us
    all_to_all x1, starting transfers between devices, per_device(): lax.all_to_all(owned_update, 'dp', split_axis=0, concat_axis=1, tiled=True)  5.17 us
    dot_general x1, matrix products, per_device(): lax.dot_general(out_grad, proj_lo, dims, preferred_element_type=jnp.float32)  4.62 us
    unnamed x12, local copies, waits for them, and re-layouts  3.42 us
    dot_general x1, matrix products, per_device(): token_proj = jnp.dot(acts, projector, preferred_element_type=jnp.float32)  3.24 us
  transfers between devices with their start and end apart: 1, of which 1 were waited for; matrix products, arithmetic and copies ran while one was open for 1% of the time, Pallas kernels for 0%

profile of v2, /device:TPU:0, one launch (start us, length us, event | category | flops | bytes accessed | tf_op | source)
XLA Modules:
  0.0 147.1 jit_solution(8914704257266039050)
XLA Ops:
  0.6 0.0 copy-start
  0.6 0.0 copy-start.2
  0.7 1.2 copy-done
  1.9 3.2 %fusion.17 = f32[128,512]{1,0:T(8,128)S(1)} fusion(bf16[128,4096]{1,0:T(8,128)(2,1)S(1)} %copy-done, bf16[4096,512]{1,0:T(8,128)(2,1)} %param.8), kind=kOutput, calls=%fused_computation.26 | convolution fusion | flops 536870912 | bytes 5505024 | tf_op jit(solution)/shard_map/dot_general | solution.py:75
  5.1 0.1 tile.2
  5.2 20.3 %all_to_all.22 = f32[4,128,512]{2,1,0:T(8,128)S(1)} all-to-all(f32[4,128,512]{2,1,0:T(8,128)S(1)} %tile.2), channel_id=1, replica_groups=mesh['dp'=32,'tensor'=4] {'tensor'}, dimensions={0} | all-to-all | bytes 2097152 | tf_op jit(solution)/shard_map/all_to_all | solution.py:77
  25.5 0.1 fusion.2
  25.6 0.0 copy-done.2
  25.6 2.4 %fusion.18 = f32[512,4096]{1,0:T(8,128)S(1)} fusion(bf16[512,512]{1,0:T(8,128)(2,1)S(1)} %get-tuple-element.4, bf16[512,4096]{1,0:T(8,128)(2,1)S(1)} %copy-done.2), kind=kOutput, calls=%fused_computation.27 | convolution fusion | flops 2147483648 | bytes 13107200 | tf_op jit(solution)/shard_map/dot_general | solution.py:83
  28.0 4.6 %fusion = bf16[4096,512]{0,1:T(8,128)(2,1)} fusion(f32[512,4096]{1,0:T(8,128)S(1)} %fusion.18, bf16[512,512]{1,0:T(8,128)(2,1)S(1)} %get-tuple-element.3, bf16[512,4096]{1,0:T(8,128)(2,1)S(1)} %copy-done.2), kind=kOutput, calls=%fused_computation.1 | convolution fusion | flops 2151677952 | bytes 17301504 | tf_op jit(solution)/shard_map/dot_general | solution.py:85
  32.7 6.5 %copy.11 = bf16[4096,512]{1,0:T(8,128)(2,1)} copy(bf16[4096,512]{0,1:T(8,128)(2,1)} %fusion) | data formatting | bytes 8388608 | tf_op jit(solution)/shard_map/convert_element_type | solution.py:87
  39.2 2.2 %copy-done.1 = bf16[4096,512]{1,0:T(8,128)(2,1)S(1)} copy-done((bf16[4096,512]{1,0:T(8,128)(2,1)S(1)}, bf16[4096,512]{1,0:T(8,128)(2,1)}, u32[]{:S(2)}) %copy-start.1) | copy-done | bytes 4194328
  41.4 75.4 %shard_map.85 = f32[128,512]{1,0:T(8,128)S(1)} custom-call(bf16[32,128,512]{2,1,0:T(8,128)(2,1)S(1)} %bitcast.43), custom_call_target="tpu_custom_call" | custom-call | tf_op jit(solution)/shard_map/pallas_call | solution.py:58
  116.8 0.0 copy-done.5
  116.8 0.0 copy-done.3
  116.8 0.0 copy-done.4
  116.8 1.4 fusion.1
  118.3 1.3 copy.16
  119.6 5.2 %all-to-all-start.1 = ((bf16[32,128,128]{1,2,0:T(8,128)(2,1)}), bf16[32,128,128]{1,2,0:T(8,128)(2,1)}, u32[]{:S(2)}, u32[]{:S(2)}) async-start(bf16[32,128,128]{1,2,0:T(8,128)(2,1)} %bitcast.42), calls=%async_computation.1 | async-start | bytes 2097152 | tf_op jit(solution)/shard_map/all_to_all | solution.py:92
  124.7 0.9 fusion.8
  125.6 15.2 %all-to-all-done.1 = bf16[32,128,128]{1,2,0:T(8,128)(2,1)} async-done(((bf16[32,128,128]{1,2,0:T(8,128)(2,1)}), bf16[32,128,128]{1,2,0:T(8,128)(2,1)}, u32[]{:S(2)}, u32[]{:S(2)}) %all-to-all-start.1) | async-done | bytes 1048608 | tf_op jit(solution)/shard_map/all_to_all | solution.py:92
  140.8 1.5 convert_multiply_fusion
  142.2 1.9 %copy.13 = f32[128,4096]{1,0:T(8,128)} copy(f32[128,4096]{0,1:T(8,128)S(1)} %bitcast.44) | data formatting | bytes 4194304 | tf_op jit(solution)/shard_map/mul | solution.py:93
  144.1 3.0 %subtract_convert_fusion = bf16[128,4096]{1,0:T(8,128)(2,1)} fusion(f32[128,4096]{1,0:T(8,128)} %copy.13, bf16[128,4096]{1,0:T(8,128)(2,1)} %param.9), kind=kLoop, calls=%fused_computation.3 | loop fusion | flops 1572864 | bytes 4194304 | tf_op jit(solution)/shard_map/convert_element_type | solution.py:93
  (4 shorter events, 0.0 us)
Async XLA Ops:
  0.6 1.2 copy-start
  0.6 25.0 %copy-start.2 = (bf16[512,4096]{1,0:T(8,128)(2,1)S(1)}, bf16[512,4096]{1,0:T(8,128)(2,1)}, u32[]{:S(2)}) copy-start(bf16[512,4096]{1,0:T(8,128)(2,1)} %param.7) | copy-start | bytes 12582916
  32.7 84.1 %copy-start.5 = (f32[1,128,512]{2,1,0:T(8,128)S(1)}, f32[1,128,512]{2,1,0:T(8,128)}, u32[]{:S(2)}) copy-start(f32[1,128,512]{2,1,0:T(8,128)} %param.11) | copy-start | bytes 786436
  39.2 2.2 %copy-start.1 = (bf16[4096,512]{1,0:T(8,128)(2,1)S(1)}, bf16[4096,512]{1,0:T(8,128)(2,1)}, u32[]{:S(2)}) copy-start(bf16[4096,512]{1,0:T(8,128)(2,1)} %copy.11) | copy-start | bytes 12582916
  41.4 75.4 %copy-start.3 = (bf16[4096,512]{1,0:T(8,128)(2,1)S(1)}, bf16[4096,512]{1,0:T(8,128)(2,1)}, u32[]{:S(2)}) copy-start(bf16[4096,512]{1,0:T(8,128)(2,1)} %param.8) | copy-start | bytes 12582916
  41.4 75.4 %copy-start.4 = (f32[1,128,512]{2,1,0:T(8,128)S(1)}, f32[1,128,512]{2,1,0:T(8,128)}, u32[]{:S(2)}) copy-start(f32[1,128,512]{2,1,0:T(8,128)} %param.10) | copy-start | bytes 786436
  119.6 21.2 %all-to-all-start.1 = ((bf16[32,128,128]{1,2,0:T(8,128)(2,1)}), bf16[32,128,128]{1,2,0:T(8,128)(2,1)}, u32[]{:S(2)}, u32[]{:S(2)}) async-start(bf16[32,128,128]{1,2,0:T(8,128)(2,1)} %bitcast.42), calls=%async_computation.1 | async-start | bytes 2097152 | tf_op jit(solution)/shard_map/all_to_all | solution.py:92

commit v3 on v2

--- a/solution.py
+++ b/solution.py
@@ -71,12 +71,51 @@
     )(part)
 
 
+def gather_kernel(n, axis, part_ref, out_ref, recv, send_sem, recv_sem):
+    me = lax.axis_index(axis)
+    barrier = pltpu.get_barrier_semaphore()
+    for k in range(1, n):
+        pl.semaphore_signal(
+            barrier, inc=1, device_id={axis: lax.rem(me + k, n)}, device_id_type=MESH_ID
+        )
+    pl.semaphore_wait(barrier, n - 1)
+    copies = []
+    for k in range(1, n):
+        copy = pltpu.make_async_remote_copy(
+            src_ref=part_ref,
+            dst_ref=recv.at[k],
+            send_sem=send_sem.at[k],
+            recv_sem=recv_sem.at[k],
+            device_id={axis: lax.rem(me + k, n)},
+            device_id_type=MESH_ID,
+        )
+        copy.start()
+        copies.append(copy)
+    out_ref[me] = part_ref[...]
+    for k, copy in enumerate(copies, 1):
+        copy.wait()
+        out_ref[lax.rem(me + n - k, n)] = recv[k]
+
+
+def gather(part, axis, n, collective_id):
+    return pl.pallas_call(
+        functools.partial(gather_kernel, n, axis),
+        out_shape=jax.ShapeDtypeStruct((n,) + part.shape, part.dtype),
+        in_specs=[pl.BlockSpec(memory_space=pltpu.VMEM)],
+        out_specs=pl.BlockSpec(memory_space=pltpu.VMEM),
+        scratch_shapes=[
+            pltpu.VMEM((n,) + part.shape, part.dtype),
+            pltpu.SemaphoreType.DMA((n,)),
+            pltpu.SemaphoreType.DMA((n,)),
+        ],
+        compiler_params=pltpu.CompilerParams(collective_id=collective_id, has_side_effects=True),
+    )(part)
+
+
 def per_device(acts, out_grad, projector, weight, first_moment, second_moment):
     token_proj = jnp.dot(acts, projector, preferred_element_type=jnp.float32)
     peers = lax.axis_size("tensor")
-    whole_proj = lax.all_to_all(
-        jnp.tile(token_proj, (peers, 1)), "tensor", split_axis=0, concat_axis=0, tiled=True
-    )
+    whole_proj = gather(token_proj, "tensor", peers, 1).reshape(-1, token_proj.shape[1])
     proj_hi = whole_proj.astype(jnp.bfloat16)
     proj_lo = (whole_proj - proj_hi.astype(jnp.float32)).astype(jnp.bfloat16)
     dims = (((0,), (0,)), ((), ()))
@@ -84,7 +123,14 @@
         out_grad, proj_hi, dims, preferred_element_type=jnp.float32
     ) + lax.dot_general(out_grad, proj_lo, dims, preferred_element_type=jnp.float32)
     owners = lax.axis_size("dp")
-    lowgrad = exchange_sum(partial.astype(jnp.bfloat16).reshape(owners, -1, partial.shape[1]))
+    blocks = lax.all_to_all(
+        partial.astype(jnp.bfloat16).reshape(owners, -1, partial.shape[1]),
+        "dp",
+        split_axis=0,
+        concat_axis=0,
+        tiled=True,
+    )
+    lowgrad = jnp.sum(blocks.astype(jnp.float32), axis=0)
     new_first, new_second, direction = adam_moments(lowgrad, first_moment[0], second_moment[0])
     owned_update = lax.dot_general(
         projector, direction, (((1,), (1,)), ((), ())), preferred_element_type=jnp.float32

time: 148 us -> 148 us (level)
  waiting for transfers between devices: 15.2 us -> 75.4 us
  Pallas kernels: 75.4 us -> 17.1 us
  blocking collectives: 20.3 us -> 0 us
  starting transfers between devices: 5.17 us -> 22.5 us
  other arithmetic: 5.45 us -> 8.88 us
  local copies, waits for them, and re-layouts: 13.2 us -> 9.95 us
    all_to_all x0 -> x1, waiting for transfers between devices: none -> 59.1 us  [per_device(): lax.all_to_all(partial.astype(jnp.bfloat16).reshape(owners, -1, partial.s...]
    pallas_call x1, Pallas kernels: 75.4 us -> 17.1 us  [gather(): pl.pallas_call(functools.partial(gather_kernel, n, axis), out_shape=jax.S...]
    all_to_all x1 -> x0, blocking collectives: 20.3 us -> none  [per_device(): lax.all_to_all(jnp.tile(token_proj, (peers, 1)), 'tensor', split_axis=0,...]
    all_to_all x1, starting transfers between devices: 5.17 us -> 14 us  [per_device(): lax.all_to_all(owned_update, 'dp', split_axis=0, concat_axis=1, tiled=True)]
    all_to_all x0 -> x1, starting transfers between devices: none -> 8.54 us  [per_device(): lax.all_to_all(partial.astype(jnp.bfloat16).reshape(owners, -1, partial.s...]
    convert_element_type x1 -> x0, local copies, waits for them, and re-layouts: 6.54 us -> none  [per_device(): partial.astype(jnp.bfloat16).reshape(owners, -1, partial.shape[1])]
    reshape x0 -> x1, local copies, waits for them, and re-layouts: none -> 3.15 us  [per_device(): partial.astype(jnp.bfloat16).reshape(owners, -1, partial.shape[1])]
    reduce_sum x0 -> x1, other arithmetic: none -> 2.94 us  [per_device(): lowgrad = jnp.sum(blocks.astype(jnp.float32), axis=0)]
  transfers between devices with their start and end apart: 1 -> 2, of which waited for: 1 -> 2; matrix products, arithmetic and copies ran while one was open for 1% -> 1% of each run, Pallas kernels for 0% -> 0%
where the time goes in v3:
time: 148 us; the launch traced here: 147 us
  waiting for transfers between devices  75.4 us (51%)
  starting transfers between devices  22.5 us (15%)
  Pallas kernels  17.1 us (12%)
  matrix products  12.7 us (9%)
  local copies, waits for them, and re-layouts  9.95 us (7%)
  other arithmetic  8.88 us (6%)
    all_to_all x1, waiting for transfers between devices, per_device(): lax.all_to_all(partial.astype(jnp.bfloat16).reshape(owners, -1, partial.s...  59.1 us
    pallas_call x1, Pallas kernels, gather(): pl.pallas_call(functools.partial(gather_kernel, n, axis), out_shape=jax.S...  17.1 us
    all_to_all x1, waiting for transfers between devices, per_device(): lax.all_to_all(owned_update, 'dp', split_axis=0, concat_axis=1, tiled=True)  16.3 us
    all_to_all x1, starting transfers between devices, per_device(): lax.all_to_all(owned_update, 'dp', split_axis=0, concat_axis=1, tiled=True)  14 us
    all_to_all x1, starting transfers between devices, per_device(): lax.all_to_all(partial.astype(jnp.bfloat16).reshape(owners, -1, partial.s...  8.54 us
    dot_general x1, matrix products, per_device(): lax.dot_general(out_grad, proj_hi, dims, preferred_element_type=jnp.float32)  4.81 us
    unnamed x14, local copies, waits for them, and re-layouts  3.66 us
    dot_general x1, matrix products, per_device(): token_proj = jnp.dot(acts, projector, preferred_element_type=jnp.float32)  3.61 us
  transfers between devices with their start and end apart: 2, of which 2 were waited for; matrix products, arithmetic and copies ran while one was open for 1% of the time, Pallas kernels for 0%

profile of v3, /device:TPU:0, one launch (start us, length us, event | category | flops | bytes accessed | tf_op | source)
XLA Modules:
  0.0 147.3 jit_solution(12649674202477041980)
XLA Ops:
  0.6 0.0 copy-start
  0.6 1.2 copy-done
  1.9 3.6 %fusion.27.part_ref = f32[128,512]{1,0:T(8,128)} fusion(bf16[128,4096]{1,0:T(8,128)(2,1)S(1)} %copy-done, bf16[4096,512]{1,0:T(8,128)(2,1)} %param.8), kind=kOutput, calls=%fused_computation.39 | convolution fusion | flops 536870912 | bytes 5505024 | tf_op jit(solution)/shard_map/dot_general | solution.py:116
  5.5 17.1 %shard_map.85 = f32[4,128,512]{2,1,0:T(8,128)} custom-call(f32[128,512]{1,0:T(8,128)} %fusion.27.part_ref), custom_call_target="tpu_custom_call" | custom-call | tf_op jit(solution)/shard_map/pallas_call | solution.py:101
  22.5 1.4 fusion.2
  23.9 4.8 %fusion.28 = f32[512,4096]{1,0:T(8,128)S(1)} fusion(bf16[512,512]{1,0:T(8,128)(2,1)S(1)} %get-tuple-element.7, bf16[512,4096]{1,0:T(8,128)(2,1)} %param.7), kind=kOutput, calls=%fused_computation.40 | convolution fusion | flops 2147483648 | bytes 13107200 | tf_op jit(solution)/shard_map/dot_general | solution.py:122
  28.8 2.7 %fusion = bf16[64,32,8,128]{3,2,1,0:T(8,128)(2,1)S(1)} fusion(f32[512,4096]{1,0:T(8,128)S(1)} %fusion.28, bf16[512,512]{1,0:T(8,128)(2,1)S(1)} %get-tuple-element.6, bf16[512,4096]{1,0:T(8,128)(2,1)S(1)} %copy-done.1), kind=kOutput, calls=%fused_computation.4 | convolution fusion | flops 2151677952 | bytes 17301504 | tf_op jit(solution)/shard_map/dot_general | solution.py:124
  31.5 3.1 %copy.23 = bf16[64,32,8,128]{3,2,0,1:T(8,128)(2,1)} copy(bf16[64,32,8,128]{3,2,1,0:T(8,128)(2,1)S(1)} %fusion) | data formatting | bytes 8388608 | tf_op jit(solution)/shard_map/reshape | solution.py:127
  34.6 8.5 %all-to-all-start = ((bf16[32,128,512]{1,2,0:T(8,128)(2,1)}), bf16[32,128,512]{1,2,0:T(8,128)(2,1)}, u32[]{:S(2)}, u32[]{:S(2)}) async-start(bf16[32,128,512]{1,2,0:T(8,128)(2,1)} %bitcast.47), calls=%async_computation | async-start | bytes 8388608 | tf_op jit(solution)/shard_map/all_to_all | solution.py:126
  43.2 0.1 copy.10
  43.3 0.1 copy.13
  43.5 59.1 %all-to-all-done = bf16[32,128,512]{1,2,0:T(8,128)(2,1)} async-done(((bf16[32,128,512]{1,2,0:T(8,128)(2,1)}), bf16[32,128,512]{1,2,0:T(8,128)(2,1)}, u32[]{:S(2)}, u32[]{:S(2)}) %all-to-all-start) | async-done | bytes 4194336 | tf_op jit(solution)/shard_map/all_to_all | solution.py:126
  102.6 2.9 %convert_reduce_fusion = f32[128,512]{0,1:T(8,128)S(1)} fusion(bf16[32,128,512]{1,2,0:T(8,128)(2,1)} %all-to-all-done), kind=kLoop, calls=%fused_computation | loop fusion | flops 4128768 | bytes 4456448 | tf_op jit(solution)/shard_map/reduce_sum | solution.py:133
  105.5 0.5 copy-done.2
  106.0 1.6 %fusion.1 = bf16[16,32,8,128]{3,2,1,0:T(8,128)(2,1)S(1)} fusion(bf16[4096,512]{1,0:T(8,128)(2,1)S(1)} %copy-done.2, f32[128,512]{0,1:T(8,128)S(1)} %convert_reduce_fusion, f32[1,128,512]{1,2,0:T(8,128)S(1)} %copy.13, f32[1,128,512]{1,2,0:T(8,128)S(1)} %copy.10), kind=kOutput, calls=%fused_computation.7 | convolution fusion | flops 538181632 | bytes 6029312 | tf_op jit(solution)/shard_map/dot_general | solution.py:135
  107.6 1.3 copy.24
  108.9 14.0 %all-to-all-start.1 = ((bf16[32,128,128]{1,2,0:T(8,128)(2,1)}), bf16[32,128,128]{1,2,0:T(8,128)(2,1)}, u32[]{:S(2)}, u32[]{:S(2)}) async-start(bf16[32,128,128]{1,2,0:T(8,128)(2,1)} %bitcast.46), calls=%async_computation.1 | async-start | bytes 2097152 | tf_op jit(solution)/shard_map/all_to_all | solution.py:138
  122.9 0.1 fusion.8
  123.0 0.8 copy.16
  123.8 0.8 copy.17
  124.6 16.3 %all-to-all-done.1 = bf16[32,128,128]{1,2,0:T(8,128)(2,1)} async-done(((bf16[32,128,128]{1,2,0:T(8,128)(2,1)}), bf16[32,128,128]{1,2,0:T(8,128)(2,1)}, u32[]{:S(2)}, u32[]{:S(2)}) %all-to-all-start.1) | async-done | bytes 1048608 | tf_op jit(solution)/shard_map/all_to_all | solution.py:138
  141.0 1.5 convert_multiply_fusion
  142.4 1.9 %copy.15 = f32[128,4096]{1,0:T(8,128)} copy(f32[128,4096]{0,1:T(8,128)S(1)} %bitcast.48) | data formatting | bytes 4194304 | tf_op jit(solution)/shard_map/mul | solution.py:139
  144.3 3.0 %subtract_convert_fusion = bf16[128,4096]{1,0:T(8,128)(2,1)} fusion(f32[128,4096]{1,0:T(8,128)} %copy.15, bf16[128,4096]{1,0:T(8,128)(2,1)} %param.9), kind=kLoop, calls=%fused_computation.5 | loop fusion | flops 1572864 | bytes 4194304 | tf_op jit(solution)/shard_map/convert_element_type | solution.py:139
  (7 shorter events, 0.0 us)
Async XLA Ops:
  0.6 1.2 copy-start
  23.9 4.8 %copy-start.1 = (bf16[512,4096]{1,0:T(8,128)(2,1)S(1)}, bf16[512,4096]{1,0:T(8,128)(2,1)}, u32[]{:S(2)}) copy-start(bf16[512,4096]{1,0:T(8,128)(2,1)} %param.7) | copy-start | bytes 12582916
  34.6 8.6 %copy-start.3 = (f32[1,128,512]{2,1,0:T(8,128)S(1)}, f32[1,128,512]{2,1,0:T(8,128)}, u32[]{:S(2)}) copy-start(f32[1,128,512]{2,1,0:T(8,128)} %param.10) | copy-start | bytes 786436
  34.6 8.7 %copy-start.4 = (f32[1,128,512]{2,1,0:T(8,128)S(1)}, f32[1,128,512]{2,1,0:T(8,128)}, u32[]{:S(2)}) copy-start(f32[1,128,512]{2,1,0:T(8,128)} %param.11) | copy-start | bytes 786436
  34.6 67.9 %all-to-all-start = ((bf16[32,128,512]{1,2,0:T(8,128)(2,1)}), bf16[32,128,512]{1,2,0:T(8,128)(2,1)}, u32[]{:S(2)}, u32[]{:S(2)}) async-start(bf16[32,128,512]{1,2,0:T(8,128)(2,1)} %bitcast.47), calls=%async_computation | async-start | bytes 8388608 | tf_op jit(solution)/shard_map/all_to_all | solution.py:126
  102.6 3.4 %copy-start.2 = (bf16[4096,512]{1,0:T(8,128)(2,1)S(1)}, bf16[4096,512]{1,0:T(8,128)(2,1)}, u32[]{:S(2)}) copy-start(bf16[4096,512]{1,0:T(8,128)(2,1)} %param.8) | copy-start | bytes 12582916
  108.9 32.1 %all-to-all-start.1 = ((bf16[32,128,128]{1,2,0:T(8,128)(2,1)}), bf16[32,128,128]{1,2,0:T(8,128)(2,1)}, u32[]{:S(2)}, u32[]{:S(2)}) async-start(bf16[32,128,128]{1,2,0:T(8,128)(2,1)} %bitcast.46), calls=%async_computation.1 | async-start | bytes 2097152 | tf_op jit(solution)/shard_map/all_to_all | solution.py:138

commit v4 on v2

--- a/solution.py
+++ b/solution.py
@@ -25,20 +25,53 @@
     return (new_first, new_second, direction)
 
 
-def exchange_sum_kernel(n, part_ref, out_ref, recv, send_sem, recv_sem):
+def tail_kernel(
+    n, blocks_ref, first_ref, second_ref, proj_ref, weight_ref,
+    new_weight_ref, new_first_ref, new_second_ref,
+    total, direction_ref, update, sendbuf, recv, local_sem, send_sem, recv_sem,
+):
     me = lax.axis_index("dp")
     col = lax.axis_index("tensor")
+    rows = sendbuf.shape[1]
+    width = sendbuf.shape[2]
     barrier = pltpu.get_barrier_semaphore()
     for k in range(1, n):
         pl.semaphore_signal(
             barrier, inc=1, device_id=(lax.rem(me + k, n), col), device_id_type=MESH_ID
         )
     pl.semaphore_wait(barrier, n - 1)
+
+    total[...] = blocks_ref[0].astype(jnp.float32)
+
+    def add_block(k, carry):
+        total[...] += blocks_ref[k].astype(jnp.float32)
+        return carry
+
+    lax.fori_loop(1, n, add_block, 0)
+    new_first, new_second, direction = adam_moments(total[...], first_ref[...], second_ref[...])
+    new_first_ref[...] = new_first
+    new_second_ref[...] = new_second
+    direction_ref[...] = direction
+
+    def update_block(j, carry):
+        start = pl.multiple_of(j * rows, rows)
+        update[j] = lax.dot_general(
+            proj_ref[pl.ds(start, rows), :],
+            direction_ref[...],
+            (((1,), (1,)), ((), ())),
+            preferred_element_type=jnp.float32,
+        ).astype(jnp.bfloat16)
+        return carry
+
+    lax.fori_loop(0, n, update_block, 0)
+    local = pltpu.make_async_copy(update, sendbuf, local_sem)
+    local.start()
+    local.wait()
     copies = []
     for k in range(1, n):
         dest = lax.rem(me + k, n)
         copy = pltpu.make_async_remote_copy(
-            src_ref=part_ref.at[dest],
+            src_ref=sendbuf.at[dest],
             dst_ref=recv.at[k],
             send_sem=send_sem.at[k],
             recv_sem=recv_sem.at[k],
@@ -47,28 +80,46 @@
         )
         copy.start()
         copies.append(copy)
-    out_ref[...] = part_ref[me].astype(jnp.float32)
+
+    def apply(source, block):
+        cols = pl.ds(pl.multiple_of(source * width, width), width)
+        new_weight_ref[:, cols] = (
+            weight_ref[:, cols].astype(jnp.float32) - step_rate * block.astype(jnp.float32)
+        ).astype(jnp.bfloat16)
+
+    apply(me, sendbuf[me])
     for k, copy in enumerate(copies, 1):
         copy.wait()
-        out_ref[...] += recv[k].astype(jnp.float32)
+        apply(lax.rem(me + n - k, n), recv[k])
 
 
-def exchange_sum(part):
-    n, rows, cols = part.shape
+def tail(blocks, first_moment, second_moment, projector, weight):
+    n, hidden, rank = blocks.shape
+    rows = weight.shape[0]
+    vmem = pl.BlockSpec(memory_space=pltpu.VMEM)
     return pl.pallas_call(
-        functools.partial(exchange_sum_kernel, n),
-        out_shape=jax.ShapeDtypeStruct((rows, cols), jnp.float32),
-        in_specs=[pl.BlockSpec(memory_space=pltpu.VMEM)],
-        out_specs=pl.BlockSpec(memory_space=pltpu.VMEM),
+        functools.partial(tail_kernel, n),
+        out_shape=(
+            jax.ShapeDtypeStruct(weight.shape, weight.dtype),
+            jax.ShapeDtypeStruct((hidden, rank), jnp.float32),
+            jax.ShapeDtypeStruct((hidden, rank), jnp.float32),
+        ),
+        in_specs=[vmem] * 5,
+        out_specs=(vmem, vmem, vmem),
         scratch_shapes=[
-            pltpu.VMEM((n, rows, cols), part.dtype),
+            pltpu.VMEM((hidden, rank), jnp.float32),
+            pltpu.VMEM((hidden, rank), jnp.bfloat16),
+            pltpu.VMEM((n, rows, hidden), jnp.bfloat16),
+            pltpu.VMEM((n, rows, hidden), jnp.bfloat16),
+            pltpu.VMEM((n, rows, hidden), jnp.bfloat16),
+            pltpu.SemaphoreType.DMA(()),
             pltpu.SemaphoreType.DMA((n,)),
             pltpu.SemaphoreType.DMA((n,)),
         ],
         compiler_params=pltpu.CompilerParams(
-            collective_id=0, has_side_effects=True, vmem_limit_bytes=48 * 1024 * 1024
+            collective_id=2, has_side_effects=True, vmem_limit_bytes=48 * 1024 * 1024
         ),
-    )(part)
+    )(blocks, first_moment, second_moment, projector, weight)
 
 
 def per_device(acts, out_grad, projector, weight, first_moment, second_moment):
@@ -84,14 +135,15 @@
         out_grad, proj_hi, dims, preferred_element_type=jnp.float32
     ) + lax.dot_general(out_grad, proj_lo, dims, preferred_element_type=jnp.float32)
     owners = lax.axis_size("dp")
-    lowgrad = exchange_sum(partial.astype(jnp.bfloat16).reshape(owners, -1, partial.shape[1]))
-    new_first, new_second, direction = adam_moments(lowgrad, first_moment[0], second_moment[0])
-    owned_update = lax.dot_general(
-        projector, direction, (((1,), (1,)), ((), ())), preferred_element_type=jnp.float32
-    ).astype(jnp.bfloat16)
-    update = lax.all_to_all(owned_update, "dp", split_axis=0, concat_axis=1, tiled=True)
-    new_weight = (weight.astype(jnp.float32) - step_rate * update.astype(jnp.float32)).astype(
-        jnp.bfloat16
+    blocks = lax.all_to_all(
+        partial.astype(jnp.bfloat16).reshape(owners, -1, partial.shape[1]),
+        "dp",
+        split_axis=0,
+        concat_axis=0,
+        tiled=True,
+    )
+    new_weight, new_first, new_second = tail(
+        blocks, first_moment[0], second_moment[0], projector, weight
     )
     return (new_weight, new_first[None], new_second[None])
 

time: 148 us -> 129 us (0.87)
  blocking collectives: 20.3 us -> 80 us
  Pallas kernels: 75.4 us -> 26.2 us
  waiting for transfers between devices: 15.2 us -> 0 us
  other arithmetic: 5.45 us -> 0.08 us
  starting transfers between devices: 5.17 us -> 0 us
  local copies, waits for them, and re-layouts: 13.2 us -> 10.2 us
    all_to_all x0 -> x1, blocking collectives: none -> 59.7 us  [per_device(): lax.all_to_all(partial.astype(jnp.bfloat16).reshape(owners, -1, partial.s...]
    pallas_call x1, Pallas kernels: 75.4 us -> 26.2 us  [tail(): pl.pallas_call(functools.partial(tail_kernel, n), out_shape=(jax.ShapeDty...]
    all_to_all x1 -> x0, waiting for transfers between devices: 15.2 us -> none  [per_device(): lax.all_to_all(owned_update, 'dp', split_axis=0, concat_axis=1, tiled=True)]
    all_to_all x1 -> x0, starting transfers between devices: 5.17 us -> none  [per_device(): lax.all_to_all(owned_update, 'dp', split_axis=0, concat_axis=1, tiled=True)]
    convert_element_type x1 -> x0, other arithmetic: 3.04 us -> none  [per_device(): (weight.astype(jnp.float32) - step_rate * update.astype(jnp.float32)).ast...]
    mul x1 -> x0, local copies, waits for them, and re-layouts: 1.85 us -> none  [per_device(): step_rate * update.astype(jnp.float32)]
    unnamed x12 -> x13, local copies, waits for them, and re-layouts: 3.42 us -> 3.61 us
  transfers between devices with their start and end apart: 1 -> 0, of which waited for: 1 -> 0; matrix products, arithmetic and copies ran while one was open for 1% -> 0% of each run, Pallas kernels for 0% -> 0%
where the time goes in v4:
time: 129 us; the launch traced here: 127 us
  blocking collectives  80 us (62%)
  Pallas kernels  26.2 us (20%)
  matrix products  10.3 us (8%)
  local copies, waits for them, and re-layouts  10.2 us (8%)
    all_to_all x1, blocking collectives, per_device(): lax.all_to_all(partial.astype(jnp.bfloat16).reshape(owners, -1, partial.s...  59.7 us
    pallas_call x1, Pallas kernels, tail(): pl.pallas_call(functools.partial(tail_kernel, n), out_shape=(jax.ShapeDty...  26.2 us
    all_to_all x1, blocking collectives, per_device(): lax.all_to_all(jnp.tile(token_proj, (peers, 1)), 'tensor', split_axis=0,...  20.3 us
    convert_element_type x1, local copies, waits for them, and re-layouts, per_device(): partial.astype(jnp.bfloat16).reshape(owners, -1, partial.shape[1])  6.46 us
    dot_general x1, matrix products, per_device(): lax.dot_general(out_grad, proj_lo, dims, preferred_element_type=jnp.float32)  4.65 us
    unnamed x13, local copies, waits for them, and re-layouts  3.61 us
    dot_general x1, matrix products, per_device(): token_proj = jnp.dot(acts, projector, preferred_element_type=jnp.float32)  3.24 us

profile of v4, /device:TPU:0, one launch (start us, length us, event | category | flops | bytes accessed | tf_op | source)
XLA Modules:
  0.0 127.5 jit_solution(18418192602160614876)
XLA Ops:
  0.6 0.0 copy-start
  0.6 0.0 copy-start.4
  0.7 1.2 copy-done
  1.9 3.2 %fusion.2 = f32[128,512]{1,0:T(8,128)S(1)} fusion(bf16[128,4096]{1,0:T(8,128)(2,1)S(1)} %copy-done, bf16[4096,512]{1,0:T(8,128)(2,1)} %proj_ref.1), kind=kOutput, calls=%fused_computation.5 | convolution fusion | flops 536870912 | bytes 5505024 | tf_op jit(solution)/shard_map/dot_general | solution.py:126
  5.1 0.1 tile.2
  5.2 20.3 %all_to_all.14 = f32[4,128,512]{2,1,0:T(8,128)S(1)} all-to-all(f32[4,128,512]{2,1,0:T(8,128)S(1)} %tile.2), channel_id=1, replica_groups=mesh['dp'=32,'tensor'=4] {'tensor'}, dimensions={0} | all-to-all | bytes 2097152 | tf_op jit(solution)/shard_map/all_to_all | solution.py:128
  25.5 0.1 fusion.1
  25.6 0.0 copy-done.4
  25.6 2.4 %fusion.3 = f32[512,4096]{1,0:T(8,128)S(1)} fusion(bf16[512,512]{1,0:T(8,128)(2,1)S(1)} %get-tuple-element.10, bf16[512,4096]{1,0:T(8,128)(2,1)S(1)} %copy-done.4), kind=kOutput, calls=%fused_computation.6 | convolution fusion | flops 2147483648 | bytes 13107200 | tf_op jit(solution)/shard_map/dot_general | solution.py:134
  28.0 4.6 %fusion = bf16[4096,512]{0,1:T(8,128)(2,1)} fusion(f32[512,4096]{1,0:T(8,128)S(1)} %fusion.3, bf16[512,512]{1,0:T(8,128)(2,1)S(1)} %get-tuple-element.9, bf16[512,4096]{1,0:T(8,128)(2,1)S(1)} %copy-done.4), kind=kOutput, calls=%fused_computation.1 | convolution fusion | flops 2151677952 | bytes 17301504 | tf_op jit(solution)/shard_map/dot_general | solution.py:136
  32.7 6.5 %copy.9 = bf16[4096,512]{1,0:T(8,128)(2,1)} copy(bf16[4096,512]{0,1:T(8,128)(2,1)} %fusion) | data formatting | bytes 8388608 | tf_op jit(solution)/shard_map/convert_element_type | solution.py:139
  39.1 0.0 copy-start.1
  39.1 0.0 copy-start.2
  39.1 0.0 copy-start.3
  39.2 59.7 %all_to_all.15.blocks_ref = bf16[32,128,512]{2,1,0:T(8,128)(2,1)} all-to-all(bf16[32,128,512]{2,1,0:T(8,128)(2,1)} %bitcast.23), channel_id=1, replica_groups=mesh['dp'=32,'tensor'=4] {'dp'}, dimensions={0} | all-to-all | bytes 8388608 | tf_op jit(solution)/shard_map/all_to_all | solution.py:138
  98.9 0.0 copy-done.1
  98.9 0.0 copy-done.2
  98.9 0.0 copy-done.3
  98.9 26.2 %shard_map.85 = (bf16[128,4096]{1,0:T(8,128)(2,1)S(1)}, f32[128,512]{1,0:T(8,128)S(1)}, f32[128,512]{1,0:T(8,128)S(1)}) custom-call(bf16[32,128,512]{2,1,0:T(8,128)(2,1)} %all_to_all.15.blocks_ref, f32[128,512]{1,0:T(8,128)S(1)} %bitcast.19, f32[128,512]{1,0:T(8,128)S(1)} %bitcast.20, bf16[4096,512]{1,0:T(8,128)(2,1)} %proj_ref.1, ...), custom_call_target="tpu_custom_call" | custom-call | tf_op jit(solution)/shard_map/pallas_call | solution.py:100
  125.1 1.0 copy.13
  126.1 0.7 copy.14
  126.8 0.7 copy.15
Async XLA Ops:
  0.6 1.2 copy-start
  0.6 25.0 %copy-start.4 = (bf16[512,4096]{1,0:T(8,128)(2,1)S(1)}, bf16[512,4096]{1,0:T(8,128)(2,1)}, u32[]{:S(2)}) copy-start(bf16[512,4096]{1,0:T(8,128)(2,1)} %param.7) | copy-start | bytes 12582916
  39.1 59.7 %copy-start.1 = (bf16[128,4096]{1,0:T(8,128)(2,1)S(1)}, bf16[128,4096]{1,0:T(8,128)(2,1)}, u32[]{:S(2)}) copy-start(bf16[128,4096]{1,0:T(8,128)(2,1)} %weight_ref.1) | copy-start | bytes 3145732
  39.1 59.7 %copy-start.2 = (f32[1,128,512]{2,1,0:T(8,128)S(1)}, f32[1,128,512]{2,1,0:T(8,128)}, u32[]{:S(2)}) copy-start(f32[1,128,512]{2,1,0:T(8,128)} %param.10) | copy-start | bytes 786436
  39.1 59.7 %copy-start.3 = (f32[1,128,512]{2,1,0:T(8,128)S(1)}, f32[1,128,512]{2,1,0:T(8,128)}, u32[]{:S(2)}) copy-start(f32[1,128,512]{2,1,0:T(8,128)} %param.11) | copy-start | bytes 786436

commit v5 on v4

--- a/solution.py
+++ b/solution.py
@@ -130,17 +130,14 @@
     )
     proj_hi = whole_proj.astype(jnp.bfloat16)
     proj_lo = (whole_proj - proj_hi.astype(jnp.float32)).astype(jnp.bfloat16)
+    owners = lax.axis_size("dp")
+    grad_blocks = out_grad.reshape(out_grad.shape[0], owners, -1)
     dims = (((0,), (0,)), ((), ()))
     partial = lax.dot_general(
-        out_grad, proj_hi, dims, preferred_element_type=jnp.float32
-    ) + lax.dot_general(out_grad, proj_lo, dims, preferred_element_type=jnp.float32)
-    owners = lax.axis_size("dp")
+        grad_blocks, proj_hi, dims, preferred_element_type=jnp.float32
+    ) + lax.dot_general(grad_blocks, proj_lo, dims, preferred_element_type=jnp.float32)
     blocks = lax.all_to_all(
-        partial.astype(jnp.bfloat16).reshape(owners, -1, partial.shape[1]),
-        "dp",
-        split_axis=0,
-        concat_axis=0,
-        tiled=True,
+        partial.astype(jnp.bfloat16), "dp", split_axis=0, concat_axis=0, tiled=True
     )
     new_weight, new_first, new_second = tail(
         blocks, first_moment[0], second_moment[0], projector, weight

time: 129 us -> 123 us (0.953)
  local copies, waits for them, and re-layouts: 10.2 us -> 4.02 us
    convert_element_type x1 -> x0, local copies, waits for them, and re-layouts: 6.46 us -> none  [per_device(): partial.astype(jnp.bfloat16).reshape(owners, -1, partial.shape[1])]
where the time goes in v5:
time: 123 us; the launch traced here: 122 us
  blocking collectives  79.8 us (65%)
  Pallas kernels  26.2 us (21%)
  matrix products  11.3 us (9%)
  local copies, waits for them, and re-layouts  4.02 us (3%)
    all_to_all x1, blocking collectives, per_device(): lax.all_to_all(partial.astype(jnp.bfloat16), 'dp', split_axis=0, concat_a...  59.5 us
    pallas_call x1, Pallas kernels, tail(): pl.pallas_call(functools.partial(tail_kernel, n), out_shape=(jax.ShapeDty...  26.2 us
    all_to_all x1, blocking collectives, per_device(): lax.all_to_all(jnp.tile(token_proj, (peers, 1)), 'tensor', split_axis=0,...  20.3 us
    dot_general x1, matrix products, per_device(): lax.dot_general(grad_blocks, proj_lo, dims, preferred_element_type=jnp.fl...  4.78 us
    dot_general x1, matrix products, per_device(): token_proj = jnp.dot(acts, projector, preferred_element_type=jnp.float32)  3.92 us
    unnamed x13, local copies, waits for them, and re-layouts  3.63 us
    dot_general x1, matrix products, per_device(): lax.dot_general(grad_blocks, proj_hi, dims, preferred_element_type=jnp.fl...  2.65 us

profile of v5, /device:TPU:0, one launch (start us, length us, event | category | flops | bytes accessed | tf_op | source)
XLA Modules:
  0.0 122.3 jit_solution(17986861180807690405)
XLA Ops:
  0.6 0.0 copy-start
  0.6 1.2 copy-done
  1.9 3.9 %fusion.9 = f32[128,512]{0,1:T(8,128)S(1)} fusion(bf16[128,4096]{1,0:T(8,128)(2,1)S(1)} %copy-done, bf16[4096,512]{1,0:T(8,128)(2,1)} %proj_ref.1), kind=kOutput, calls=%fused_computation.9 | convolution fusion | flops 536870912 | bytes 5505024 | tf_op jit(solution)/shard_map/dot_general | solution.py:126
  5.8 0.1 tile.2
  5.9 20.3 %all_to_all.11 = f32[4,128,512]{1,2,0:T(8,128)S(1)} all-to-all(f32[4,128,512]{1,2,0:T(8,128)S(1)} %tile.2), channel_id=1, replica_groups=mesh['dp'=32,'tensor'=4] {'tensor'}, dimensions={0} | all-to-all | bytes 2097152 | tf_op jit(solution)/shard_map/all_to_all | solution.py:128
  26.2 0.3 copy.21
  26.5 0.1 subtract_convert_fusion
  26.7 0.0 copy-start.4
  26.7 4.8 %fusion.1 = f32[512,32,128]{0,2,1:T(8,128)S(1)} fusion(bf16[512,512,1]{1,0,2:T(8,128)(2,1)S(1)} %bitcast.36, bf16[512,4096]{1,0:T(8,128)(2,1)} %param.7), kind=kOutput, calls=%fused_computation.2 | convolution fusion | flops 2147483648 | bytes 13107200 | tf_op jit(solution)/shard_map/dot_general | solution.py:138
  31.5 0.0 copy-done.4
  31.5 2.6 %fusion = bf16[32,128,512]{2,1,0:T(8,128)(2,1)S(1)} fusion(f32[512,32,128]{0,2,1:T(8,128)S(1)} %fusion.1, bf16[512,512,1]{1,0,2:T(8,128)(2,1)S(1)} %bitcast.35, bf16[512,4096]{1,0:T(8,128)(2,1)S(1)} %copy-done.4), kind=kOutput, calls=%fused_computation.1 | convolution fusion | flops 2151677952 | bytes 17301504 | tf_op jit(solution)/shard_map/dot_general | solution.py:136
  34.1 0.0 copy-start.1
  34.1 0.0 copy-start.2
  34.2 0.0 copy-start.3
  34.2 59.5 %all_to_all.12.blocks_ref = bf16[32,128,512]{2,1,0:T(8,128)(2,1)} all-to-all(bf16[32,128,512]{2,1,0:T(8,128)(2,1)S(1)} %fusion), channel_id=1, replica_groups=mesh['dp'=32,'tensor'=4] {'dp'}, dimensions={0} | all-to-all | bytes 8388608 | tf_op jit(solution)/shard_map/all_to_all | solution.py:139
  93.7 0.0 copy-done.1
  93.7 0.0 copy-done.2
  93.7 0.0 copy-done.3
  93.7 26.2 %shard_map.85 = (bf16[128,4096]{1,0:T(8,128)(2,1)S(1)}, f32[128,512]{1,0:T(8,128)S(1)}, f32[128,512]{1,0:T(8,128)S(1)}) custom-call(bf16[32,128,512]{2,1,0:T(8,128)(2,1)} %all_to_all.12.blocks_ref, f32[128,512]{1,0:T(8,128)S(1)} %bitcast.31, f32[128,512]{1,0:T(8,128)S(1)} %bitcast.32, bf16[4096,512]{1,0:T(8,128)(2,1)} %proj_ref.1, ...), custom_call_target="tpu_custom_call" | custom-call | tf_op jit(solution)/shard_map/pallas_call | solution.py:100
  119.9 1.0 copy.49
  120.9 0.7 copy.50
  121.6 0.7 copy.51
Async XLA Ops:
  0.6 1.2 %copy-start = (bf16[128,4096]{1,0:T(8,128)(2,1)S(1)}, bf16[128,4096]{1,0:T(8,128)(2,1)}, u32[]{:S(2)}) copy-start(bf16[128,4096]{1,0:T(8,128)(2,1)} %param.6) | copy-start | bytes 3145732
  26.7 4.8 %copy-start.4 = (bf16[512,4096]{1,0:T(8,128)(2,1)S(1)}, bf16[512,4096]{1,0:T(8,128)(2,1)}, u32[]{:S(2)}) copy-start(bf16[512,4096]{1,0:T(8,128)(2,1)} %param.7) | copy-start | bytes 12582916
  34.1 59.5 %copy-start.1 = (bf16[128,4096]{1,0:T(8,128)(2,1)S(1)}, bf16[128,4096]{1,0:T(8,128)(2,1)}, u32[]{:S(2)}) copy-start(bf16[128,4096]{1,0:T(8,128)(2,1)} %weight_ref.1) | copy-start | bytes 3145732
  34.1 59.5 %copy-start.2 = (f32[1,128,512]{2,1,0:T(8,128)S(1)}, f32[1,128,512]{2,1,0:T(8,128)}, u32[]{:S(2)}) copy-start(f32[1,128,512]{2,1,0:T(8,128)} %param.10) | copy-start | bytes 786436
  34.2 59.5 %copy-start.3 = (f32[1,128,512]{2,1,0:T(8,128)S(1)}, f32[1,128,512]{2,1,0:T(8,128)}, u32[]{:S(2)}) copy-start(f32[1,128,512]{2,1,0:T(8,128)} %param.11) | copy-start | bytes 786436

commit v6 on v5

--- a/solution.py
+++ b/solution.py
@@ -122,12 +122,58 @@
     )(blocks, first_moment, second_moment, projector, weight)
 
 
+def chip_gather_kernel(q_ref, out_ref, recv, send_sem, recv_sem):
+    me = lax.axis_index("tensor")
+    core_peer = me + 1 - 2 * lax.rem(me, 2)
+    chip_peer = lax.rem(me + 2, 4)
+    barrier = pltpu.get_barrier_semaphore()
+    for peer in (core_peer, chip_peer):
+        pl.semaphore_signal(barrier, inc=1, device_id={"tensor": peer}, device_id_type=MESH_ID)
+    pl.semaphore_wait(barrier, 2)
+
+    def send(src, slot, peer):
+        copy = pltpu.make_async_remote_copy(
+            src_ref=src,
+            dst_ref=recv.at[slot],
+            send_sem=send_sem.at[slot],
+            recv_sem=recv_sem.at[slot],
+            device_id={"tensor": peer},
+            device_id_type=MESH_ID,
+        )
+        copy.start()
+        return copy
+
+    across = send(q_ref, 1, chip_peer)
+    beside = send(q_ref, 0, core_peer)
+    out_ref[me] = q_ref[...]
+    across.wait()
+    forward = send(recv.at[1], 2, core_peer)
+    out_ref[chip_peer] = recv[1]
+    beside.wait()
+    out_ref[core_peer] = recv[0]
+    forward.wait()
+    out_ref[3 - me] = recv[2]
+
+
+def chip_gather(q):
+    return pl.pallas_call(
+        chip_gather_kernel,
+        out_shape=jax.ShapeDtypeStruct((4,) + q.shape, q.dtype),
+        in_specs=[pl.BlockSpec(memory_space=pltpu.VMEM)],
+        out_specs=pl.BlockSpec(memory_space=pltpu.VMEM),
+        scratch_shapes=[
+            pltpu.VMEM((3,) + q.shape, q.dtype),
+            pltpu.SemaphoreType.DMA((3,)),
+            pltpu.SemaphoreType.DMA((3,)),
+        ],
+        compiler_params=pltpu.CompilerParams(collective_id=1, has_side_effects=True),
+    )(q)
+
+
 def per_device(acts, out_grad, projector, weight, first_moment, second_moment):
     token_proj = jnp.dot(acts, projector, preferred_element_type=jnp.float32)
-    peers = lax.axis_size("tensor")
-    whole_proj = lax.all_to_all(
-        jnp.tile(token_proj, (peers, 1)), "tensor", split_axis=0, concat_axis=0, tiled=True
-    )
+    assert lax.axis_size("tensor") == 4
+    whole_proj = chip_gather(token_proj).reshape(-1, token_proj.shape[1])
     proj_hi = whole_proj.astype(jnp.bfloat16)
     proj_lo = (whole_proj - proj_hi.astype(jnp.float32)).astype(jnp.bfloat16)
     owners = lax.axis_size("dp")

time: 123 us -> 121 us (0.984)
  blocking collectives: 79.8 us -> 60.7 us
  Pallas kernels: 26.2 us -> 42.1 us
  other arithmetic: 0.14 us -> 1.83 us
    all_to_all x1 -> x0, blocking collectives: 20.3 us -> none  [per_device(): lax.all_to_all(jnp.tile(token_proj, (peers, 1)), 'tensor', split_axis=0,...]
    pallas_call x0 -> x1, Pallas kernels: none -> 13.4 us  [chip_gather(): pl.pallas_call(chip_gather_kernel, out_shape=jax.ShapeDtypeStruct((4,) +...]
    pallas_call x1, Pallas kernels: 26.2 us -> 28.7 us  [tail(): pl.pallas_call(functools.partial(tail_kernel, n), out_shape=(jax.ShapeDty...]
    convert_element_type x1, other arithmetic: 0.14 us -> 1.83 us  [per_device(): proj_lo = (whole_proj - proj_hi.astype(jnp.float32)).astype(jnp.bfloat16)]
where the time goes in v6:
time: 121 us; the launch traced here: 120 us
  blocking collectives  60.7 us (50%)
  Pallas kernels  42.1 us (35%)
  matrix products  11 us (9%)
  local copies, waits for them, and re-layouts  3.63 us (3%)
  other arithmetic  1.83 us (2%)
    all_to_all x1, blocking collectives, per_device(): lax.all_to_all(partial.astype(jnp.bfloat16), 'dp', split_axis=0, concat_a...  60.7 us
    pallas_call x1, Pallas kernels, tail(): pl.pallas_call(functools.partial(tail_kernel, n), out_shape=(jax.ShapeDty...  28.7 us
    pallas_call x1, Pallas kernels, chip_gather(): pl.pallas_call(chip_gather_kernel, out_shape=jax.ShapeDtypeStruct((4,) +...  13.4 us
    dot_general x1, matrix products, per_device(): lax.dot_general(grad_blocks, proj_lo, dims, preferred_element_type=jnp.fl...  4.78 us
    unnamed x13, local copies, waits for them, and re-layouts  3.63 us
    dot_general x1, matrix products, per_device(): token_proj = jnp.dot(acts, projector, preferred_element_type=jnp.float32)  3.61 us
    dot_general x1, matrix products, per_device(): lax.dot_general(grad_blocks, proj_hi, dims, preferred_element_type=jnp.fl...  2.65 us

profile of v6, /device:TPU:0, one launch (start us, length us, event | category | flops | bytes accessed | tf_op | source)
XLA Modules:
  0.0 120.0 jit_solution(641408761548770404)
XLA Ops:
  0.6 0.0 copy-start
  0.6 1.2 %copy-done = bf16[128,4096]{1,0:T(8,128)(2,1)S(1)} copy-done((bf16[128,4096]{1,0:T(8,128)(2,1)S(1)}, bf16[128,4096]{1,0:T(8,128)(2,1)}, u32[]{:S(2)}) %copy-start) | copy-done | bytes 1048600
  1.9 3.6 %fusion.9.q_ref = f32[128,512]{1,0:T(8,128)} fusion(bf16[128,4096]{1,0:T(8,128)(2,1)S(1)} %copy-done, bf16[4096,512]{1,0:T(8,128)(2,1)} %proj_ref.1), kind=kOutput, calls=%fused_computation.9 | convolution fusion | flops 536870912 | bytes 5505024 | tf_op jit(solution)/shard_map/dot_general | solution.py:174
  5.5 13.4 %shard_map.85 = f32[4,128,512]{2,1,0:T(8,128)} custom-call(f32[128,512]{1,0:T(8,128)} %fusion.9.q_ref), custom_call_target="tpu_custom_call" | custom-call | tf_op jit(solution)/shard_map/pallas_call | solution.py:159
  18.9 1.8 %subtract_convert_fusion = (bf16[4,128,512]{2,1,0:T(8,128)(2,1)S(1)}, bf16[4,128,512]{2,1,0:T(8,128)(2,1)S(1)}) fusion(f32[4,128,512]{2,1,0:T(8,128)} %shard_map.85), kind=kLoop, calls=%fused_computation.8 | loop fusion | flops 1048576 | bytes 2097152 | tf_op jit(solution)/shard_map/convert_element_type | solution.py:178
  20.7 0.0 copy-start.4
  20.7 4.8 %fusion.1 = f32[512,32,128]{0,2,1:T(8,128)S(1)} fusion(bf16[512,512,1]{1,0,2:T(8,128)(2,1)S(1)} %bitcast.35, bf16[512,4096]{1,0:T(8,128)(2,1)} %param.7), kind=kOutput, calls=%fused_computation.2 | convolution fusion | flops 2147483648 | bytes 13107200 | tf_op jit(solution)/shard_map/dot_general | solution.py:184
  25.5 0.0 copy-done.4
  25.5 2.7 %fusion = bf16[32,128,512]{2,1,0:T(8,128)(2,1)S(1)} fusion(f32[512,32,128]{0,2,1:T(8,128)S(1)} %fusion.1, bf16[512,512,1]{1,0,2:T(8,128)(2,1)S(1)} %bitcast.34, bf16[512,4096]{1,0:T(8,128)(2,1)S(1)} %copy-done.4), kind=kOutput, calls=%fused_computation.1 | convolution fusion | flops 2151677952 | bytes 17301504 | tf_op jit(solution)/shard_map/dot_general | solution.py:182
  28.2 0.0 copy-start.1
  28.2 0.0 copy-start.2
  28.2 0.0 copy-start.3
  28.2 60.7 %all_to_all.5.blocks_ref = bf16[32,128,512]{2,1,0:T(8,128)(2,1)} all-to-all(bf16[32,128,512]{2,1,0:T(8,128)(2,1)S(1)} %fusion), channel_id=1, replica_groups=mesh['dp'=32,'tensor'=4] {'dp'}, dimensions={0} | all-to-all | bytes 8388608 | tf_op jit(solution)/shard_map/all_to_all | solution.py:185
  88.9 0.0 copy-done.1
  88.9 0.0 copy-done.2
  88.9 0.0 copy-done.3
  88.9 28.7 %shard_map.86 = (bf16[128,4096]{1,0:T(8,128)(2,1)S(1)}, f32[128,512]{1,0:T(8,128)S(1)}, f32[128,512]{1,0:T(8,128)S(1)}) custom-call(bf16[32,128,512]{2,1,0:T(8,128)(2,1)} %all_to_all.5.blocks_ref, f32[128,512]{1,0:T(8,128)S(1)} %bitcast.30, f32[128,512]{1,0:T(8,128)S(1)} %bitcast.31, bf16[4096,512]{1,0:T(8,128)(2,1)} %proj_ref.1, bf16[128,4096]{1,0:T(8,128)(2,1)S(1)} %copy-done.1), custom_call_target="tpu_custom_call" | custom-call | tf_op jit(solution)/shard_map/pallas_call | solution.py:100
  117.6 1.0 copy.35
  118.5 0.7 copy.36
  119.2 0.7 copy.37
Async XLA Ops:
  0.6 1.2 %copy-start = (bf16[128,4096]{1,0:T(8,128)(2,1)S(1)}, bf16[128,4096]{1,0:T(8,128)(2,1)}, u32[]{:S(2)}) copy-start(bf16[128,4096]{1,0:T(8,128)(2,1)} %param.6) | copy-start | bytes 3145732
  20.7 4.8 %copy-start.4 = (bf16[512,4096]{1,0:T(8,128)(2,1)S(1)}, bf16[512,4096]{1,0:T(8,128)(2,1)}, u32[]{:S(2)}) copy-start(bf16[512,4096]{1,0:T(8,128)(2,1)} %param.7) | copy-start | bytes 12582916
  28.2 60.7 %copy-start.1 = (bf16[128,4096]{1,0:T(8,128)(2,1)S(1)}, bf16[128,4096]{1,0:T(8,128)(2,1)}, u32[]{:S(2)}) copy-start(bf16[128,4096]{1,0:T(8,128)(2,1)} %weight_ref.1) | copy-start | bytes 3145732
  28.2 60.7 %copy-start.2 = (f32[1,128,512]{2,1,0:T(8,128)S(1)}, f32[1,128,512]{2,1,0:T(8,128)}, u32[]{:S(2)}) copy-start(f32[1,128,512]{2,1,0:T(8,128)} %param.10) | copy-start | bytes 786436
  28.2 60.7 %copy-start.3 = (f32[1,128,512]{2,1,0:T(8,128)S(1)}, f32[1,128,512]{2,1,0:T(8,128)}, u32[]{:S(2)}) copy-start(f32[1,128,512]{2,1,0:T(8,128)} %param.11) | copy-start | bytes 786436

commit v7 on v6

--- a/solution.py
+++ b/solution.py
@@ -39,7 +39,6 @@
         pl.semaphore_signal(
             barrier, inc=1, device_id=(lax.rem(me + k, n), col), device_id_type=MESH_ID
         )
-    pl.semaphore_wait(barrier, n - 1)
 
     total[...] = blocks_ref[0].astype(jnp.float32)
 
@@ -53,20 +52,20 @@
     new_second_ref[...] = new_second
     direction_ref[...] = direction
 
-    def update_block(j, carry):
-        start = pl.multiple_of(j * rows, rows)
-        update[j] = lax.dot_general(
-            proj_ref[pl.ds(start, rows), :],
+    update[...] = (
+        lax.dot_general(
+            proj_ref[...],
             direction_ref[...],
             (((1,), (1,)), ((), ())),
             preferred_element_type=jnp.float32,
-        ).astype(jnp.bfloat16)
-        return carry
-
-    lax.fori_loop(0, n, update_block, 0)
+        )
+        .astype(jnp.bfloat16)
+        .reshape(update.shape)
+    )
     local = pltpu.make_async_copy(update, sendbuf, local_sem)
     local.start()
     local.wait()
+    pl.semaphore_wait(barrier, n - 1)
     copies = []
     for k in range(1, n):
         dest = lax.rem(me + k, n)

time: 121 us -> 114 us (0.942)
  Pallas kernels: 42.1 us -> 34.8 us
    pallas_call x1, Pallas kernels: 28.7 us -> 21.4 us  [tail(): pl.pallas_call(functools.partial(tail_kernel, n), out_shape=(jax.ShapeDty...]
where the time goes in v7:
time: 114 us; the launch traced here: 113 us
  blocking collectives  60.7 us (53%)
  Pallas kernels  34.8 us (31%)
  matrix products  11 us (10%)
  local copies, waits for them, and re-layouts  3.63 us (3%)
  other arithmetic  1.83 us (2%)
    all_to_all x1, blocking collectives, per_device(): lax.all_to_all(partial.astype(jnp.bfloat16), 'dp', split_axis=0, concat_a...  60.7 us
    pallas_call x1, Pallas kernels, tail(): pl.pallas_call(functools.partial(tail_kernel, n), out_shape=(jax.ShapeDty...  21.4 us
    pallas_call x1, Pallas kernels, chip_gather(): pl.pallas_call(chip_gather_kernel, out_shape=jax.ShapeDtypeStruct((4,) +...  13.4 us
    dot_general x1, matrix products, per_device(): lax.dot_general(grad_blocks, proj_lo, dims, preferred_element_type=jnp.fl...  4.78 us
    unnamed x13, local copies, waits for them, and re-layouts  3.63 us
    dot_general x1, matrix products, per_device(): token_proj = jnp.dot(acts, projector, preferred_element_type=jnp.float32)  3.61 us
    dot_general x1, matrix products, per_device(): lax.dot_general(grad_blocks, proj_hi, dims, preferred_element_type=jnp.fl...  2.65 us

profile of v7, /device:TPU:0, one launch (start us, length us, event | category | flops | bytes accessed | tf_op | source)
XLA Modules:
  0.0 112.7 jit_solution(6670146131741565209)
XLA Ops:
  0.6 0.0 copy-start
  0.6 1.2 %copy-done = bf16[128,4096]{1,0:T(8,128)(2,1)S(1)} copy-done((bf16[128,4096]{1,0:T(8,128)(2,1)S(1)}, bf16[128,4096]{1,0:T(8,128)(2,1)}, u32[]{:S(2)}) %copy-start) | copy-done | bytes 1048600
  1.9 3.6 %fusion.9.q_ref = f32[128,512]{1,0:T(8,128)} fusion(bf16[128,4096]{1,0:T(8,128)(2,1)S(1)} %copy-done, bf16[4096,512]{1,0:T(8,128)(2,1)} %proj_ref.1), kind=kOutput, calls=%fused_computation.9 | convolution fusion | flops 536870912 | bytes 5505024 | tf_op jit(solution)/shard_map/dot_general | solution.py:173
  5.5 13.4 %shard_map.85 = f32[4,128,512]{2,1,0:T(8,128)} custom-call(f32[128,512]{1,0:T(8,128)} %fusion.9.q_ref), custom_call_target="tpu_custom_call" | custom-call | tf_op jit(solution)/shard_map/pallas_call | solution.py:158
  18.9 1.8 %subtract_convert_fusion = (bf16[4,128,512]{2,1,0:T(8,128)(2,1)S(1)}, bf16[4,128,512]{2,1,0:T(8,128)(2,1)S(1)}) fusion(f32[4,128,512]{2,1,0:T(8,128)} %shard_map.85), kind=kLoop, calls=%fused_computation.8 | loop fusion | flops 1048576 | bytes 2097152 | tf_op jit(solution)/shard_map/convert_element_type | solution.py:177
  20.7 0.0 copy-start.4
  20.7 4.8 %fusion.1 = f32[512,32,128]{0,2,1:T(8,128)S(1)} fusion(bf16[512,512,1]{1,0,2:T(8,128)(2,1)S(1)} %bitcast.35, bf16[512,4096]{1,0:T(8,128)(2,1)} %param.7), kind=kOutput, calls=%fused_computation.2 | convolution fusion | flops 2147483648 | bytes 13107200 | tf_op jit(solution)/shard_map/dot_general | solution.py:183
  25.5 0.0 copy-done.4
  25.5 2.7 %fusion = bf16[32,128,512]{2,1,0:T(8,128)(2,1)S(1)} fusion(f32[512,32,128]{0,2,1:T(8,128)S(1)} %fusion.1, bf16[512,512,1]{1,0,2:T(8,128)(2,1)S(1)} %bitcast.34, bf16[512,4096]{1,0:T(8,128)(2,1)S(1)} %copy-done.4), kind=kOutput, calls=%fused_computation.1 | convolution fusion | flops 2151677952 | bytes 17301504 | tf_op jit(solution)/shard_map/dot_general | solution.py:181
  28.2 0.0 copy-start.1
  28.2 0.0 copy-start.2
  28.2 0.0 copy-start.3
  28.2 60.7 %all_to_all.5.blocks_ref = bf16[32,128,512]{2,1,0:T(8,128)(2,1)} all-to-all(bf16[32,128,512]{2,1,0:T(8,128)(2,1)S(1)} %fusion), channel_id=1, replica_groups=mesh['dp'=32,'tensor'=4] {'dp'}, dimensions={0} | all-to-all | bytes 8388608 | tf_op jit(solution)/shard_map/all_to_all | solution.py:184
  88.9 0.0 copy-done.1
  88.9 0.0 copy-done.2
  88.9 0.0 copy-done.3
  88.9 21.4 %shard_map.86 = (bf16[128,4096]{1,0:T(8,128)(2,1)S(1)}, f32[128,512]{1,0:T(8,128)S(1)}, f32[128,512]{1,0:T(8,128)S(1)}) custom-call(bf16[32,128,512]{2,1,0:T(8,128)(2,1)} %all_to_all.5.blocks_ref, f32[128,512]{1,0:T(8,128)S(1)} %bitcast.30, f32[128,512]{1,0:T(8,128)S(1)} %bitcast.31, bf16[4096,512]{1,0:T(8,128)(2,1)} %proj_ref.1, bf16[128,4096]{1,0:T(8,128)(2,1)S(1)} %copy-done.1), custom_call_target="tpu_custom_call" | custom-call | tf_op jit(solution)/shard_map/pallas_call | solution.py:99
  110.3 1.0 copy.35
  111.3 0.7 copy.36
  112.0 0.7 copy.37
Async XLA Ops:
  0.6 1.2 %copy-start = (bf16[128,4096]{1,0:T(8,128)(2,1)S(1)}, bf16[128,4096]{1,0:T(8,128)(2,1)}, u32[]{:S(2)}) copy-start(bf16[128,4096]{1,0:T(8,128)(2,1)} %param.6) | copy-start | bytes 3145732
  20.7 4.8 %copy-start.4 = (bf16[512,4096]{1,0:T(8,128)(2,1)S(1)}, bf16[512,4096]{1,0:T(8,128)(2,1)}, u32[]{:S(2)}) copy-start(bf16[512,4096]{1,0:T(8,128)(2,1)} %param.7) | copy-start | bytes 12582916
  28.2 60.7 %copy-start.1 = (bf16[128,4096]{1,0:T(8,128)(2,1)S(1)}, bf16[128,4096]{1,0:T(8,128)(2,1)}, u32[]{:S(2)}) copy-start(bf16[128,4096]{1,0:T(8,128)(2,1)} %weight_ref.1) | copy-start | bytes 3145732
  28.2 60.7 %copy-start.2 = (f32[1,128,512]{2,1,0:T(8,128)S(1)}, f32[1,128,512]{2,1,0:T(8,128)}, u32[]{:S(2)}) copy-start(f32[1,128,512]{2,1,0:T(8,128)} %param.10) | copy-start | bytes 786436
  28.2 60.7 %copy-start.3 = (f32[1,128,512]{2,1,0:T(8,128)S(1)}, f32[1,128,512]{2,1,0:T(8,128)}, u32[]{:S(2)}) copy-start(f32[1,128,512]{2,1,0:T(8,128)} %param.11) | copy-start | bytes 786436

commit v8 on v7

--- a/solution.py
+++ b/solution.py
@@ -121,13 +121,19 @@
     )(blocks, first_moment, second_moment, projector, weight)
 
 
-def chip_gather_kernel(q_ref, out_ref, recv, send_sem, recv_sem):
+def chip_gather_kernel(
+    acts_ref, proj_ref, hi_ref, lo_ref, q_buf, send_buf, recv, local_sem, send_sem, recv_sem
+):
     me = lax.axis_index("tensor")
     core_peer = me + 1 - 2 * lax.rem(me, 2)
     chip_peer = lax.rem(me + 2, 4)
     barrier = pltpu.get_barrier_semaphore()
     for peer in (core_peer, chip_peer):
         pl.semaphore_signal(barrier, inc=1, device_id={"tensor": peer}, device_id_type=MESH_ID)
+    q_buf[...] = jnp.dot(acts_ref[...], proj_ref[...], preferred_element_type=jnp.float32)
+    local = pltpu.make_async_copy(q_buf, send_buf, local_sem)
+    local.start()
+    local.wait()
     pl.semaphore_wait(barrier, 2)
 
     def send(src, slot, peer):
@@ -142,39 +148,53 @@
         copy.start()
         return copy
 
-    across = send(q_ref, 1, chip_peer)
-    beside = send(q_ref, 0, core_peer)
-    out_ref[me] = q_ref[...]
+    def split(slot, piece):
+        hi = piece.astype(jnp.bfloat16)
+        hi_ref[slot] = hi
+        lo_ref[slot] = (piece - hi.astype(jnp.float32)).astype(jnp.bfloat16)
+
+    across = send(send_buf, 1, chip_peer)
+    beside = send(send_buf, 0, core_peer)
+    split(me, send_buf[...])
     across.wait()
     forward = send(recv.at[1], 2, core_peer)
-    out_ref[chip_peer] = recv[1]
+    split(chip_peer, recv[1])
     beside.wait()
-    out_ref[core_peer] = recv[0]
+    split(core_peer, recv[0])
     forward.wait()
-    out_ref[3 - me] = recv[2]
-
-
-def chip_gather(q):
+    split(3 - me, recv[2])
+
+
+def chip_gather(acts, projector):
+    shape = (acts.shape[0], projector.shape[1])
+    vmem = pl.BlockSpec(memory_space=pltpu.VMEM)
     return pl.pallas_call(
         chip_gather_kernel,
-        out_shape=jax.ShapeDtypeStruct((4,) + q.shape, q.dtype),
-        in_specs=[pl.BlockSpec(memory_space=pltpu.VMEM)],
-        out_specs=pl.BlockSpec(memory_space=pltpu.VMEM),
+        out_shape=(
+            jax.ShapeDtypeStruct((4,) + shape, jnp.bfloat16),
+            jax.ShapeDtypeStruct((4,) + shape, jnp.bfloat16),
+        ),
+        in_specs=[vmem, vmem],
+        out_specs=(vmem, vmem),
         scratch_shapes=[
-            pltpu.VMEM((3,) + q.shape, q.dtype),
+            pltpu.VMEM(shape, jnp.float32),
+            pltpu.VMEM(shape, jnp.float32),
+            pltpu.VMEM((3,) + shape, jnp.float32),
+            pltpu.SemaphoreType.DMA(()),
             pltpu.SemaphoreType.DMA((3,)),
             pltpu.SemaphoreType.DMA((3,)),
         ],
-        compiler_params=pltpu.CompilerParams(collective_id=1, has_side_effects=True),
-    )(q)
+        compiler_params=pltpu.CompilerParams(
+            collective_id=1, has_side_effects=True, vmem_limit_bytes=48 * 1024 * 1024
+        ),
+    )(acts, projector)
 
 
 def per_device(acts, out_grad, projector, weight, first_moment, second_moment):
-    token_proj = jnp.dot(acts, projector, preferred_element_type=jnp.float32)
     assert lax.axis_size("tensor") == 4
-    whole_proj = chip_gather(token_proj).reshape(-1, token_proj.shape[1])
-    proj_hi = whole_proj.astype(jnp.bfloat16)
-    proj_lo = (whole_proj - proj_hi.astype(jnp.float32)).astype(jnp.bfloat16)
+    proj_hi, proj_lo = chip_gather(acts, projector)
+    proj_hi = proj_hi.reshape(-1, proj_hi.shape[2])
+    proj_lo = proj_lo.reshape(-1, proj_lo.shape[2])
     owners = lax.axis_size("dp")
     grad_blocks = out_grad.reshape(out_grad.shape[0], owners, -1)
     dims = (((0,), (0,)), ((), ()))

time: 114 us -> 106 us (0.930)
  matrix products: 11 us -> 4.79 us
  other arithmetic: 1.83 us -> 0 us
    dot_general x1 -> x0, matrix products: 3.61 us -> none  [per_device(): token_proj = jnp.dot(acts, projector, preferred_element_type=jnp.float32)]
    dot_general x1, matrix products: 4.78 us -> 2.38 us  [per_device(): lax.dot_general(grad_blocks, proj_lo, dims, preferred_element_type=jnp.fl...]
    convert_element_type x1 -> x0, other arithmetic: 1.83 us -> none  [per_device(): proj_lo = (whole_proj - proj_hi.astype(jnp.float32)).astype(jnp.bfloat16)]
where the time goes in v8:
time: 106 us; the launch traced here: 105 us
  blocking collectives  60.6 us (57%)
  Pallas kernels  35.3 us (33%)
  matrix products  4.79 us (5%)
  local copies, waits for them, and re-layouts  3.62 us (3%)
    all_to_all x1, blocking collectives, per_device(): lax.all_to_all(partial.astype(jnp.bfloat16), 'dp', split_axis=0, concat_a...  60.6 us
    pallas_call x1, Pallas kernels, tail(): pl.pallas_call(functools.partial(tail_kernel, n), out_shape=(jax.ShapeDty...  21.4 us
    pallas_call x1, Pallas kernels, chip_gather(): pl.pallas_call(chip_gather_kernel, out_shape=(jax.ShapeDtypeStruct((4,) +...  13.9 us
    unnamed x13, local copies, waits for them, and re-layouts  3.62 us
    dot_general x1, matrix products, per_device(): lax.dot_general(grad_blocks, proj_hi, dims, preferred_element_type=jnp.fl...  2.41 us
    dot_general x1, matrix products, per_device(): lax.dot_general(grad_blocks, proj_lo, dims, preferred_element_type=jnp.fl...  2.38 us

profile of v8, /device:TPU:0, one launch (start us, length us, event | category | flops | bytes accessed | tf_op | source)
XLA Modules:
  0.0 105.0 jit_solution(4448835025907455214)
XLA Ops:
  0.6 0.0 copy-start
  0.6 1.2 %copy-done = bf16[128,4096]{1,0:T(8,128)(2,1)S(1)} copy-done((bf16[128,4096]{1,0:T(8,128)(2,1)S(1)}, bf16[128,4096]{1,0:T(8,128)(2,1)}, u32[]{:S(2)}) %copy-start) | copy-done | bytes 1048600
  1.9 0.0 copy-start.4
  1.9 13.9 %shard_map.85 = (bf16[4,128,512]{2,1,0:T(8,128)(2,1)S(1)}, bf16[4,128,512]{2,1,0:T(8,128)(2,1)S(1)}) custom-call(bf16[128,4096]{1,0:T(8,128)(2,1)S(1)} %copy-done, bf16[4096,512]{1,0:T(8,128)(2,1)} %proj_ref.3), custom_call_target="tpu_custom_call" | custom-call | tf_op jit(solution)/shard_map/pallas_call | solution.py:171
  15.8 0.0 copy-done.4
  15.8 2.4 %fusion.1 = f32[512,32,128]{0,2,1:T(8,128)S(1)} fusion(bf16[512,512,1]{1,0,2:T(8,128)(2,1)S(1)} %bitcast.29, bf16[512,4096]{1,0:T(8,128)(2,1)S(1)} %copy-done.4), kind=kOutput, calls=%fused_computation.2 | convolution fusion | flops 2147483648 | bytes 13107200 | tf_op jit(solution)/shard_map/dot_general | solution.py:203
  18.2 2.4 %fusion = bf16[32,128,512]{2,1,0:T(8,128)(2,1)S(1)} fusion(f32[512,32,128]{0,2,1:T(8,128)S(1)} %fusion.1, bf16[512,512,1]{1,0,2:T(8,128)(2,1)S(1)} %bitcast.28, bf16[512,4096]{1,0:T(8,128)(2,1)S(1)} %copy-done.4), kind=kOutput, calls=%fused_computation.1 | convolution fusion | flops 2151677952 | bytes 17301504 | tf_op jit(solution)/shard_map/dot_general | solution.py:201
  20.6 0.0 copy-start.1
  20.6 0.0 copy-start.2
  20.6 0.0 copy-start.3
  20.6 60.6 %all_to_all.5.blocks_ref = bf16[32,128,512]{2,1,0:T(8,128)(2,1)} all-to-all(bf16[32,128,512]{2,1,0:T(8,128)(2,1)S(1)} %fusion), channel_id=1, replica_groups=mesh['dp'=32,'tensor'=4] {'dp'}, dimensions={0} | all-to-all | bytes 8388608 | tf_op jit(solution)/shard_map/all_to_all | solution.py:204
  81.2 0.0 copy-done.1
  81.3 0.0 copy-done.2
  81.3 0.0 copy-done.3
  81.3 21.4 %shard_map.86 = (bf16[128,4096]{1,0:T(8,128)(2,1)S(1)}, f32[128,512]{1,0:T(8,128)S(1)}, f32[128,512]{1,0:T(8,128)S(1)}) custom-call(bf16[32,128,512]{2,1,0:T(8,128)(2,1)} %all_to_all.5.blocks_ref, f32[128,512]{1,0:T(8,128)S(1)} %bitcast.30, f32[128,512]{1,0:T(8,128)S(1)} %bitcast.31, bf16[4096,512]{1,0:T(8,128)(2,1)} %proj_ref.3, bf16[128,4096]{1,0:T(8,128)(2,1)S(1)} %copy-done.1), custom_call_target="tpu_custom_call" | custom-call | tf_op jit(solution)/shard_map/pallas_call | solution.py:99
  102.6 1.0 copy.35
  103.6 0.7 copy.36
  104.3 0.7 copy.37
Async XLA Ops:
  0.6 1.2 %copy-start = (bf16[128,4096]{1,0:T(8,128)(2,1)S(1)}, bf16[128,4096]{1,0:T(8,128)(2,1)}, u32[]{:S(2)}) copy-start(bf16[128,4096]{1,0:T(8,128)(2,1)} %acts_ref.1) | copy-start | bytes 3145732
  1.9 13.9 %copy-start.4 = (bf16[512,4096]{1,0:T(8,128)(2,1)S(1)}, bf16[512,4096]{1,0:T(8,128)(2,1)}, u32[]{:S(2)}) copy-start(bf16[512,4096]{1,0:T(8,128)(2,1)} %param.7) | copy-start | bytes 12582916
  20.6 60.7 %copy-start.1 = (bf16[128,4096]{1,0:T(8,128)(2,1)S(1)}, bf16[128,4096]{1,0:T(8,128)(2,1)}, u32[]{:S(2)}) copy-start(bf16[128,4096]{1,0:T(8,128)(2,1)} %weight_ref.1) | copy-start | bytes 3145732
  20.6 60.6 %copy-start.2 = (f32[1,128,512]{2,1,0:T(8,128)S(1)}, f32[1,128,512]{2,1,0:T(8,128)}, u32[]{:S(2)}) copy-start(f32[1,128,512]{2,1,0:T(8,128)} %param.10) | copy-start | bytes 786436
  20.6 60.6 %copy-start.3 = (f32[1,128,512]{2,1,0:T(8,128)S(1)}, f32[1,128,512]{2,1,0:T(8,128)}, u32[]{:S(2)}) copy-start(f32[1,128,512]{2,1,0:T(8,128)} %param.11) | copy-start | bytes 786436

commit v9 on v8

--- a/solution.py
+++ b/solution.py
@@ -25,13 +25,15 @@
     return (new_first, new_second, direction)
 
 
-def tail_kernel(
-    n, blocks_ref, first_ref, second_ref, proj_ref, weight_ref,
+def step_kernel(
+    n, pieces, grad_ref, hi_ref, lo_ref, first_ref, second_ref, proj_ref, weight_ref,
     new_weight_ref, new_first_ref, new_second_ref,
-    total, direction_ref, update, sendbuf, recv, local_sem, send_sem, recv_sem,
+    part, part_out, blocks, total, direction_ref, update, sendbuf, recv,
+    local_sem, part_send, part_recv, send_sem, recv_sem,
 ):
     me = lax.axis_index("dp")
     col = lax.axis_index("tensor")
+    owned = part.shape[1]
     rows = sendbuf.shape[1]
     width = sendbuf.shape[2]
     barrier = pltpu.get_barrier_semaphore()
@@ -40,10 +42,44 @@
             barrier, inc=1, device_id=(lax.rem(me + k, n), col), device_id_type=MESH_ID
         )
 
-    total[...] = blocks_ref[0].astype(jnp.float32)
+    def partial_block(j, carry):
+        grad = grad_ref[:, pl.ds(pl.multiple_of(j * owned, owned), owned)]
+        dims = (((0,), (0,)), ((), ()))
+        term = lax.dot_general(grad, hi_ref[...], dims, preferred_element_type=jnp.float32)
+        term += lax.dot_general(grad, lo_ref[...], dims, preferred_element_type=jnp.float32)
+        part[j] = term.astype(jnp.bfloat16)
+        return carry
+
+    lax.fori_loop(0, n, partial_block, 0)
+    local = pltpu.make_async_copy(part, part_out, local_sem)
+    local.start()
+    local.wait()
+    pl.semaphore_wait(barrier, n - 1)
+    piece = owned // pieces
+
+    def part_copy(k, p):
+        dest = lax.rem(me + k, n)
+        span = pl.ds(pl.multiple_of(p * piece, piece), piece)
+        return pltpu.make_async_remote_copy(
+            src_ref=part_out.at[dest, span],
+            dst_ref=blocks.at[k, span],
+            send_sem=part_send.at[p, k],
+            recv_sem=part_recv.at[p, k],
+            device_id=(dest, col),
+            device_id_type=MESH_ID,
+        )
+
+    def start_part(i, carry):
+        part_copy(lax.rem(i, n - 1) + 1, i // (n - 1)).start()
+        return carry
+
+    lax.fori_loop(0, (n - 1) * pieces, start_part, 0)
+    total[...] = part_out[me].astype(jnp.float32)
 
     def add_block(k, carry):
-        total[...] += blocks_ref[k].astype(jnp.float32)
+        for p in range(pieces):
+            part_copy(k, p).wait()
+        total[...] += blocks[k].astype(jnp.float32)
         return carry
 
     lax.fori_loop(1, n, add_block, 0)
@@ -65,7 +101,6 @@
     local = pltpu.make_async_copy(update, sendbuf, local_sem)
     local.start()
     local.wait()
-    pl.semaphore_wait(barrier, n - 1)
     copies = []
     for k in range(1, n):
         dest = lax.rem(me + k, n)
@@ -92,33 +127,40 @@
         apply(lax.rem(me + n - k, n), recv[k])
 
 
-def tail(blocks, first_moment, second_moment, projector, weight):
-    n, hidden, rank = blocks.shape
+def step(out_grad, proj_hi, proj_lo, first_moment, second_moment, projector, weight, n):
+    pieces = 8
+    hidden = out_grad.shape[1] // n
+    rank = proj_hi.shape[1]
     rows = weight.shape[0]
     vmem = pl.BlockSpec(memory_space=pltpu.VMEM)
     return pl.pallas_call(
-        functools.partial(tail_kernel, n),
+        functools.partial(step_kernel, n, pieces),
         out_shape=(
             jax.ShapeDtypeStruct(weight.shape, weight.dtype),
             jax.ShapeDtypeStruct((hidden, rank), jnp.float32),
             jax.ShapeDtypeStruct((hidden, rank), jnp.float32),
         ),
-        in_specs=[vmem] * 5,
+        in_specs=[vmem] * 7,
         out_specs=(vmem, vmem, vmem),
         scratch_shapes=[
+            pltpu.VMEM((n, hidden, rank), jnp.bfloat16),
+            pltpu.VMEM((n, hidden, rank), jnp.bfloat16),
+            pltpu.VMEM((n, hidden, rank), jnp.bfloat16),
             pltpu.VMEM((hidden, rank), jnp.float32),
             pltpu.VMEM((hidden, rank), jnp.bfloat16),
             pltpu.VMEM((n, rows, hidden), jnp.bfloat16),
             pltpu.VMEM((n, rows, hidden), jnp.bfloat16),
             pltpu.VMEM((n, rows, hidden), jnp.bfloat16),
             pltpu.SemaphoreType.DMA(()),
+            pltpu.SemaphoreType.DMA((pieces, n)),
+            pltpu.SemaphoreType.DMA((pieces, n)),
             pltpu.SemaphoreType.DMA((n,)),
             pltpu.SemaphoreType.DMA((n,)),
         ],
         compiler_params=pltpu.CompilerParams(
-            collective_id=2, has_side_effects=True, vmem_limit_bytes=48 * 1024 * 1024
-        ),
-    )(blocks, first_moment, second_moment, projector, weight)
+            collective_id=2, has_side_effects=True, vmem_limit_bytes=64 * 1024 * 1024
+        ),
+    )(out_grad, proj_hi, proj_lo, first_moment, second_moment, projector, weight)
 
 
 def chip_gather_kernel(
@@ -195,17 +237,9 @@
     proj_hi, proj_lo = chip_gather(acts, projector)
     proj_hi = proj_hi.reshape(-1, proj_hi.shape[2])
     proj_lo = proj_lo.reshape(-1, proj_lo.shape[2])
-    owners = lax.axis_size("dp")
-    grad_blocks = out_grad.reshape(out_grad.shape[0], owners, -1)
-    dims = (((0,), (0,)), ((), ()))
-    partial = lax.dot_general(
-        grad_blocks, proj_hi, dims, preferred_element_type=jnp.float32
-    ) + lax.dot_general(grad_blocks, proj_lo, dims, preferred_element_type=jnp.float32)
-    blocks = lax.all_to_all(
-        partial.astype(jnp.bfloat16), "dp", split_axis=0, concat_axis=0, tiled=True
-    )
-    new_weight, new_first, new_second = tail(
-        blocks, first_moment[0], second_moment[0], projector, weight
+    new_weight, new_first, new_second = step(
+        out_grad, proj_hi, proj_lo, first_moment[0], second_moment[0], projector, weight,
+        lax.axis_size("dp"),
     )
     return (new_weight, new_first[None], new_second[None])
 

time: 106 us -> 118 us (1.11)
  Pallas kernels: 35.3 us -> 108 us
  blocking collectives: 60.6 us -> 0 us
  local copies, waits for them, and re-layouts: 3.62 us -> 8.44 us
  matrix products: 4.79 us -> 0 us
    pallas_call x1, Pallas kernels: 21.4 us -> 94.6 us  [step(): pl.pallas_call(functools.partial(step_kernel, n, pieces), out_shape=(jax....]
    all_to_all x1 -> x0, blocking collectives: 60.6 us -> none  [per_device(): lax.all_to_all(partial.astype(jnp.bfloat16), 'dp', split_axis=0, concat_a...]
    unnamed x13 -> x9, local copies, waits for them, and re-layouts: 3.62 us -> 8.44 us
    dot_general x2 -> x0, matrix products: 4.79 us -> none  [the longest x1 2.41 us: per_device(): lax.dot_general(grad_blocks, proj_hi, dims, preferred_element_type=jnp.fl...]
where the time goes in v9:
time: 118 us; the launch traced here: 117 us
  Pallas kernels  108 us (92%)
  local copies, waits for them, and re-layouts  8.44 us (7%)
    pallas_call x1, Pallas kernels, step(): pl.pallas_call(functools.partial(step_kernel, n, pieces), out_shape=(jax....  94.6 us
    pallas_call x1, Pallas kernels, chip_gather(): pl.pallas_call(chip_gather_kernel, out_shape=(jax.ShapeDtypeStruct((4,) +...  13.8 us
    unnamed x9, local copies, waits for them, and re-layouts  8.44 us

profile of v9, /device:TPU:0, one launch (start us, length us, event | category | flops | bytes accessed | tf_op | source)
XLA Modules:
  0.0 117.5 jit_solution(14367717611629876069)
XLA Ops:
  0.6 0.0 copy-start
  0.6 1.2 %copy-done = bf16[128,4096]{1,0:T(8,128)(2,1)S(1)} copy-done((bf16[128,4096]{1,0:T(8,128)(2,1)S(1)}, bf16[128,4096]{1,0:T(8,128)(2,1)}, u32[]{:S(2)}) %copy-start) | copy-done | bytes 1048600
  1.9 13.8 %shard_map.85 = (bf16[4,128,512]{2,1,0:T(8,128)(2,1)S(1)}, bf16[4,128,512]{2,1,0:T(8,128)(2,1)S(1)}) custom-call(bf16[128,4096]{1,0:T(8,128)(2,1)S(1)} %copy-done, bf16[4096,512]{1,0:T(8,128)(2,1)} %proj_ref.3), custom_call_target="tpu_custom_call" | custom-call | tf_op jit(solution)/shard_map/pallas_call | solution.py:213
  15.6 0.0 copy-start.1
  15.6 0.8 copy-done.1
  16.4 0.0 copy-start.2
  16.4 0.8 copy-done.2
  17.2 94.6 %shard_map.86 = (bf16[128,4096]{1,0:T(8,128)(2,1)}, f32[128,512]{1,0:T(8,128)}, f32[128,512]{1,0:T(8,128)}) custom-call(bf16[512,4096]{1,0:T(8,128)(2,1)} %grad_ref.1, bf16[512,512]{1,0:T(8,128)(2,1)} %bitcast.6, bf16[512,512]{1,0:T(8,128)(2,1)} %bitcast.7, f32[128,512]{1,0:T(8,128)} %bitcast.8, f32[128,512]{1,0:T(8,128)} %bitcast.9, ...), custom_call_target="tpu_custom_call" | custom-call | tf_op jit(solution)/shard_map/pallas_call | solution.py:136
  111.8 2.3 %copy.12 = bf16[128,4096]{1,0:T(8,128)(2,1)} copy(bf16[128,4096]{1,0:T(8,128)(2,1)} %get-tuple-element.16) | data formatting | bytes 2097152
  114.1 1.7 %copy.13 = f32[1,128,512]{2,1,0:T(8,128)} copy(f32[1,128,512]{2,1,0:T(8,128)} %bitcast.11) | data formatting | bytes 524288
  115.8 1.7 %copy.14 = f32[1,128,512]{2,1,0:T(8,128)} copy(f32[1,128,512]{2,1,0:T(8,128)} %bitcast.10) | data formatting | bytes 524288
Async XLA Ops:
  0.6 1.2 %copy-start = (bf16[128,4096]{1,0:T(8,128)(2,1)S(1)}, bf16[128,4096]{1,0:T(8,128)(2,1)}, u32[]{:S(2)}) copy-start(bf16[128,4096]{1,0:T(8,128)(2,1)} %acts_ref.1) | copy-start | bytes 3145732
  15.6 0.8 copy-start.1
  16.4 0.8 copy-start.2

commit v10 on v8

--- a/solution.py
+++ b/solution.py
@@ -26,7 +26,7 @@
 
 
 def tail_kernel(
-    n, blocks_ref, first_ref, second_ref, proj_ref, weight_ref,
+    n, pieces, blocks_ref, first_ref, second_ref, proj_ref, weight_ref,
     new_weight_ref, new_first_ref, new_second_ref,
     total, direction_ref, update, sendbuf, recv, local_sem, send_sem, recv_sem,
 ):
@@ -66,19 +66,25 @@
     local.start()
     local.wait()
     pl.semaphore_wait(barrier, n - 1)
-    copies = []
-    for k in range(1, n):
+    piece = rows // pieces
+
+    def block_copy(k, p):
         dest = lax.rem(me + k, n)
-        copy = pltpu.make_async_remote_copy(
-            src_ref=sendbuf.at[dest],
-            dst_ref=recv.at[k],
-            send_sem=send_sem.at[k],
-            recv_sem=recv_sem.at[k],
+        span = pl.ds(pl.multiple_of(p * piece, piece), piece)
+        return pltpu.make_async_remote_copy(
+            src_ref=sendbuf.at[dest, span],
+            dst_ref=recv.at[k, span],
+            send_sem=send_sem.at[p, k],
+            recv_sem=recv_sem.at[p, k],
             device_id=(dest, col),
             device_id_type=MESH_ID,
         )
-        copy.start()
-        copies.append(copy)
+
+    def start_block(i, carry):
+        block_copy(lax.rem(i, n - 1) + 1, i // (n - 1)).start()
+        return carry
+
+    lax.fori_loop(0, (n - 1) * pieces, start_block, 0)
 
     def apply(source, block):
         cols = pl.ds(pl.multiple_of(source * width, width), width)
@@ -87,9 +93,14 @@
         ).astype(jnp.bfloat16)
 
     apply(me, sendbuf[me])
-    for k, copy in enumerate(copies, 1):
-        copy.wait()
+
+    def land(k, carry):
+        for p in range(pieces):
+            block_copy(k, p).wait()
         apply(lax.rem(me + n - k, n), recv[k])
+        return carry
+
+    lax.fori_loop(1, n, land, 0)
 
 
 def tail(blocks, first_moment, second_moment, projector, weight):
@@ -97,7 +108,7 @@
     rows = weight.shape[0]
     vmem = pl.BlockSpec(memory_space=pltpu.VMEM)
     return pl.pallas_call(
-        functools.partial(tail_kernel, n),
+        functools.partial(tail_kernel, n, 4),
         out_shape=(
             jax.ShapeDtypeStruct(weight.shape, weight.dtype),
             jax.ShapeDtypeStruct((hidden, rank), jnp.float32),
@@ -112,8 +123,8 @@
             pltpu.VMEM((n, rows, hidden), jnp.bfloat16),
             pltpu.VMEM((n, rows, hidden), jnp.bfloat16),
             pltpu.SemaphoreType.DMA(()),
-            pltpu.SemaphoreType.DMA((n,)),
-            pltpu.SemaphoreType.DMA((n,)),
+            pltpu.SemaphoreType.DMA((4, n)),
+            pltpu.SemaphoreType.DMA((4, n)),
         ],
         compiler_params=pltpu.CompilerParams(
             collective_id=2, has_side_effects=True, vmem_limit_bytes=48 * 1024 * 1024

time: 106 us -> 107 us (level)
  Pallas kernels: 35.3 us -> 37.2 us
    pallas_call x1, Pallas kernels: 21.4 us -> 23.3 us  [tail(): pl.pallas_call(functools.partial(tail_kernel, n, 4), out_shape=(jax.Shape...]
where the time goes in v10:
time: 107 us
  blocking collectives  60.6 us (57%)
  Pallas kernels  37.2 us (35%)
  matrix products  4.79 us (4%)
  local copies, waits for them, and re-layouts  3.62 us (3%)
    all_to_all x1, blocking collectives, per_device(): lax.all_to_all(partial.astype(jnp.bfloat16), 'dp', split_axis=0, concat_a...  60.6 us
    pallas_call x1, Pallas kernels, tail(): pl.pallas_call(functools.partial(tail_kernel, n, 4), out_shape=(jax.Shape...  23.3 us
    pallas_call x1, Pallas kernels, chip_gather(): pl.pallas_call(chip_gather_kernel, out_shape=(jax.ShapeDtypeStruct((4,) +...  13.9 us
    unnamed x13, local copies, waits for them, and re-layouts  3.62 us
    dot_general x1, matrix products, per_device(): lax.dot_general(grad_blocks, proj_hi, dims, preferred_element_type=jnp.fl...  2.41 us
    dot_general x1, matrix products, per_device(): lax.dot_general(grad_blocks, proj_lo, dims, preferred_element_type=jnp.fl...  2.38 us

profile of v10, /device:TPU:0, one launch (start us, length us, event | category | flops | bytes accessed | tf_op | source)
XLA Modules:
  0.0 106.9 jit_solution(14818377108349642736)
XLA Ops:
  0.6 0.0 copy-start
  0.6 1.2 %copy-done = bf16[128,4096]{1,0:T(8,128)(2,1)S(1)} copy-done((bf16[128,4096]{1,0:T(8,128)(2,1)S(1)}, bf16[128,4096]{1,0:T(8,128)(2,1)}, u32[]{:S(2)}) %copy-start) | copy-done | bytes 1048600
  1.9 0.0 copy-start.4
  1.9 13.9 %shard_map.85 = (bf16[4,128,512]{2,1,0:T(8,128)(2,1)S(1)}, bf16[4,128,512]{2,1,0:T(8,128)(2,1)S(1)}) custom-call(bf16[128,4096]{1,0:T(8,128)(2,1)S(1)} %copy-done, bf16[4096,512]{1,0:T(8,128)(2,1)} %proj_ref.3), custom_call_target="tpu_custom_call" | custom-call | tf_op jit(solution)/shard_map/pallas_call | solution.py:182
  15.8 0.0 copy-done.4
  15.8 2.4 %fusion.1 = f32[512,32,128]{0,2,1:T(8,128)S(1)} fusion(bf16[512,512,1]{1,0,2:T(8,128)(2,1)S(1)} %bitcast.29, bf16[512,4096]{1,0:T(8,128)(2,1)S(1)} %copy-done.4), kind=kOutput, calls=%fused_computation.2 | convolution fusion | flops 2147483648 | bytes 13107200 | tf_op jit(solution)/shard_map/dot_general | solution.py:214
  18.2 2.4 %fusion = bf16[32,128,512]{2,1,0:T(8,128)(2,1)S(1)} fusion(f32[512,32,128]{0,2,1:T(8,128)S(1)} %fusion.1, bf16[512,512,1]{1,0,2:T(8,128)(2,1)S(1)} %bitcast.28, bf16[512,4096]{1,0:T(8,128)(2,1)S(1)} %copy-done.4), kind=kOutput, calls=%fused_computation.1 | convolution fusion | flops 2151677952 | bytes 17301504 | tf_op jit(solution)/shard_map/dot_general | solution.py:212
  20.6 0.0 copy-start.1
  20.6 0.0 copy-start.2
  20.6 0.0 copy-start.3
  20.6 60.6 %all_to_all.5.blocks_ref = bf16[32,128,512]{2,1,0:T(8,128)(2,1)} all-to-all(bf16[32,128,512]{2,1,0:T(8,128)(2,1)S(1)} %fusion), channel_id=1, replica_groups=mesh['dp'=32,'tensor'=4] {'dp'}, dimensions={0} | all-to-all | bytes 8388608 | tf_op jit(solution)/shard_map/all_to_all | solution.py:215
  81.2 0.0 copy-done.1
  81.3 0.0 copy-done.2
  81.3 0.0 copy-done.3
  81.3 23.3 %shard_map.86 = (bf16[128,4096]{1,0:T(8,128)(2,1)S(1)}, f32[128,512]{1,0:T(8,128)S(1)}, f32[128,512]{1,0:T(8,128)S(1)}) custom-call(bf16[32,128,512]{2,1,0:T(8,128)(2,1)} %all_to_all.5.blocks_ref, f32[128,512]{1,0:T(8,128)S(1)} %bitcast.30, f32[128,512]{1,0:T(8,128)S(1)} %bitcast.31, bf16[4096,512]{1,0:T(8,128)(2,1)} %proj_ref.3, bf16[128,4096]{1,0:T(8,128)(2,1)S(1)} %copy-done.1), custom_call_target="tpu_custom_call" | custom-call | tf_op jit(solution)/shard_map/pallas_call | solution.py:110
  104.5 1.0 copy.35
  105.5 0.7 copy.36
  106.2 0.7 copy.37
Async XLA Ops:
  0.6 1.2 %copy-start = (bf16[128,4096]{1,0:T(8,128)(2,1)S(1)}, bf16[128,4096]{1,0:T(8,128)(2,1)}, u32[]{:S(2)}) copy-start(bf16[128,4096]{1,0:T(8,128)(2,1)} %acts_ref.1) | copy-start | bytes 3145732
  1.9 13.9 %copy-start.4 = (bf16[512,4096]{1,0:T(8,128)(2,1)S(1)}, bf16[512,4096]{1,0:T(8,128)(2,1)}, u32[]{:S(2)}) copy-start(bf16[512,4096]{1,0:T(8,128)(2,1)} %param.7) | copy-start | bytes 12582916
  20.6 60.7 %copy-start.1 = (bf16[128,4096]{1,0:T(8,128)(2,1)S(1)}, bf16[128,4096]{1,0:T(8,128)(2,1)}, u32[]{:S(2)}) copy-start(bf16[128,4096]{1,0:T(8,128)(2,1)} %weight_ref.1) | copy-start | bytes 3145732
  20.6 60.6 %copy-start.2 = (f32[1,128,512]{2,1,0:T(8,128)S(1)}, f32[1,128,512]{2,1,0:T(8,128)}, u32[]{:S(2)}) copy-start(f32[1,128,512]{2,1,0:T(8,128)} %param.10) | copy-start | bytes 786436
  20.6 60.6 %copy-start.3 = (f32[1,128,512]{2,1,0:T(8,128)S(1)}, f32[1,128,512]{2,1,0:T(8,128)}, u32[]{:S(2)}) copy-start(f32[1,128,512]{2,1,0:T(8,128)} %param.11) | copy-start | bytes 786436

commit v11 on v8

--- a/solution.py
+++ b/solution.py
@@ -40,17 +40,22 @@
             barrier, inc=1, device_id=(lax.rem(me + k, n), col), device_id_type=MESH_ID
         )
 
-    total[...] = blocks_ref[0].astype(jnp.float32)
-
-    def add_block(k, carry):
-        total[...] += blocks_ref[k].astype(jnp.float32)
+    band = 16
+
+    def rows_step(r, carry):
+        rs = pl.ds(pl.multiple_of(r * band, band), band)
+        lowgrad = blocks_ref[0, rs, :].astype(jnp.float32)
+        for k in range(1, n):
+            lowgrad += blocks_ref[k, rs, :].astype(jnp.float32)
+        new_first, new_second, direction = adam_moments(
+            lowgrad, first_ref[rs, :], second_ref[rs, :]
+        )
+        new_first_ref[rs, :] = new_first
+        new_second_ref[rs, :] = new_second
+        direction_ref[rs, :] = direction
         return carry
 
-    lax.fori_loop(1, n, add_block, 0)
-    new_first, new_second, direction = adam_moments(total[...], first_ref[...], second_ref[...])
-    new_first_ref[...] = new_first
-    new_second_ref[...] = new_second
-    direction_ref[...] = direction
+    lax.fori_loop(0, blocks_ref.shape[1] // band, rows_step, 0)
 
     update[...] = (
         lax.dot_general(

time: 106 us -> 106 us (level)
  no operation moved by 1% of the time
where the time goes in v11:
time: 106 us; the launch traced here: 105 us
  blocking collectives  60.6 us (57%)
  Pallas kernels  35.3 us (33%)
  matrix products  4.79 us (5%)
  local copies, waits for them, and re-layouts  3.62 us (3%)
    all_to_all x1, blocking collectives, per_device(): lax.all_to_all(partial.astype(jnp.bfloat16), 'dp', split_axis=0, concat_a...  60.6 us
    pallas_call x1, Pallas kernels, tail(): pl.pallas_call(functools.partial(tail_kernel, n), out_shape=(jax.ShapeDty...  21.4 us
    pallas_call x1, Pallas kernels, chip_gather(): pl.pallas_call(chip_gather_kernel, out_shape=(jax.ShapeDtypeStruct((4,) +...  13.9 us
    unnamed x13, local copies, waits for them, and re-layouts  3.62 us
    dot_general x1, matrix products, per_device(): lax.dot_general(grad_blocks, proj_hi, dims, preferred_element_type=jnp.fl...  2.41 us
    dot_general x1, matrix products, per_device(): lax.dot_general(grad_blocks, proj_lo, dims, preferred_element_type=jnp.fl...  2.38 us

profile of v11, /device:TPU:0, one launch (start us, length us, event | category | flops | bytes accessed | tf_op | source)
XLA Modules:
  0.0 105.0 jit_solution(4543270952971340302)
XLA Ops:
  0.6 0.0 copy-start
  0.6 1.2 %copy-done = bf16[128,4096]{1,0:T(8,128)(2,1)S(1)} copy-done((bf16[128,4096]{1,0:T(8,128)(2,1)S(1)}, bf16[128,4096]{1,0:T(8,128)(2,1)}, u32[]{:S(2)}) %copy-start) | copy-done | bytes 1048600
  1.9 0.0 copy-start.4
  1.9 13.9 %shard_map.85 = (bf16[4,128,512]{2,1,0:T(8,128)(2,1)S(1)}, bf16[4,128,512]{2,1,0:T(8,128)(2,1)S(1)}) custom-call(bf16[128,4096]{1,0:T(8,128)(2,1)S(1)} %copy-done, bf16[4096,512]{1,0:T(8,128)(2,1)} %proj_ref.3), custom_call_target="tpu_custom_call" | custom-call | tf_op jit(solution)/shard_map/pallas_call | solution.py:176
  15.8 0.0 copy-done.4
  15.8 2.4 %fusion.1 = f32[512,32,128]{0,2,1:T(8,128)S(1)} fusion(bf16[512,512,1]{1,0,2:T(8,128)(2,1)S(1)} %bitcast.29, bf16[512,4096]{1,0:T(8,128)(2,1)S(1)} %copy-done.4), kind=kOutput, calls=%fused_computation.2 | convolution fusion | flops 2147483648 | bytes 13107200 | tf_op jit(solution)/shard_map/dot_general | solution.py:208
  18.2 2.4 %fusion = bf16[32,128,512]{2,1,0:T(8,128)(2,1)S(1)} fusion(f32[512,32,128]{0,2,1:T(8,128)S(1)} %fusion.1, bf16[512,512,1]{1,0,2:T(8,128)(2,1)S(1)} %bitcast.28, bf16[512,4096]{1,0:T(8,128)(2,1)S(1)} %copy-done.4), kind=kOutput, calls=%fused_computation.1 | convolution fusion | flops 2151677952 | bytes 17301504 | tf_op jit(solution)/shard_map/dot_general | solution.py:206
  20.6 0.0 copy-start.1
  20.6 0.0 copy-start.2
  20.6 0.0 copy-start.3
  20.6 60.6 %all_to_all.5.blocks_ref = bf16[32,128,512]{2,1,0:T(8,128)(2,1)} all-to-all(bf16[32,128,512]{2,1,0:T(8,128)(2,1)S(1)} %fusion), channel_id=1, replica_groups=mesh['dp'=32,'tensor'=4] {'dp'}, dimensions={0} | all-to-all | bytes 8388608 | tf_op jit(solution)/shard_map/all_to_all | solution.py:209
  81.2 0.0 copy-done.1
  81.3 0.0 copy-done.2
  81.3 0.0 copy-done.3
  81.3 21.4 %shard_map.86 = (bf16[128,4096]{1,0:T(8,128)(2,1)S(1)}, f32[128,512]{1,0:T(8,128)S(1)}, f32[128,512]{1,0:T(8,128)S(1)}) custom-call(bf16[32,128,512]{2,1,0:T(8,128)(2,1)} %all_to_all.5.blocks_ref, f32[128,512]{1,0:T(8,128)S(1)} %bitcast.30, f32[128,512]{1,0:T(8,128)S(1)} %bitcast.31, bf16[4096,512]{1,0:T(8,128)(2,1)} %proj_ref.3, bf16[128,4096]{1,0:T(8,128)(2,1)S(1)} %copy-done.1), custom_call_target="tpu_custom_call" | custom-call | tf_op jit(solution)/shard_map/pallas_call | solution.py:104
  102.6 1.0 copy.35
  103.6 0.7 copy.36
  104.3 0.7 copy.37
Async XLA Ops:
  0.6 1.2 %copy-start = (bf16[128,4096]{1,0:T(8,128)(2,1)S(1)}, bf16[128,4096]{1,0:T(8,128)(2,1)}, u32[]{:S(2)}) copy-start(bf16[128,4096]{1,0:T(8,128)(2,1)} %acts_ref.1) | copy-start | bytes 3145732
  1.9 13.9 %copy-start.4 = (bf16[512,4096]{1,0:T(8,128)(2,1)S(1)}, bf16[512,4096]{1,0:T(8,128)(2,1)}, u32[]{:S(2)}) copy-start(bf16[512,4096]{1,0:T(8,128)(2,1)} %param.7) | copy-start | bytes 12582916
  20.6 60.7 %copy-start.1 = (bf16[128,4096]{1,0:T(8,128)(2,1)S(1)}, bf16[128,4096]{1,0:T(8,128)(2,1)}, u32[]{:S(2)}) copy-start(bf16[128,4096]{1,0:T(8,128)(2,1)} %weight_ref.1) | copy-start | bytes 3145732
  20.6 60.6 %copy-start.2 = (f32[1,128,512]{2,1,0:T(8,128)S(1)}, f32[1,128,512]{2,1,0:T(8,128)}, u32[]{:S(2)}) copy-start(f32[1,128,512]{2,1,0:T(8,128)} %param.10) | copy-start | bytes 786436
  20.6 60.6 %copy-start.3 = (f32[1,128,512]{2,1,0:T(8,128)S(1)}, f32[1,128,512]{2,1,0:T(8,128)}, u32[]{:S(2)}) copy-start(f32[1,128,512]{2,1,0:T(8,128)} %param.11) | copy-start | bytes 786436

commit v12 on v11

--- a/solution.py
+++ b/solution.py
@@ -141,12 +141,15 @@
     local.wait()
     pl.semaphore_wait(barrier, 2)
 
-    def send(src, slot, peer):
+    half = send_buf.shape[0] // 2
+
+    def send(src, slot, peer, p):
+        span = pl.ds(p * half, half)
         copy = pltpu.make_async_remote_copy(
-            src_ref=src,
-            dst_ref=recv.at[slot],
-            send_sem=send_sem.at[slot],
-            recv_sem=recv_sem.at[slot],
+            src_ref=src.at[span],
+            dst_ref=recv.at[slot, span],
+            send_sem=send_sem.at[slot, p],
+            recv_sem=recv_sem.at[slot, p],
             device_id={"tensor": peer},
             device_id_type=MESH_ID,
         )
@@ -158,15 +161,19 @@
         hi_ref[slot] = hi
         lo_ref[slot] = (piece - hi.astype(jnp.float32)).astype(jnp.bfloat16)
 
-    across = send(send_buf, 1, chip_peer)
-    beside = send(send_buf, 0, core_peer)
+    across = [send(send_buf, 1, chip_peer, p) for p in range(2)]
+    beside = [send(send_buf, 0, core_peer, p) for p in range(2)]
     split(me, send_buf[...])
-    across.wait()
-    forward = send(recv.at[1], 2, core_peer)
+    forward = []
+    for p in range(2):
+        across[p].wait()
+        forward.append(send(recv.at[1], 2, core_peer, p))
     split(chip_peer, recv[1])
-    beside.wait()
+    for copy in beside:
+        copy.wait()
     split(core_peer, recv[0])
-    forward.wait()
+    for copy in forward:
+        copy.wait()
     split(3 - me, recv[2])
 
 
@@ -186,8 +193,8 @@
             pltpu.VMEM(shape, jnp.float32),
             pltpu.VMEM((3,) + shape, jnp.float32),
             pltpu.SemaphoreType.DMA(()),
-            pltpu.SemaphoreType.DMA((3,)),
-            pltpu.SemaphoreType.DMA((3,)),
+            pltpu.SemaphoreType.DMA((3, 2)),
+            pltpu.SemaphoreType.DMA((3, 2)),
         ],
         compiler_params=pltpu.CompilerParams(
             collective_id=1, has_side_effects=True, vmem_limit_bytes=48 * 1024 * 1024

time: 106 us -> 106 us (level)
  no operation moved by 1% of the time
where the time goes in v12:
time: 106 us; the launch traced here: 105 us
  blocking collectives  60.6 us (57%)
  Pallas kernels  35.2 us (33%)
  matrix products  4.8 us (5%)
  local copies, waits for them, and re-layouts  3.62 us (3%)
    all_to_all x1, blocking collectives, per_device(): lax.all_to_all(partial.astype(jnp.bfloat16), 'dp', split_axis=0, concat_a...  60.6 us
    pallas_call x1, Pallas kernels, tail(): pl.pallas_call(functools.partial(tail_kernel, n), out_shape=(jax.ShapeDty...  21.4 us
    pallas_call x1, Pallas kernels, chip_gather(): pl.pallas_call(chip_gather_kernel, out_shape=(jax.ShapeDtypeStruct((4,) +...  13.8 us
    unnamed x13, local copies, waits for them, and re-layouts  3.62 us
    dot_general x1, matrix products, per_device(): lax.dot_general(grad_blocks, proj_hi, dims, preferred_element_type=jnp.fl...  2.42 us
    dot_general x1, matrix products, per_device(): lax.dot_general(grad_blocks, proj_lo, dims, preferred_element_type=jnp.fl...  2.38 us

profile of v12, /device:TPU:0, one launch (start us, length us, event | category | flops | bytes accessed | tf_op | source)
XLA Modules:
  0.0 104.9 jit_solution(13110570011383578021)
XLA Ops:
  0.6 0.0 copy-start
  0.6 1.2 %copy-done = bf16[128,4096]{1,0:T(8,128)(2,1)S(1)} copy-done((bf16[128,4096]{1,0:T(8,128)(2,1)S(1)}, bf16[128,4096]{1,0:T(8,128)(2,1)}, u32[]{:S(2)}) %copy-start) | copy-done | bytes 1048600
  1.9 0.0 copy-start.4
  1.9 13.8 %shard_map.85 = (bf16[4,128,512]{2,1,0:T(8,128)(2,1)S(1)}, bf16[4,128,512]{2,1,0:T(8,128)(2,1)S(1)}) custom-call(bf16[128,4096]{1,0:T(8,128)(2,1)S(1)} %copy-done, bf16[4096,512]{1,0:T(8,128)(2,1)} %proj_ref.3), custom_call_target="tpu_custom_call" | custom-call | tf_op jit(solution)/shard_map/pallas_call | solution.py:183
  15.7 0.0 copy-done.4
  15.7 2.4 %fusion.1 = f32[512,32,128]{0,2,1:T(8,128)S(1)} fusion(bf16[512,512,1]{1,0,2:T(8,128)(2,1)S(1)} %bitcast.29, bf16[512,4096]{1,0:T(8,128)(2,1)S(1)} %copy-done.4), kind=kOutput, calls=%fused_computation.2 | convolution fusion | flops 2147483648 | bytes 13107200 | tf_op jit(solution)/shard_map/dot_general | solution.py:215
  18.1 2.4 %fusion = bf16[32,128,512]{2,1,0:T(8,128)(2,1)S(1)} fusion(f32[512,32,128]{0,2,1:T(8,128)S(1)} %fusion.1, bf16[512,512,1]{1,0,2:T(8,128)(2,1)S(1)} %bitcast.28, bf16[512,4096]{1,0:T(8,128)(2,1)S(1)} %copy-done.4), kind=kOutput, calls=%fused_computation.1 | convolution fusion | flops 2151677952 | bytes 17301504 | tf_op jit(solution)/shard_map/dot_general | solution.py:213
  20.5 0.0 copy-start.1
  20.5 0.0 copy-start.2
  20.5 0.0 copy-start.3
  20.5 60.6 %all_to_all.5.blocks_ref = bf16[32,128,512]{2,1,0:T(8,128)(2,1)} all-to-all(bf16[32,128,512]{2,1,0:T(8,128)(2,1)S(1)} %fusion), channel_id=1, replica_groups=mesh['dp'=32,'tensor'=4] {'dp'}, dimensions={0} | all-to-all | bytes 8388608 | tf_op jit(solution)/shard_map/all_to_all | solution.py:216
  81.1 0.0 copy-done.1
  81.1 0.0 copy-done.2
  81.1 0.0 copy-done.3
  81.1 21.4 %shard_map.86 = (bf16[128,4096]{1,0:T(8,128)(2,1)S(1)}, f32[128,512]{1,0:T(8,128)S(1)}, f32[128,512]{1,0:T(8,128)S(1)}) custom-call(bf16[32,128,512]{2,1,0:T(8,128)(2,1)} %all_to_all.5.blocks_ref, f32[128,512]{1,0:T(8,128)S(1)} %bitcast.30, f32[128,512]{1,0:T(8,128)S(1)} %bitcast.31, bf16[4096,512]{1,0:T(8,128)(2,1)} %proj_ref.3, bf16[128,4096]{1,0:T(8,128)(2,1)S(1)} %copy-done.1), custom_call_target="tpu_custom_call" | custom-call | tf_op jit(solution)/shard_map/pallas_call | solution.py:104
  102.5 1.0 copy.35
  103.5 0.7 copy.36
  104.2 0.7 copy.37
Async XLA Ops:
  0.6 1.2 %copy-start = (bf16[128,4096]{1,0:T(8,128)(2,1)S(1)}, bf16[128,4096]{1,0:T(8,128)(2,1)}, u32[]{:S(2)}) copy-start(bf16[128,4096]{1,0:T(8,128)(2,1)} %acts_ref.1) | copy-start | bytes 3145732
  1.9 13.8 %copy-start.4 = (bf16[512,4096]{1,0:T(8,128)(2,1)S(1)}, bf16[512,4096]{1,0:T(8,128)(2,1)}, u32[]{:S(2)}) copy-start(bf16[512,4096]{1,0:T(8,128)(2,1)} %param.7) | copy-start | bytes 12582916
  20.5 60.6 %copy-start.1 = (bf16[128,4096]{1,0:T(8,128)(2,1)S(1)}, bf16[128,4096]{1,0:T(8,128)(2,1)}, u32[]{:S(2)}) copy-start(bf16[128,4096]{1,0:T(8,128)(2,1)} %weight_ref.1) | copy-start | bytes 3145732
  20.5 60.6 %copy-start.2 = (f32[1,128,512]{2,1,0:T(8,128)S(1)}, f32[1,128,512]{2,1,0:T(8,128)}, u32[]{:S(2)}) copy-start(f32[1,128,512]{2,1,0:T(8,128)} %param.10) | copy-start | bytes 786436
  20.5 60.6 %copy-start.3 = (f32[1,128,512]{2,1,0:T(8,128)S(1)}, f32[1,128,512]{2,1,0:T(8,128)}, u32[]{:S(2)}) copy-start(f32[1,128,512]{2,1,0:T(8,128)} %param.11) | copy-start | bytes 786436

commit v13 on v9

--- a/solution.py
+++ b/solution.py
@@ -28,12 +28,12 @@
 def step_kernel(
     n, pieces, grad_ref, hi_ref, lo_ref, first_ref, second_ref, proj_ref, weight_ref,
     new_weight_ref, new_first_ref, new_second_ref,
-    part, part_out, blocks, total, direction_ref, update, sendbuf, recv,
+    part, part_out, blocks, total, hi_t, lo_t, direction_ref, update, sendbuf, recv,
     local_sem, part_send, part_recv, send_sem, recv_sem,
 ):
     me = lax.axis_index("dp")
     col = lax.axis_index("tensor")
-    owned = part.shape[1]
+    owned = part.shape[2]
     rows = sendbuf.shape[1]
     width = sendbuf.shape[2]
     barrier = pltpu.get_barrier_semaphore()
@@ -42,11 +42,13 @@
             barrier, inc=1, device_id=(lax.rem(me + k, n), col), device_id_type=MESH_ID
         )
 
+    hi_t[...] = hi_ref[...].T
+    lo_t[...] = lo_ref[...].T
+
     def partial_block(j, carry):
         grad = grad_ref[:, pl.ds(pl.multiple_of(j * owned, owned), owned)]
-        dims = (((0,), (0,)), ((), ()))
-        term = lax.dot_general(grad, hi_ref[...], dims, preferred_element_type=jnp.float32)
-        term += lax.dot_general(grad, lo_ref[...], dims, preferred_element_type=jnp.float32)
+        term = jnp.dot(hi_t[...], grad, preferred_element_type=jnp.float32)
+        term += jnp.dot(lo_t[...], grad, preferred_element_type=jnp.float32)
         part[j] = term.astype(jnp.bfloat16)
         return carry
 
@@ -55,7 +57,7 @@
     local.start()
     local.wait()
     pl.semaphore_wait(barrier, n - 1)
-    piece = owned // pieces
+    piece = part.shape[1] // pieces
 
     def part_copy(k, p):
         dest = lax.rem(me + k, n)
@@ -83,7 +85,7 @@
         return carry
 
     lax.fori_loop(1, n, add_block, 0)
-    new_first, new_second, direction = adam_moments(total[...], first_ref[...], second_ref[...])
+    new_first, new_second, direction = adam_moments(total[...].T, first_ref[...], second_ref[...])
     new_first_ref[...] = new_first
     new_second_ref[...] = new_second
     direction_ref[...] = direction
@@ -143,10 +145,12 @@
         in_specs=[vmem] * 7,
         out_specs=(vmem, vmem, vmem),
         scratch_shapes=[
-            pltpu.VMEM((n, hidden, rank), jnp.bfloat16),
-            pltpu.VMEM((n, hidden, rank), jnp.bfloat16),
-            pltpu.VMEM((n, hidden, rank), jnp.bfloat16),
-            pltpu.VMEM((hidden, rank), jnp.float32),
+            pltpu.VMEM((n, rank, hidden), jnp.bfloat16),
+            pltpu.VMEM((n, rank, hidden), jnp.bfloat16),
+            pltpu.VMEM((n, rank, hidden), jnp.bfloat16),
+            pltpu.VMEM((rank, hidden), jnp.float32),
+            pltpu.VMEM((rank, proj_hi.shape[0]), jnp.bfloat16),
+            pltpu.VMEM((rank, proj_hi.shape[0]), jnp.bfloat16),
             pltpu.VMEM((hidden, rank), jnp.bfloat16),
             pltpu.VMEM((n, rows, hidden), jnp.bfloat16),
             pltpu.VMEM((n, rows, hidden), jnp.bfloat16),

time: 118 us -> 121 us (1.025)
  Pallas kernels: 108 us -> 112 us
    pallas_call x1, Pallas kernels: 94.6 us -> 98 us  [step(): pl.pallas_call(functools.partial(step_kernel, n, pieces), out_shape=(jax....]
where the time goes in v13:
time: 121 us
  Pallas kernels  112 us (93%)
  local copies, waits for them, and re-layouts  8.44 us (7%)
    pallas_call x1, Pallas kernels, step(): pl.pallas_call(functools.partial(step_kernel, n, pieces), out_shape=(jax....  98 us
    pallas_call x1, Pallas kernels, chip_gather(): pl.pallas_call(chip_gather_kernel, out_shape=(jax.ShapeDtypeStruct((4,) +...  13.8 us
    unnamed x9, local copies, waits for them, and re-layouts  8.44 us

profile of v13, /device:TPU:0, one launch (start us, length us, event | category | flops | bytes accessed | tf_op | source)
XLA Modules:
  0.0 120.9 jit_solution(5756930302471312702)
XLA Ops:
  0.6 0.0 copy-start
  0.6 1.2 %copy-done = bf16[128,4096]{1,0:T(8,128)(2,1)S(1)} copy-done((bf16[128,4096]{1,0:T(8,128)(2,1)S(1)}, bf16[128,4096]{1,0:T(8,128)(2,1)}, u32[]{:S(2)}) %copy-start) | copy-done | bytes 1048600
  1.9 13.8 %shard_map.85 = (bf16[4,128,512]{2,1,0:T(8,128)(2,1)S(1)}, bf16[4,128,512]{2,1,0:T(8,128)(2,1)S(1)}) custom-call(bf16[128,4096]{1,0:T(8,128)(2,1)S(1)} %copy-done, bf16[4096,512]{1,0:T(8,128)(2,1)} %proj_ref.3), custom_call_target="tpu_custom_call" | custom-call | tf_op jit(solution)/shard_map/pallas_call | solution.py:217
  15.6 0.0 copy-start.1
  15.6 0.8 copy-done.1
  16.4 0.0 copy-start.2
  16.4 0.8 copy-done.2
  17.2 98.0 %shard_map.86 = (bf16[128,4096]{1,0:T(8,128)(2,1)}, f32[128,512]{1,0:T(8,128)}, f32[128,512]{1,0:T(8,128)}) custom-call(bf16[512,4096]{1,0:T(8,128)(2,1)} %grad_ref.1, bf16[512,512]{1,0:T(8,128)(2,1)} %bitcast.6, bf16[512,512]{1,0:T(8,128)(2,1)} %bitcast.7, f32[128,512]{1,0:T(8,128)} %bitcast.8, f32[128,512]{1,0:T(8,128)} %bitcast.9, ...), custom_call_target="tpu_custom_call" | custom-call | tf_op jit(solution)/shard_map/pallas_call | solution.py:138
  115.3 2.3 %copy.12 = bf16[128,4096]{1,0:T(8,128)(2,1)} copy(bf16[128,4096]{1,0:T(8,128)(2,1)} %get-tuple-element.16) | data formatting | bytes 2097152
  117.6 1.7 %copy.13 = f32[1,128,512]{2,1,0:T(8,128)} copy(f32[1,128,512]{2,1,0:T(8,128)} %bitcast.11) | data formatting | bytes 524288
  119.2 1.7 %copy.14 = f32[1,128,512]{2,1,0:T(8,128)} copy(f32[1,128,512]{2,1,0:T(8,128)} %bitcast.10) | data formatting | bytes 524288
Async XLA Ops:
  0.6 1.2 %copy-start = (bf16[128,4096]{1,0:T(8,128)(2,1)S(1)}, bf16[128,4096]{1,0:T(8,128)(2,1)}, u32[]{:S(2)}) copy-start(bf16[128,4096]{1,0:T(8,128)(2,1)} %acts_ref.1) | copy-start | bytes 3145732
  15.6 0.8 copy-start.1
  16.4 0.8 copy-start.2

commit v14 on v12

--- a/solution.py
+++ b/solution.py
@@ -25,8 +25,66 @@
     return (new_first, new_second, direction)
 
 
+def exchange_sum_kernel(n, pieces, part_ref, out_ref, recv, send_sem, recv_sem):
+    me = lax.axis_index("dp")
+    col = lax.axis_index("tensor")
+    barrier = pltpu.get_barrier_semaphore()
+    for k in range(1, n):
+        pl.semaphore_signal(
+            barrier, inc=1, device_id=(lax.rem(me + k, n), col), device_id_type=MESH_ID
+        )
+    pl.semaphore_wait(barrier, n - 1)
+    piece = part_ref.shape[1] // pieces
+
+    def part_copy(k, p):
+        dest = lax.rem(me + k, n)
+        span = pl.ds(pl.multiple_of(p * piece, piece), piece)
+        return pltpu.make_async_remote_copy(
+            src_ref=part_ref.at[dest, span],
+            dst_ref=recv.at[k, span],
+            send_sem=send_sem.at[p, k],
+            recv_sem=recv_sem.at[p, k],
+            device_id=(dest, col),
+            device_id_type=MESH_ID,
+        )
+
+    def start_part(i, carry):
+        part_copy(lax.rem(i, n - 1) + 1, i // (n - 1)).start()
+        return carry
+
+    lax.fori_loop(0, (n - 1) * pieces, start_part, 0)
+    out_ref[...] = part_ref[me].astype(jnp.float32)
+
+    def add_block(k, carry):
+        for p in range(pieces):
+            part_copy(k, p).wait()
+        out_ref[...] += recv[k].astype(jnp.float32)
+        return carry
+
+    lax.fori_loop(1, n, add_block, 0)
+
+
+def exchange_sum(part):
+    n, rows, cols = part.shape
+    pieces = 8
+    return pl.pallas_call(
+        functools.partial(exchange_sum_kernel, n, pieces),
+        out_shape=jax.ShapeDtypeStruct((rows, cols), jnp.float32),
+        in_specs=[pl.BlockSpec(memory_space=pltpu.VMEM)],
+        out_specs=pl.BlockSpec(memory_space=pltpu.VMEM),
+        scratch_shapes=[
+            pltpu.VMEM((n, rows, cols), part.dtype),
+            pltpu.SemaphoreType.DMA((pieces, n)),
+            pltpu.SemaphoreType.DMA((pieces, n)),
+        ],
+        compiler_params=pltpu.CompilerParams(
+            collective_id=0, has_side_effects=True, vmem_limit_bytes=48 * 1024 * 1024
+        ),
+    )(part)
+
+
 def tail_kernel(
-    n, blocks_ref, first_ref, second_ref, proj_ref, weight_ref,
+    n, blocks_ref, rest_ref, first_ref, second_ref, proj_ref, weight_ref,
     new_weight_ref, new_first_ref, new_second_ref,
     total, direction_ref, update, sendbuf, recv, local_sem, send_sem, recv_sem,
 ):
@@ -47,6 +105,7 @@
         lowgrad = blocks_ref[0, rs, :].astype(jnp.float32)
         for k in range(1, n):
             lowgrad += blocks_ref[k, rs, :].astype(jnp.float32)
+        lowgrad = jnp.concatenate([lowgrad, rest_ref[rs, :]], axis=1)
         new_first, new_second, direction = adam_moments(
             lowgrad, first_ref[rs, :], second_ref[rs, :]
         )
@@ -97,8 +156,9 @@
         apply(lax.rem(me + n - k, n), recv[k])
 
 
-def tail(blocks, first_moment, second_moment, projector, weight):
+def tail(blocks, rest, first_moment, second_moment, projector, weight):
     n, hidden, rank = blocks.shape
+    rank = rank + rest.shape[1]
     rows = weight.shape[0]
     vmem = pl.BlockSpec(memory_space=pltpu.VMEM)
     return pl.pallas_call(
@@ -108,7 +168,7 @@
             jax.ShapeDtypeStruct((hidden, rank), jnp.float32),
             jax.ShapeDtypeStruct((hidden, rank), jnp.float32),
         ),
-        in_specs=[vmem] * 5,
+        in_specs=[vmem] * 6,
         out_specs=(vmem, vmem, vmem),
         scratch_shapes=[
             pltpu.VMEM((hidden, rank), jnp.float32),
@@ -123,7 +183,7 @@
         compiler_params=pltpu.CompilerParams(
             collective_id=2, has_side_effects=True, vmem_limit_bytes=48 * 1024 * 1024
         ),
-    )(blocks, first_moment, second_moment, projector, weight)
+    )(blocks, rest, first_moment, second_moment, projector, weight)
 
 
 def chip_gather_kernel(
@@ -210,14 +270,20 @@
     owners = lax.axis_size("dp")
     grad_blocks = out_grad.reshape(out_grad.shape[0], owners, -1)
     dims = (((0,), (0,)), ((), ()))
-    partial = lax.dot_general(
-        grad_blocks, proj_hi, dims, preferred_element_type=jnp.float32
-    ) + lax.dot_general(grad_blocks, proj_lo, dims, preferred_element_type=jnp.float32)
+    half = proj_hi.shape[1] // 2
+
+    def partial_of(cols):
+        return (
+            lax.dot_general(grad_blocks, proj_hi[:, cols], dims, preferred_element_type=jnp.float32)
+            + lax.dot_general(grad_blocks, proj_lo[:, cols], dims, preferred_element_type=jnp.float32)
+        ).astype(jnp.bfloat16)
+
     blocks = lax.all_to_all(
-        partial.astype(jnp.bfloat16), "dp", split_axis=0, concat_axis=0, tiled=True
+        partial_of(slice(0, half)), "dp", split_axis=0, concat_axis=0, tiled=True
     )
+    rest = exchange_sum(partial_of(slice(half, None)))
     new_weight, new_first, new_second = tail(
-        blocks, first_moment[0], second_moment[0], projector, weight
+        blocks, rest, first_moment[0], second_moment[0], projector, weight
     )
     return (new_weight, new_first[None], new_second[None])
 

time: 106 us -> 113 us (1.066)
  blocking collectives: 60.6 us -> 0 us
  Pallas kernels: 35.2 us -> 86.8 us
  starting transfers between devices: 0 us -> 8.68 us
  matrix products: 4.8 us -> 10.7 us
    all_to_all x1 -> x0, blocking collectives: 60.6 us -> none  [per_device(): lax.all_to_all(partial.astype(jnp.bfloat16), 'dp', split_axis=0, concat_a...]
    pallas_call x0 -> x1, Pallas kernels: none -> 52 us  [exchange_sum(): pl.pallas_call(functools.partial(exchange_sum_kernel, n, pieces), out_sha...]
    all_to_all x0 -> x1, starting transfers between devices: none -> 8.68 us  [per_device(): lax.all_to_all(partial_of(slice(0, half)), 'dp', split_axis=0, concat_axi...]
    dot_general x2 -> x4, matrix products: 4.8 us -> 10.7 us  [the longest x2 5.82 us: partial_of(): lax.dot_general(grad_blocks, proj_lo[:, cols], dims, preferred_element_ty...]
    unnamed x13 -> x19, local copies, waits for them, and re-layouts: 3.62 us -> 4.58 us
  transfers between devices with their start and end apart: 0 -> 1, of which waited for: 0 -> 0; matrix products, arithmetic and copies ran while one was open for 0% -> 5% of each run, Pallas kernels for 0% -> 47%
where the time goes in v14:
time: 113 us; the launch traced here: 112 us
  Pallas kernels  86.8 us (77%)
  matrix products  10.7 us (9%)
  starting transfers between devices  8.68 us (8%)
  local copies, waits for them, and re-layouts  4.58 us (4%)
    pallas_call x1, Pallas kernels, exchange_sum(): pl.pallas_call(functools.partial(exchange_sum_kernel, n, pieces), out_sha...  52 us
    pallas_call x1, Pallas kernels, tail(): pl.pallas_call(functools.partial(tail_kernel, n), out_shape=(jax.ShapeDty...  21 us
    pallas_call x1, Pallas kernels, chip_gather(): pl.pallas_call(chip_gather_kernel, out_shape=(jax.ShapeDtypeStruct((4,) +...  13.8 us
    all_to_all x1, starting transfers between devices, per_device(): lax.all_to_all(partial_of(slice(0, half)), 'dp', split_axis=0, concat_axi...  8.68 us
    dot_general x2, matrix products, partial_of(): lax.dot_general(grad_blocks, proj_lo[:, cols], dims, preferred_element_ty...  5.82 us
    dot_general x2, matrix products, partial_of(): lax.dot_general(grad_blocks, proj_hi[:, cols], dims, preferred_element_ty...  4.85 us
    unnamed x19, local copies, waits for them, and re-layouts  4.58 us
  transfers between devices with their start and end apart: 1, of which 0 were waited for; matrix products, arithmetic and copies ran while one was open for 5% of the time, Pallas kernels for 47%

profile of v14, /device:TPU:0, one launch (start us, length us, event | category | flops | bytes accessed | tf_op | source)
XLA Modules:
  0.0 111.5 jit_solution(411962387060560029)
XLA Ops:
  0.6 0.0 copy-start
  0.6 1.2 %copy-done = bf16[128,4096]{1,0:T(8,128)(2,1)S(1)} copy-done((bf16[128,4096]{1,0:T(8,128)(2,1)S(1)}, bf16[128,4096]{1,0:T(8,128)(2,1)}, u32[]{:S(2)}) %copy-start) | copy-done | bytes 1048600
  1.9 13.8 %shard_map.85 = (bf16[4,128,512]{2,1,0:T(8,128)(2,1)S(1)}, bf16[4,128,512]{2,1,0:T(8,128)(2,1)S(1)}) custom-call(bf16[128,4096]{1,0:T(8,128)(2,1)S(1)} %copy-done, bf16[4096,512]{1,0:T(8,128)(2,1)} %proj_ref.3), custom_call_target="tpu_custom_call" | custom-call | tf_op jit(solution)/shard_map/pallas_call | solution.py:243
  15.7 0.0 copy-start.2
  15.7 0.0 copy-done.6
  15.7 1.7 %fusion.4 = f32[256,32,128]{0,2,1:T(8,128)S(1)} fusion(bf16[512,512]{1,0:T(8,128)(2,1)S(1)} %bitcast.52, bf16[512,4096]{1,0:T(8,128)(2,1)S(1)} %copy-done.6), kind=kOutput, calls=%fused_computation.4 | convolution fusion | flops 1073741824 | bytes 8650752 | tf_op jit(solution)/shard_map/dot_general | solution.py:278
  17.4 0.0 copy-done.2
  17.4 3.1 %fusion.12 = bf16[32,128,256]{2,1,0:T(8,128)(2,1)} fusion(f32[256,32,128]{0,2,1:T(8,128)S(1)} %fusion.4, bf16[512,512]{1,0:T(8,128)(2,1)S(1)} %bitcast.54, bf16[512,4096]{1,0:T(8,128)(2,1)S(1)} %copy-done.6), kind=kOutput, calls=%fused_computation.14 | convolution fusion | flops 1075838976 | bytes 10747904 | tf_op jit(solution)/shard_map/dot_general | solution.py:277
  20.5 8.7 %all-to-all-start = ((bf16[32,128,256]{2,1,0:T(8,128)(2,1)}), bf16[32,128,256]{2,1,0:T(8,128)(2,1)S(1)}, u32[]{:S(2)}, u32[]{:S(2)}) async-start(bf16[32,128,256]{2,1,0:T(8,128)(2,1)} %fusion.12), calls=%async_computation | async-start | bytes 4194304 | tf_op jit(solution)/shard_map/all_to_all | solution.py:281
  29.2 0.0 copy-start.3
  29.2 0.0 copy-start.7
  29.3 4.1 %fusion = f32[256,32,128]{0,2,1:T(8,128)S(1)} fusion(bf16[512,512]{1,0:T(8,128)(2,1)S(1)} %bitcast.53, bf16[512,4096]{1,0:T(8,128)(2,1)} %param.7), kind=kOutput, calls=%fused_computation | convolution fusion | flops 1073741824 | bytes 8650752 | tf_op jit(solution)/shard_map/dot_general | solution.py:278
  33.3 0.0 copy-done.3
  33.4 0.0 copy-start.1
  33.4 0.0 copy-start.4
  33.4 1.8 %fusion.13.part_ref = bf16[32,128,256]{2,1,0:T(8,128)(2,1)S(1)} fusion(f32[256,32,128]{0,2,1:T(8,128)S(1)} %fusion, bf16[512,512]{1,0:T(8,128)(2,1)S(1)} %bitcast.55, bf16[512,4096]{1,0:T(8,128)(2,1)S(1)} %copy-done.7), kind=kOutput, calls=%fused_computation.15 | convolution fusion | flops 1075838976 | bytes 10747904 | tf_op jit(solution)/shard_map/dot_general | solution.py:277
  35.1 52.0 %shard_map.86.rest_ref = f32[128,256]{1,0:T(8,128)S(1)} custom-call(bf16[32,128,256]{2,1,0:T(8,128)(2,1)S(1)} %fusion.13.part_ref), custom_call_target="tpu_custom_call" | custom-call | tf_op jit(solution)/shard_map/pallas_call | solution.py:70
  87.1 0.0 all-to-all-done.blocks_ref
  87.2 0.0 copy-start.5
  87.2 0.9 copy-done.5
  88.1 21.0 %shard_map.87 = (bf16[128,4096]{1,0:T(8,128)(2,1)S(1)}, f32[128,512]{1,0:T(8,128)S(1)}, f32[128,512]{1,0:T(8,128)S(1)}) custom-call(bf16[32,128,256]{2,1,0:T(8,128)(2,1)S(1)} %all-to-all-done.blocks_ref, f32[128,256]{1,0:T(8,128)S(1)} %shard_map.86.rest_ref, f32[128,512]{1,0:T(8,128)S(1)} %bitcast.56, f32[128,512]{1,0:T(8,128)S(1)} %bitcast.57, ...), custom_call_target="tpu_custom_call" | custom-call | tf_op jit(solution)/shard_map/pallas_call | solution.py:164
  109.2 1.0 copy.53
  110.1 0.7 copy.54
  110.8 0.7 copy.55
  (4 shorter events, 0.0 us)
Async XLA Ops:
  0.6 1.2 %copy-start = (bf16[128,4096]{1,0:T(8,128)(2,1)S(1)}, bf16[128,4096]{1,0:T(8,128)(2,1)}, u32[]{:S(2)}) copy-start(bf16[128,4096]{1,0:T(8,128)(2,1)} %acts_ref.1) | copy-start | bytes 3145732
  1.9 13.8 %copy-start.6 = (bf16[512,4096]{1,0:T(8,128)(2,1)S(1)}, bf16[512,4096]{1,0:T(8,128)(2,1)}, u32[]{:S(2)}) copy-start(bf16[512,4096]{1,0:T(8,128)(2,1)} %param.7) | copy-start | bytes 12582916
  15.7 1.8 %copy-start.2 = (bf16[4,128,512]{2,1,0:T(8,128)(2,1)}, bf16[4,128,512]{2,1,0:T(8,128)(2,1)S(1)}, u32[]{:S(2)}) copy-start(bf16[4,128,512]{2,1,0:T(8,128)(2,1)S(1)} %get-tuple-element.8) | copy-start | bytes 1572868
  20.5 66.6 %all-to-all-start = ((bf16[32,128,256]{2,1,0:T(8,128)(2,1)}), bf16[32,128,256]{2,1,0:T(8,128)(2,1)S(1)}, u32[]{:S(2)}, u32[]{:S(2)}) async-start(bf16[32,128,256]{2,1,0:T(8,128)(2,1)} %fusion.12), calls=%async_computation | async-start | bytes 4194304 | tf_op jit(solution)/shard_map/all_to_all | solution.py:281
  29.2 4.1 %copy-start.3 = (bf16[4,128,512]{2,1,0:T(8,128)(2,1)S(1)}, bf16[4,128,512]{2,1,0:T(8,128)(2,1)}, u32[]{:S(2)}) copy-start(bf16[4,128,512]{2,1,0:T(8,128)(2,1)} %copy-done.2) | copy-start | bytes 1572868
  29.2 4.1 %copy-start.7 = (bf16[512,4096]{1,0:T(8,128)(2,1)S(1)}, bf16[512,4096]{1,0:T(8,128)(2,1)}, u32[]{:S(2)}) copy-start(bf16[512,4096]{1,0:T(8,128)(2,1)} %param.7) | copy-start | bytes 12582916
  33.4 53.8 %copy-start.1 = (bf16[128,4096]{1,0:T(8,128)(2,1)S(1)}, bf16[128,4096]{1,0:T(8,128)(2,1)}, u32[]{:S(2)}) copy-start(bf16[128,4096]{1,0:T(8,128)(2,1)} %weight_ref.1) | copy-start | bytes 3145732
  33.4 53.8 %copy-start.4 = (f32[1,128,512]{2,1,0:T(8,128)S(1)}, f32[1,128,512]{2,1,0:T(8,128)}, u32[]{:S(2)}) copy-start(f32[1,128,512]{2,1,0:T(8,128)} %param.10) | copy-start | bytes 786436
  87.2 1.0 copy-start.5

commit v15 on v12

--- a/solution.py
+++ b/solution.py
@@ -127,7 +127,7 @@
 
 
 def chip_gather_kernel(
-    acts_ref, proj_ref, hi_ref, lo_ref, q_buf, send_buf, recv, local_sem, send_sem, recv_sem
+    acts_ref, proj_ref, hi_ref, q_buf, send_buf, recv, local_sem, send_sem, recv_sem
 ):
     me = lax.axis_index("tensor")
     core_peer = me + 1 - 2 * lax.rem(me, 2)
@@ -157,9 +157,7 @@
         return copy
 
     def split(slot, piece):
-        hi = piece.astype(jnp.bfloat16)
-        hi_ref[slot] = hi
-        lo_ref[slot] = (piece - hi.astype(jnp.float32)).astype(jnp.bfloat16)
+        hi_ref[slot] = piece.astype(jnp.bfloat16)
 
     across = [send(send_buf, 1, chip_peer, p) for p in range(2)]
     beside = [send(send_buf, 0, core_peer, p) for p in range(2)]
@@ -182,12 +180,9 @@
     vmem = pl.BlockSpec(memory_space=pltpu.VMEM)
     return pl.pallas_call(
         chip_gather_kernel,
-        out_shape=(
-            jax.ShapeDtypeStruct((4,) + shape, jnp.bfloat16),
-            jax.ShapeDtypeStruct((4,) + shape, jnp.bfloat16),
-        ),
+        out_shape=jax.ShapeDtypeStruct((4,) + shape, jnp.bfloat16),
         in_specs=[vmem, vmem],
-        out_specs=(vmem, vmem),
+        out_specs=vmem,
         scratch_shapes=[
             pltpu.VMEM(shape, jnp.float32),
             pltpu.VMEM(shape, jnp.float32),
@@ -204,15 +199,12 @@
 
 def per_device(acts, out_grad, projector, weight, first_moment, second_moment):
     assert lax.axis_size("tensor") == 4
-    proj_hi, proj_lo = chip_gather(acts, projector)
+    proj_hi = chip_gather(acts, projector)
     proj_hi = proj_hi.reshape(-1, proj_hi.shape[2])
-    proj_lo = proj_lo.reshape(-1, proj_lo.shape[2])
     owners = lax.axis_size("dp")
     grad_blocks = out_grad.reshape(out_grad.shape[0], owners, -1)
     dims = (((0,), (0,)), ((), ()))
-    partial = lax.dot_general(
-        grad_blocks, proj_hi, dims, preferred_element_type=jnp.float32
-    ) + lax.dot_general(grad_blocks, proj_lo, dims, preferred_element_type=jnp.float32)
+    partial = lax.dot_general(grad_blocks, proj_hi, dims, preferred_element_type=jnp.float32)
     blocks = lax.all_to_all(
         partial.astype(jnp.bfloat16), "dp", split_axis=0, concat_axis=0, tiled=True
     )

time: 106 us -> 103 us (0.972)
  matrix products: 4.8 us -> 2.38 us
  Pallas kernels: 35.2 us -> 32.8 us
  local copies, waits for them, and re-layouts: 3.62 us -> 5.81 us
    dot_general x1 -> x0, matrix products: 2.38 us -> none  [per_device(): lax.dot_general(grad_blocks, proj_lo, dims, preferred_element_type=jnp.fl...]
    pallas_call x1, Pallas kernels: 13.8 us -> 11.4 us  [chip_gather(): pl.pallas_call(chip_gather_kernel, out_shape=jax.ShapeDtypeStruct((4,) +...]
    unnamed x13 -> x15, local copies, waits for them, and re-layouts: 3.62 us -> 5.81 us
where the time goes in v15:
time: 103 us; the launch traced here: 102 us
  blocking collectives  60.6 us (59%)
  Pallas kernels  32.8 us (32%)
  local copies, waits for them, and re-layouts  5.81 us (6%)
  matrix products  2.38 us (2%)
    all_to_all x1, blocking collectives, per_device(): lax.all_to_all(partial.astype(jnp.bfloat16), 'dp', split_axis=0, concat_a...  60.6 us
    pallas_call x1, Pallas kernels, tail(): pl.pallas_call(functools.partial(tail_kernel, n), out_shape=(jax.ShapeDty...  21.4 us
    pallas_call x1, Pallas kernels, chip_gather(): pl.pallas_call(chip_gather_kernel, out_shape=jax.ShapeDtypeStruct((4,) +...  11.4 us
    unnamed x15, local copies, waits for them, and re-layouts  5.81 us
    dot_general x1, matrix products, per_device(): lax.dot_general(grad_blocks, proj_hi, dims, preferred_element_type=jnp.fl...  2.38 us

profile of v15, /device:TPU:0, one launch (start us, length us, event | category | flops | bytes accessed | tf_op | source)
XLA Modules:
  0.0 102.3 jit_solution(3380179485134470732)
XLA Ops:
  0.6 0.0 copy-start
  0.6 2.2 %copy-done = bf16[4096,512]{1,0:T(8,128)(2,1)S(1)} copy-done((bf16[4096,512]{1,0:T(8,128)(2,1)S(1)}, bf16[4096,512]{1,0:T(8,128)(2,1)}, u32[]{:S(2)}) %copy-start) | copy-done | bytes 4194328
  2.8 0.0 copy-start.2
  2.8 1.2 %copy-done.2 = bf16[128,4096]{1,0:T(8,128)(2,1)S(1)} copy-done((bf16[128,4096]{1,0:T(8,128)(2,1)S(1)}, bf16[128,4096]{1,0:T(8,128)(2,1)}, u32[]{:S(2)}) %copy-start.2) | copy-done | bytes 1048600
  4.0 0.0 copy-start.5
  4.0 11.4 %shard_map.85 = bf16[4,128,512]{2,1,0:T(8,128)(2,1)S(1)} custom-call(bf16[128,4096]{1,0:T(8,128)(2,1)S(1)} %copy-done.2, bf16[4096,512]{1,0:T(8,128)(2,1)S(1)} %copy-done), custom_call_target="tpu_custom_call" | custom-call | tf_op jit(solution)/shard_map/pallas_call | solution.py:181
  15.5 0.0 copy-done.5
  15.5 2.4 %convert_bitcast_fusion = bf16[32,128,512]{2,1,0:T(8,128)(2,1)S(1)} fusion(bf16[512,512,1]{1,0,2:T(8,128)(2,1)S(1)} %bitcast.19, bf16[512,4096]{1,0:T(8,128)(2,1)S(1)} %copy-done.5), kind=kOutput, calls=%fused_computation.3 | convolution fusion | flops 2149580800 | bytes 8912896 | tf_op jit(solution)/shard_map/dot_general | solution.py:207
  17.9 0.0 copy-start.1
  17.9 0.0 copy-start.3
  17.9 0.0 copy-start.4
  17.9 60.6 %all_to_all.5.blocks_ref = bf16[32,128,512]{2,1,0:T(8,128)(2,1)} all-to-all(bf16[32,128,512]{2,1,0:T(8,128)(2,1)S(1)} %convert_bitcast_fusion), channel_id=1, replica_groups=mesh['dp'=32,'tensor'=4] {'dp'}, dimensions={0} | all-to-all | bytes 8388608 | tf_op jit(solution)/shard_map/all_to_all | solution.py:208
  78.5 0.0 copy-done.1
  78.5 0.0 copy-done.3
  78.5 0.0 copy-done.4
  78.5 21.4 %shard_map.86 = (bf16[128,4096]{1,0:T(8,128)(2,1)S(1)}, f32[128,512]{1,0:T(8,128)S(1)}, f32[128,512]{1,0:T(8,128)S(1)}) custom-call(bf16[32,128,512]{2,1,0:T(8,128)(2,1)} %all_to_all.5.blocks_ref, f32[128,512]{1,0:T(8,128)S(1)} %bitcast.20, f32[128,512]{1,0:T(8,128)S(1)} %bitcast.21, bf16[4096,512]{1,0:T(8,128)(2,1)} %proj_ref.3, bf16[128,4096]{1,0:T(8,128)(2,1)S(1)} %copy-done.1), custom_call_target="tpu_custom_call" | custom-call | tf_op jit(solution)/shard_map/pallas_call | solution.py:104
  99.9 1.0 copy.25
  100.9 0.7 copy.26
  101.6 0.7 copy.27
Async XLA Ops:
  0.6 2.2 %copy-start = (bf16[4096,512]{1,0:T(8,128)(2,1)S(1)}, bf16[4096,512]{1,0:T(8,128)(2,1)}, u32[]{:S(2)}) copy-start(bf16[4096,512]{1,0:T(8,128)(2,1)} %proj_ref.3) | copy-start | bytes 12582916
  2.8 1.2 %copy-start.2 = (bf16[128,4096]{1,0:T(8,128)(2,1)S(1)}, bf16[128,4096]{1,0:T(8,128)(2,1)}, u32[]{:S(2)}) copy-start(bf16[128,4096]{1,0:T(8,128)(2,1)} %acts_ref.1) | copy-start | bytes 3145732
  4.0 11.5 %copy-start.5 = (bf16[512,4096]{1,0:T(8,128)(2,1)S(1)}, bf16[512,4096]{1,0:T(8,128)(2,1)}, u32[]{:S(2)}) copy-start(bf16[512,4096]{1,0:T(8,128)(2,1)} %param.7) | copy-start | bytes 12582916
  17.9 60.6 %copy-start.1 = (bf16[128,4096]{1,0:T(8,128)(2,1)S(1)}, bf16[128,4096]{1,0:T(8,128)(2,1)}, u32[]{:S(2)}) copy-start(bf16[128,4096]{1,0:T(8,128)(2,1)} %weight_ref.1) | copy-start | bytes 3145732
  17.9 60.6 %copy-start.3 = (f32[1,128,512]{2,1,0:T(8,128)S(1)}, f32[1,128,512]{2,1,0:T(8,128)}, u32[]{:S(2)}) copy-start(f32[1,128,512]{2,1,0:T(8,128)} %param.10) | copy-start | bytes 786436
  17.9 60.6 %copy-start.4 = (f32[1,128,512]{2,1,0:T(8,128)S(1)}, f32[1,128,512]{2,1,0:T(8,128)}, u32[]{:S(2)}) copy-start(f32[1,128,512]{2,1,0:T(8,128)} %param.11) | copy-start | bytes 786436

commit v16 on v15

--- a/solution.py
+++ b/solution.py
@@ -135,7 +135,9 @@
     barrier = pltpu.get_barrier_semaphore()
     for peer in (core_peer, chip_peer):
         pl.semaphore_signal(barrier, inc=1, device_id={"tensor": peer}, device_id_type=MESH_ID)
-    q_buf[...] = jnp.dot(acts_ref[...], proj_ref[...], preferred_element_type=jnp.float32)
+    q_buf[...] = jnp.dot(acts_ref[...], proj_ref[...], preferred_element_type=jnp.float32).astype(
+        jnp.bfloat16
+    )
     local = pltpu.make_async_copy(q_buf, send_buf, local_sem)
     local.start()
     local.wait()
@@ -157,7 +159,7 @@
         return copy
 
     def split(slot, piece):
-        hi_ref[slot] = piece.astype(jnp.bfloat16)
+        hi_ref[slot] = piece
 
     across = [send(send_buf, 1, chip_peer, p) for p in range(2)]
     beside = [send(send_buf, 0, core_peer, p) for p in range(2)]
@@ -184,9 +186,9 @@
         in_specs=[vmem, vmem],
         out_specs=vmem,
         scratch_shapes=[
-            pltpu.VMEM(shape, jnp.float32),
-            pltpu.VMEM(shape, jnp.float32),
-            pltpu.VMEM((3,) + shape, jnp.float32),
+            pltpu.VMEM(shape, jnp.bfloat16),
+            pltpu.VMEM(shape, jnp.bfloat16),
+            pltpu.VMEM((3,) + shape, jnp.bfloat16),
             pltpu.SemaphoreType.DMA(()),
             pltpu.SemaphoreType.DMA((3, 2)),
             pltpu.SemaphoreType.DMA((3, 2)),

time: 103 us -> 101 us (0.981)
  Pallas kernels: 32.8 us -> 30.1 us
    pallas_call x1, Pallas kernels: 11.4 us -> 8.69 us  [chip_gather(): pl.pallas_call(chip_gather_kernel, out_shape=jax.ShapeDtypeStruct((4,) +...]
where the time goes in v16:
time: 101 us; the launch traced here: 99.4 us
  blocking collectives  60.4 us (60%)
  Pallas kernels  30.1 us (30%)
  local copies, waits for them, and re-layouts  5.81 us (6%)
  matrix products  2.38 us (2%)
    all_to_all x1, blocking collectives, per_device(): lax.all_to_all(partial.astype(jnp.bfloat16), 'dp', split_axis=0, concat_a...  60.4 us
    pallas_call x1, Pallas kernels, tail(): pl.pallas_call(functools.partial(tail_kernel, n), out_shape=(jax.ShapeDty...  21.4 us
    pallas_call x1, Pallas kernels, chip_gather(): pl.pallas_call(chip_gather_kernel, out_shape=jax.ShapeDtypeStruct((4,) +...  8.69 us
    unnamed x15, local copies, waits for them, and re-layouts  5.81 us
    dot_general x1, matrix products, per_device(): lax.dot_general(grad_blocks, proj_hi, dims, preferred_element_type=jnp.fl...  2.38 us

profile of v16, /device:TPU:0, one launch (start us, length us, event | category | flops | bytes accessed | tf_op | source)
XLA Modules:
  0.0 99.4 jit_solution(17330560168118468092)
XLA Ops:
  0.6 0.0 copy-start
  0.6 2.2 %copy-done = bf16[4096,512]{1,0:T(8,128)(2,1)S(1)} copy-done((bf16[4096,512]{1,0:T(8,128)(2,1)S(1)}, bf16[4096,512]{1,0:T(8,128)(2,1)}, u32[]{:S(2)}) %copy-start) | copy-done | bytes 4194328
  2.8 0.0 copy-start.2
  2.8 1.2 %copy-done.2 = bf16[128,4096]{1,0:T(8,128)(2,1)S(1)} copy-done((bf16[128,4096]{1,0:T(8,128)(2,1)S(1)}, bf16[128,4096]{1,0:T(8,128)(2,1)}, u32[]{:S(2)}) %copy-start.2) | copy-done | bytes 1048600
  4.0 0.0 copy-start.5
  4.0 8.7 %shard_map.85 = bf16[4,128,512]{2,1,0:T(8,128)(2,1)S(1)} custom-call(bf16[128,4096]{1,0:T(8,128)(2,1)S(1)} %copy-done.2, bf16[4096,512]{1,0:T(8,128)(2,1)S(1)} %copy-done), custom_call_target="tpu_custom_call" | custom-call | tf_op jit(solution)/shard_map/pallas_call | solution.py:183
  12.7 0.0 copy-done.5
  12.8 2.4 %convert_bitcast_fusion = bf16[32,128,512]{2,1,0:T(8,128)(2,1)S(1)} fusion(bf16[512,512,1]{1,0,2:T(8,128)(2,1)S(1)} %bitcast.19, bf16[512,4096]{1,0:T(8,128)(2,1)S(1)} %copy-done.5), kind=kOutput, calls=%fused_computation.3 | convolution fusion | flops 2149580800 | bytes 8912896 | tf_op jit(solution)/shard_map/dot_general | solution.py:209
  15.1 0.0 copy-start.1
  15.2 0.0 copy-start.3
  15.2 0.0 copy-start.4
  15.2 60.4 %all_to_all.5.blocks_ref = bf16[32,128,512]{2,1,0:T(8,128)(2,1)} all-to-all(bf16[32,128,512]{2,1,0:T(8,128)(2,1)S(1)} %convert_bitcast_fusion), channel_id=1, replica_groups=mesh['dp'=32,'tensor'=4] {'dp'}, dimensions={0} | all-to-all | bytes 8388608 | tf_op jit(solution)/shard_map/all_to_all | solution.py:210
  75.6 0.0 copy-done.1
  75.6 0.0 copy-done.3
  75.6 0.0 copy-done.4
  75.6 21.4 %shard_map.86 = (bf16[128,4096]{1,0:T(8,128)(2,1)S(1)}, f32[128,512]{1,0:T(8,128)S(1)}, f32[128,512]{1,0:T(8,128)S(1)}) custom-call(bf16[32,128,512]{2,1,0:T(8,128)(2,1)} %all_to_all.5.blocks_ref, f32[128,512]{1,0:T(8,128)S(1)} %bitcast.20, f32[128,512]{1,0:T(8,128)S(1)} %bitcast.21, bf16[4096,512]{1,0:T(8,128)(2,1)} %proj_ref.3, bf16[128,4096]{1,0:T(8,128)(2,1)S(1)} %copy-done.1), custom_call_target="tpu_custom_call" | custom-call | tf_op jit(solution)/shard_map/pallas_call | solution.py:104
  97.0 1.0 copy.25
  98.0 0.7 copy.26
  98.7 0.7 copy.27
Async XLA Ops:
  0.6 2.2 %copy-start = (bf16[4096,512]{1,0:T(8,128)(2,1)S(1)}, bf16[4096,512]{1,0:T(8,128)(2,1)}, u32[]{:S(2)}) copy-start(bf16[4096,512]{1,0:T(8,128)(2,1)} %proj_ref.3) | copy-start | bytes 12582916
  2.8 1.2 %copy-start.2 = (bf16[128,4096]{1,0:T(8,128)(2,1)S(1)}, bf16[128,4096]{1,0:T(8,128)(2,1)}, u32[]{:S(2)}) copy-start(bf16[128,4096]{1,0:T(8,128)(2,1)} %acts_ref.1) | copy-start | bytes 3145732
  4.0 8.7 %copy-start.5 = (bf16[512,4096]{1,0:T(8,128)(2,1)S(1)}, bf16[512,4096]{1,0:T(8,128)(2,1)}, u32[]{:S(2)}) copy-start(bf16[512,4096]{1,0:T(8,128)(2,1)} %param.7) | copy-start | bytes 12582916
  15.1 60.5 %copy-start.1 = (bf16[128,4096]{1,0:T(8,128)(2,1)S(1)}, bf16[128,4096]{1,0:T(8,128)(2,1)}, u32[]{:S(2)}) copy-start(bf16[128,4096]{1,0:T(8,128)(2,1)} %weight_ref.1) | copy-start | bytes 3145732
  15.2 60.5 %copy-start.3 = (f32[1,128,512]{2,1,0:T(8,128)S(1)}, f32[1,128,512]{2,1,0:T(8,128)}, u32[]{:S(2)}) copy-start(f32[1,128,512]{2,1,0:T(8,128)} %param.10) | copy-start | bytes 786436
  15.2 60.5 %copy-start.4 = (f32[1,128,512]{2,1,0:T(8,128)S(1)}, f32[1,128,512]{2,1,0:T(8,128)}, u32[]{:S(2)}) copy-start(f32[1,128,512]{2,1,0:T(8,128)} %param.11) | copy-start | bytes 786436

commit v17 on v16

--- a/solution.py
+++ b/solution.py
@@ -127,7 +127,8 @@
 
 
 def chip_gather_kernel(
-    acts_ref, proj_ref, hi_ref, q_buf, send_buf, recv, local_sem, send_sem, recv_sem
+    acts_ref, proj_ref, hi_ref, acts_v, proj_v, q_acc, q_buf, send_buf, recv,
+    load_sem, local_sem, send_sem, recv_sem,
 ):
     me = lax.axis_index("tensor")
     core_peer = me + 1 - 2 * lax.rem(me, 2)
@@ -135,9 +136,26 @@
     barrier = pltpu.get_barrier_semaphore()
     for peer in (core_peer, chip_peer):
         pl.semaphore_signal(barrier, inc=1, device_id={"tensor": peer}, device_id_type=MESH_ID)
-    q_buf[...] = jnp.dot(acts_ref[...], proj_ref[...], preferred_element_type=jnp.float32).astype(
-        jnp.bfloat16
-    )
+    chunks = proj_v.shape[0]
+    depth = proj_v.shape[1]
+    loads = [pltpu.make_async_copy(acts_ref, acts_v, load_sem.at[chunks])]
+    for i in range(chunks):
+        loads.append(
+            pltpu.make_async_copy(proj_ref.at[pl.ds(i * depth, depth)], proj_v.at[i], load_sem.at[i])
+        )
+    for load in loads:
+        load.start()
+    loads[0].wait()
+    for i in range(chunks):
+        loads[i + 1].wait()
+        term = jnp.dot(
+            acts_v[:, pl.ds(i * depth, depth)], proj_v[i], preferred_element_type=jnp.float32
+        )
+        if i == 0:
+            q_acc[...] = term
+        else:
+            q_acc[...] += term
+    q_buf[...] = q_acc[...].astype(jnp.bfloat16)
     local = pltpu.make_async_copy(q_buf, send_buf, local_sem)
     local.start()
     local.wait()
@@ -179,16 +197,23 @@
 
 def chip_gather(acts, projector):
     shape = (acts.shape[0], projector.shape[1])
+    chunks = 4
+    depth = projector.shape[0] // chunks
     vmem = pl.BlockSpec(memory_space=pltpu.VMEM)
+    hbm = pl.BlockSpec(memory_space=pl.ANY)
     return pl.pallas_call(
         chip_gather_kernel,
         out_shape=jax.ShapeDtypeStruct((4,) + shape, jnp.bfloat16),
-        in_specs=[vmem, vmem],
+        in_specs=[hbm, hbm],
         out_specs=vmem,
         scratch_shapes=[
+            pltpu.VMEM(acts.shape, acts.dtype),
+            pltpu.VMEM((chunks, depth, shape[1]), projector.dtype),
+            pltpu.VMEM(shape, jnp.float32),
             pltpu.VMEM(shape, jnp.bfloat16),
             pltpu.VMEM(shape, jnp.bfloat16),
             pltpu.VMEM((3,) + shape, jnp.bfloat16),
+            pltpu.SemaphoreType.DMA((chunks + 1,)),
             pltpu.SemaphoreType.DMA(()),
             pltpu.SemaphoreType.DMA((3, 2)),
             pltpu.SemaphoreType.DMA((3, 2)),

time: 101 us -> 101 us (level)
  no operation moved by 1% of the time
where the time goes in v17:
time: 101 us; the launch traced here: 99.9 us
  blocking collectives  60.4 us (60%)
  Pallas kernels  30.7 us (30%)
  local copies, waits for them, and re-layouts  5.81 us (6%)
  matrix products  2.38 us (2%)
    all_to_all x1, blocking collectives, per_device(): lax.all_to_all(partial.astype(jnp.bfloat16), 'dp', split_axis=0, concat_a...  60.4 us
    pallas_call x1, Pallas kernels, tail(): pl.pallas_call(functools.partial(tail_kernel, n), out_shape=(jax.ShapeDty...  21.4 us
    pallas_call x1, Pallas kernels, chip_gather(): pl.pallas_call(chip_gather_kernel, out_shape=jax.ShapeDtypeStruct((4,) +...  9.29 us
    unnamed x15, local copies, waits for them, and re-layouts  5.81 us
    dot_general x1, matrix products, per_device(): lax.dot_general(grad_blocks, proj_hi, dims, preferred_element_type=jnp.fl...  2.38 us

profile of v17, /device:TPU:0, one launch (start us, length us, event | category | flops | bytes accessed | tf_op | source)
XLA Modules:
  0.0 99.9 jit_solution(74987187880468069)
XLA Ops:
  0.6 0.0 copy-start
  0.6 2.2 %copy-done = bf16[4096,512]{1,0:T(8,128)(2,1)S(1)} copy-done((bf16[4096,512]{1,0:T(8,128)(2,1)S(1)}, bf16[4096,512]{1,0:T(8,128)(2,1)}, u32[]{:S(2)}) %copy-start) | copy-done | bytes 4194328
  2.8 0.0 copy-start.2
  2.8 1.2 %copy-done.2 = bf16[128,4096]{1,0:T(8,128)(2,1)S(1)} copy-done((bf16[128,4096]{1,0:T(8,128)(2,1)S(1)}, bf16[128,4096]{1,0:T(8,128)(2,1)}, u32[]{:S(2)}) %copy-start.2) | copy-done | bytes 1048600
  4.0 0.0 copy-start.5
  4.0 9.3 %shard_map.85 = bf16[4,128,512]{2,1,0:T(8,128)(2,1)S(1)} custom-call(bf16[128,4096]{1,0:T(8,128)(2,1)S(1)} %copy-done.2, bf16[4096,512]{1,0:T(8,128)(2,1)S(1)} %copy-done), custom_call_target="tpu_custom_call" | custom-call | tf_op jit(solution)/shard_map/pallas_call | solution.py:204
  13.3 0.0 copy-done.5
  13.4 2.4 %convert_bitcast_fusion = bf16[32,128,512]{2,1,0:T(8,128)(2,1)S(1)} fusion(bf16[512,512,1]{1,0,2:T(8,128)(2,1)S(1)} %bitcast.19, bf16[512,4096]{1,0:T(8,128)(2,1)S(1)} %copy-done.5), kind=kOutput, calls=%fused_computation.3 | convolution fusion | flops 2149580800 | bytes 8912896 | tf_op jit(solution)/shard_map/dot_general | solution.py:234
  15.7 0.0 copy-start.1
  15.8 0.0 copy-start.3
  15.8 0.0 copy-start.4
  15.8 60.4 %all_to_all.5.blocks_ref = bf16[32,128,512]{2,1,0:T(8,128)(2,1)} all-to-all(bf16[32,128,512]{2,1,0:T(8,128)(2,1)S(1)} %convert_bitcast_fusion), channel_id=1, replica_groups=mesh['dp'=32,'tensor'=4] {'dp'}, dimensions={0} | all-to-all | bytes 8388608 | tf_op jit(solution)/shard_map/all_to_all | solution.py:235
  76.1 0.0 copy-done.1
  76.1 0.0 copy-done.3
  76.2 0.0 copy-done.4
  76.2 21.4 %shard_map.86 = (bf16[128,4096]{1,0:T(8,128)(2,1)S(1)}, f32[128,512]{1,0:T(8,128)S(1)}, f32[128,512]{1,0:T(8,128)S(1)}) custom-call(bf16[32,128,512]{2,1,0:T(8,128)(2,1)} %all_to_all.5.blocks_ref, f32[128,512]{1,0:T(8,128)S(1)} %bitcast.20, f32[128,512]{1,0:T(8,128)S(1)} %bitcast.21, bf16[4096,512]{1,0:T(8,128)(2,1)} %proj_ref.3, bf16[128,4096]{1,0:T(8,128)(2,1)S(1)} %copy-done.1), custom_call_target="tpu_custom_call" | custom-call | tf_op jit(solution)/shard_map/pallas_call | solution.py:104
  97.5 1.0 copy.25
  98.5 0.7 copy.26
  99.2 0.7 copy.27
Async XLA Ops:
  0.6 2.2 %copy-start = (bf16[4096,512]{1,0:T(8,128)(2,1)S(1)}, bf16[4096,512]{1,0:T(8,128)(2,1)}, u32[]{:S(2)}) copy-start(bf16[4096,512]{1,0:T(8,128)(2,1)} %proj_ref.3) | copy-start | bytes 12582916
  2.8 1.2 %copy-start.2 = (bf16[128,4096]{1,0:T(8,128)(2,1)S(1)}, bf16[128,4096]{1,0:T(8,128)(2,1)}, u32[]{:S(2)}) copy-start(bf16[128,4096]{1,0:T(8,128)(2,1)} %acts_ref.1) | copy-start | bytes 3145732
  4.0 9.3 %copy-start.5 = (bf16[512,4096]{1,0:T(8,128)(2,1)S(1)}, bf16[512,4096]{1,0:T(8,128)(2,1)}, u32[]{:S(2)}) copy-start(bf16[512,4096]{1,0:T(8,128)(2,1)} %param.7) | copy-start | bytes 12582916
  15.7 60.4 %copy-start.1 = (bf16[128,4096]{1,0:T(8,128)(2,1)S(1)}, bf16[128,4096]{1,0:T(8,128)(2,1)}, u32[]{:S(2)}) copy-start(bf16[128,4096]{1,0:T(8,128)(2,1)} %weight_ref.1) | copy-start | bytes 3145732
  15.8 60.4 %copy-start.3 = (f32[1,128,512]{2,1,0:T(8,128)S(1)}, f32[1,128,512]{2,1,0:T(8,128)}, u32[]{:S(2)}) copy-start(f32[1,128,512]{2,1,0:T(8,128)} %param.10) | copy-start | bytes 786436
  15.8 60.4 %copy-start.4 = (f32[1,128,512]{2,1,0:T(8,128)S(1)}, f32[1,128,512]{2,1,0:T(8,128)}, u32[]{:S(2)}) copy-start(f32[1,128,512]{2,1,0:T(8,128)} %param.11) | copy-start | bytes 786436

commit v18 on v17

--- a/solution.py
+++ b/solution.py
@@ -218,9 +218,7 @@
             pltpu.SemaphoreType.DMA((3, 2)),
             pltpu.SemaphoreType.DMA((3, 2)),
         ],
-        compiler_params=pltpu.CompilerParams(
-            collective_id=1, has_side_effects=True, vmem_limit_bytes=48 * 1024 * 1024
-        ),
+        compiler_params=pltpu.CompilerParams(collective_id=1, has_side_effects=True),
     )(acts, projector)
 
 

time: 101 us -> 102 us (level)
  local copies, waits for them, and re-layouts: 5.81 us -> 2.4 us
  Pallas kernels: 30.7 us -> 33.1 us
  matrix products: 2.38 us -> 4.74 us
    unnamed x15 -> x9, local copies, waits for them, and re-layouts: 5.81 us -> 2.4 us
    pallas_call x1, Pallas kernels: 9.29 us -> 11.7 us  [chip_gather(): pl.pallas_call(chip_gather_kernel, out_shape=jax.ShapeDtypeStruct((4,) +...]
    dot_general x1, matrix products: 2.38 us -> 4.74 us  [per_device(): lax.dot_general(grad_blocks, proj_hi, dims, preferred_element_type=jnp.fl...]
where the time goes in v18:
time: 102 us; the launch traced here: 101 us
  blocking collectives  60.4 us (59%)
  Pallas kernels  33.1 us (32%)
  matrix products  4.74 us (5%)
  local copies, waits for them, and re-layouts  2.4 us (2%)
    all_to_all x1, blocking collectives, per_device(): lax.all_to_all(partial.astype(jnp.bfloat16), 'dp', split_axis=0, concat_a...  60.4 us
    pallas_call x1, Pallas kernels, tail(): pl.pallas_call(functools.partial(tail_kernel, n), out_shape=(jax.ShapeDty...  21.4 us
    pallas_call x1, Pallas kernels, chip_gather(): pl.pallas_call(chip_gather_kernel, out_shape=jax.ShapeDtypeStruct((4,) +...  11.7 us
    dot_general x1, matrix products, per_device(): lax.dot_general(grad_blocks, proj_hi, dims, preferred_element_type=jnp.fl...  4.74 us
    unnamed x9, local copies, waits for them, and re-layouts  2.4 us

profile of v18, /device:TPU:0, one launch (start us, length us, event | category | flops | bytes accessed | tf_op | source)
XLA Modules:
  0.0 101.2 jit_solution(6535041244607831893)
XLA Ops:
  0.6 11.7 %shard_map.85 = bf16[4,128,512]{2,1,0:T(8,128)(2,1)} custom-call(bf16[128,4096]{1,0:T(8,128)(2,1)} %acts_ref.1, bf16[4096,512]{1,0:T(8,128)(2,1)} %proj_ref.3), custom_call_target="tpu_custom_call" | custom-call | tf_op jit(solution)/shard_map/pallas_call | solution.py:204
  12.3 4.7 %convert_bitcast_fusion = bf16[32,128,512]{2,1,0:T(8,128)(2,1)S(1)} fusion(bf16[512,512,1]{1,0,2:T(8,128)(2,1)} %bitcast.23, bf16[512,4096]{1,0:T(8,128)(2,1)} %param.7), kind=kOutput, calls=%fused_computation.3 | convolution fusion | flops 2149580800 | bytes 8912896 | tf_op jit(solution)/shard_map/dot_general | solution.py:232
  17.1 0.0 copy-start
  17.1 0.0 copy-start.1
  17.1 0.0 copy-start.2
  17.1 60.4 %all_to_all.5.blocks_ref = bf16[32,128,512]{2,1,0:T(8,128)(2,1)} all-to-all(bf16[32,128,512]{2,1,0:T(8,128)(2,1)S(1)} %convert_bitcast_fusion), channel_id=1, replica_groups=mesh['dp'=32,'tensor'=4] {'dp'}, dimensions={0} | all-to-all | bytes 8388608 | tf_op jit(solution)/shard_map/all_to_all | solution.py:233
  77.5 0.0 copy-done
  77.5 0.0 copy-done.1
  77.5 0.0 copy-done.2
  77.5 21.4 %shard_map.86 = (bf16[128,4096]{1,0:T(8,128)(2,1)S(1)}, f32[128,512]{1,0:T(8,128)S(1)}, f32[128,512]{1,0:T(8,128)S(1)}) custom-call(bf16[32,128,512]{2,1,0:T(8,128)(2,1)} %all_to_all.5.blocks_ref, f32[128,512]{1,0:T(8,128)S(1)} %bitcast.19, f32[128,512]{1,0:T(8,128)S(1)} %bitcast.20, bf16[4096,512]{1,0:T(8,128)(2,1)} %proj_ref.3, bf16[128,4096]{1,0:T(8,128)(2,1)S(1)} %copy-done), custom_call_target="tpu_custom_call" | custom-call | tf_op jit(solution)/shard_map/pallas_call | solution.py:104
  98.9 1.0 copy.25
  99.8 0.7 copy.26
  100.5 0.7 copy.27
Async XLA Ops:
  17.1 60.4 %copy-start = (bf16[128,4096]{1,0:T(8,128)(2,1)S(1)}, bf16[128,4096]{1,0:T(8,128)(2,1)}, u32[]{:S(2)}) copy-start(bf16[128,4096]{1,0:T(8,128)(2,1)} %weight_ref.1) | copy-start | bytes 3145732
  17.1 60.4 %copy-start.1 = (f32[1,128,512]{2,1,0:T(8,128)S(1)}, f32[1,128,512]{2,1,0:T(8,128)}, u32[]{:S(2)}) copy-start(f32[1,128,512]{2,1,0:T(8,128)} %param.10) | copy-start | bytes 786436
  17.1 60.4 %copy-start.2 = (f32[1,128,512]{2,1,0:T(8,128)S(1)}, f32[1,128,512]{2,1,0:T(8,128)}, u32[]{:S(2)}) copy-start(f32[1,128,512]{2,1,0:T(8,128)} %param.11) | copy-start | bytes 786436

commit v19 on v16

--- a/solution.py
+++ b/solution.py
@@ -28,7 +28,7 @@
 def tail_kernel(
     n, blocks_ref, first_ref, second_ref, proj_ref, weight_ref,
     new_weight_ref, new_first_ref, new_second_ref,
-    total, direction_ref, update, sendbuf, recv, local_sem, send_sem, recv_sem,
+    blocks_v, direction_ref, update, sendbuf, recv, load_sem, local_sem, send_sem, recv_sem,
 ):
     me = lax.axis_index("dp")
     col = lax.axis_index("tensor")
@@ -41,12 +41,22 @@
         )
 
     band = 16
+    groups = 4
+    span = blocks_v.shape[1] // groups
+    loads = []
+    for g in range(groups):
+        rows_g = pl.ds(g * span, span)
+        load = pltpu.make_async_copy(
+            blocks_ref.at[:, rows_g, :], blocks_v.at[:, rows_g, :], load_sem.at[g]
+        )
+        load.start()
+        loads.append(load)
 
     def rows_step(r, carry):
         rs = pl.ds(pl.multiple_of(r * band, band), band)
-        lowgrad = blocks_ref[0, rs, :].astype(jnp.float32)
+        lowgrad = blocks_v[0, rs, :].astype(jnp.float32)
         for k in range(1, n):
-            lowgrad += blocks_ref[k, rs, :].astype(jnp.float32)
+            lowgrad += blocks_v[k, rs, :].astype(jnp.float32)
         new_first, new_second, direction = adam_moments(
             lowgrad, first_ref[rs, :], second_ref[rs, :]
         )
@@ -55,7 +65,9 @@
         direction_ref[rs, :] = direction
         return carry
 
-    lax.fori_loop(0, blocks_ref.shape[1] // band, rows_step, 0)
+    for g in range(groups):
+        loads[g].wait()
+        lax.fori_loop(g * span // band, (g + 1) * span // band, rows_step, 0)
 
     update[...] = (
         lax.dot_general(
@@ -108,14 +120,15 @@
             jax.ShapeDtypeStruct((hidden, rank), jnp.float32),
             jax.ShapeDtypeStruct((hidden, rank), jnp.float32),
         ),
-        in_specs=[vmem] * 5,
+        in_specs=[pl.BlockSpec(memory_space=pl.ANY)] + [vmem] * 4,
         out_specs=(vmem, vmem, vmem),
         scratch_shapes=[
-            pltpu.VMEM((hidden, rank), jnp.float32),
+            pltpu.VMEM(blocks.shape, blocks.dtype),
             pltpu.VMEM((hidden, rank), jnp.bfloat16),
             pltpu.VMEM((n, rows, hidden), jnp.bfloat16),
             pltpu.VMEM((n, rows, hidden), jnp.bfloat16),
             pltpu.VMEM((n, rows, hidden), jnp.bfloat16),
+            pltpu.SemaphoreType.DMA((4,)),
             pltpu.SemaphoreType.DMA(()),
             pltpu.SemaphoreType.DMA((n,)),
             pltpu.SemaphoreType.DMA((n,)),

time: 101 us -> 98.4 us (0.974); the launches traced: 99.4 us -> 98.2 us
  Pallas kernels: 30.1 us -> 28.9 us
    pallas_call x1, Pallas kernels: 21.4 us -> 20.2 us  [tail(): pl.pallas_call(functools.partial(tail_kernel, n), out_shape=(jax.ShapeDty...]
where the time goes in v19:
time: 98.4 us; the launch traced here: 98.2 us
  blocking collectives  60.4 us (61%)
  Pallas kernels  28.9 us (29%)
  local copies, waits for them, and re-layouts  5.81 us (6%)
  matrix products  2.38 us (2%)
    all_to_all x1, blocking collectives, per_device(): lax.all_to_all(partial.astype(jnp.bfloat16), 'dp', split_axis=0, concat_a...  60.4 us
    pallas_call x1, Pallas kernels, tail(): pl.pallas_call(functools.partial(tail_kernel, n), out_shape=(jax.ShapeDty...  20.2 us
    pallas_call x1, Pallas kernels, chip_gather(): pl.pallas_call(chip_gather_kernel, out_shape=jax.ShapeDtypeStruct((4,) +...  8.69 us
    unnamed x15, local copies, waits for them, and re-layouts  5.81 us
    dot_general x1, matrix products, per_device(): lax.dot_general(grad_blocks, proj_hi, dims, preferred_element_type=jnp.fl...  2.38 us

profile of v19, /device:TPU:0, one launch (start us, length us, event | category | flops | bytes accessed | tf_op | source)
XLA Modules:
  0.0 98.2 jit_solution(11391714874917704155)
XLA Ops:
  0.6 0.0 copy-start
  0.6 2.2 %copy-done = bf16[4096,512]{1,0:T(8,128)(2,1)S(1)} copy-done((bf16[4096,512]{1,0:T(8,128)(2,1)S(1)}, bf16[4096,512]{1,0:T(8,128)(2,1)}, u32[]{:S(2)}) %copy-start) | copy-done | bytes 4194328
  2.8 0.0 copy-start.2
  2.8 1.2 %copy-done.2 = bf16[128,4096]{1,0:T(8,128)(2,1)S(1)} copy-done((bf16[128,4096]{1,0:T(8,128)(2,1)S(1)}, bf16[128,4096]{1,0:T(8,128)(2,1)}, u32[]{:S(2)}) %copy-start.2) | copy-done | bytes 1048600
  4.0 0.0 copy-start.5
  4.0 8.7 %shard_map.85 = bf16[4,128,512]{2,1,0:T(8,128)(2,1)S(1)} custom-call(bf16[128,4096]{1,0:T(8,128)(2,1)S(1)} %copy-done.2, bf16[4096,512]{1,0:T(8,128)(2,1)S(1)} %copy-done), custom_call_target="tpu_custom_call" | custom-call | tf_op jit(solution)/shard_map/pallas_call | solution.py:196
  12.7 0.0 copy-done.5
  12.8 2.4 %convert_bitcast_fusion = bf16[32,128,512]{2,1,0:T(8,128)(2,1)S(1)} fusion(bf16[512,512,1]{1,0,2:T(8,128)(2,1)S(1)} %bitcast.19, bf16[512,4096]{1,0:T(8,128)(2,1)S(1)} %copy-done.5), kind=kOutput, calls=%fused_computation.3 | convolution fusion | flops 2149580800 | bytes 8912896 | tf_op jit(solution)/shard_map/dot_general | solution.py:222
  15.1 0.0 copy-start.1
  15.2 0.0 copy-start.3
  15.2 0.0 copy-start.4
  15.2 60.4 %all_to_all.5.blocks_ref = bf16[32,128,512]{2,1,0:T(8,128)(2,1)} all-to-all(bf16[32,128,512]{2,1,0:T(8,128)(2,1)S(1)} %convert_bitcast_fusion), channel_id=1, replica_groups=mesh['dp'=32,'tensor'=4] {'dp'}, dimensions={0} | all-to-all | bytes 8388608 | tf_op jit(solution)/shard_map/all_to_all | solution.py:223
  75.6 0.0 copy-done.1
  75.6 0.0 copy-done.3
  75.6 0.0 copy-done.4
  75.6 20.2 %shard_map.86 = (bf16[128,4096]{1,0:T(8,128)(2,1)S(1)}, f32[128,512]{1,0:T(8,128)S(1)}, f32[128,512]{1,0:T(8,128)S(1)}) custom-call(bf16[32,128,512]{2,1,0:T(8,128)(2,1)} %all_to_all.5.blocks_ref, f32[128,512]{1,0:T(8,128)S(1)} %bitcast.20, f32[128,512]{1,0:T(8,128)S(1)} %bitcast.21, bf16[4096,512]{1,0:T(8,128)(2,1)} %proj_ref.3, bf16[128,4096]{1,0:T(8,128)(2,1)S(1)} %copy-done.1), custom_call_target="tpu_custom_call" | custom-call | tf_op jit(solution)/shard_map/pallas_call | solution.py:116
  95.8 1.0 copy.25
  96.8 0.7 copy.26
  97.5 0.7 copy.27
Async XLA Ops:
  0.6 2.2 %copy-start = (bf16[4096,512]{1,0:T(8,128)(2,1)S(1)}, bf16[4096,512]{1,0:T(8,128)(2,1)}, u32[]{:S(2)}) copy-start(bf16[4096,512]{1,0:T(8,128)(2,1)} %proj_ref.3) | copy-start | bytes 12582916
  2.8 1.2 %copy-start.2 = (bf16[128,4096]{1,0:T(8,128)(2,1)S(1)}, bf16[128,4096]{1,0:T(8,128)(2,1)}, u32[]{:S(2)}) copy-start(bf16[128,4096]{1,0:T(8,128)(2,1)} %acts_ref.1) | copy-start | bytes 3145732
  4.0 8.7 %copy-start.5 = (bf16[512,4096]{1,0:T(8,128)(2,1)S(1)}, bf16[512,4096]{1,0:T(8,128)(2,1)}, u32[]{:S(2)}) copy-start(bf16[512,4096]{1,0:T(8,128)(2,1)} %param.7) | copy-start | bytes 12582916
  15.1 60.5 %copy-start.1 = (bf16[128,4096]{1,0:T(8,128)(2,1)S(1)}, bf16[128,4096]{1,0:T(8,128)(2,1)}, u32[]{:S(2)}) copy-start(bf16[128,4096]{1,0:T(8,128)(2,1)} %weight_ref.1) | copy-start | bytes 3145732
  15.2 60.5 %copy-start.3 = (f32[1,128,512]{2,1,0:T(8,128)S(1)}, f32[1,128,512]{2,1,0:T(8,128)}, u32[]{:S(2)}) copy-start(f32[1,128,512]{2,1,0:T(8,128)} %param.10) | copy-start | bytes 786436
  15.2 60.5 %copy-start.4 = (f32[1,128,512]{2,1,0:T(8,128)S(1)}, f32[1,128,512]{2,1,0:T(8,128)}, u32[]{:S(2)}) copy-start(f32[1,128,512]{2,1,0:T(8,128)} %param.11) | copy-start | bytes 786436

commit v20 on v19

--- a/solution.py
+++ b/solution.py
@@ -139,21 +139,14 @@
     )(blocks, first_moment, second_moment, projector, weight)
 
 
-def chip_gather_kernel(
-    acts_ref, proj_ref, hi_ref, q_buf, send_buf, recv, local_sem, send_sem, recv_sem
-):
+def chip_gather_kernel(q_ref, hi_ref, recv, send_sem, recv_sem):
     me = lax.axis_index("tensor")
     core_peer = me + 1 - 2 * lax.rem(me, 2)
     chip_peer = lax.rem(me + 2, 4)
     barrier = pltpu.get_barrier_semaphore()
     for peer in (core_peer, chip_peer):
         pl.semaphore_signal(barrier, inc=1, device_id={"tensor": peer}, device_id_type=MESH_ID)
-    q_buf[...] = jnp.dot(acts_ref[...], proj_ref[...], preferred_element_type=jnp.float32).astype(
-        jnp.bfloat16
-    )
-    local = pltpu.make_async_copy(q_buf, send_buf, local_sem)
-    local.start()
-    local.wait()
+    send_buf = q_ref
     pl.semaphore_wait(barrier, 2)
 
     half = send_buf.shape[0] // 2
@@ -190,31 +183,26 @@
     split(3 - me, recv[2])
 
 
-def chip_gather(acts, projector):
-    shape = (acts.shape[0], projector.shape[1])
+def chip_gather(q):
     vmem = pl.BlockSpec(memory_space=pltpu.VMEM)
     return pl.pallas_call(
         chip_gather_kernel,
-        out_shape=jax.ShapeDtypeStruct((4,) + shape, jnp.bfloat16),
-        in_specs=[vmem, vmem],
+        out_shape=jax.ShapeDtypeStruct((4,) + q.shape, q.dtype),
+        in_specs=[vmem],
         out_specs=vmem,
         scratch_shapes=[
-            pltpu.VMEM(shape, jnp.bfloat16),
-            pltpu.VMEM(shape, jnp.bfloat16),
-            pltpu.VMEM((3,) + shape, jnp.bfloat16),
-            pltpu.SemaphoreType.DMA(()),
+            pltpu.VMEM((3,) + q.shape, q.dtype),
             pltpu.SemaphoreType.DMA((3, 2)),
             pltpu.SemaphoreType.DMA((3, 2)),
         ],
-        compiler_params=pltpu.CompilerParams(
-            collective_id=1, has_side_effects=True, vmem_limit_bytes=48 * 1024 * 1024
-        ),
-    )(acts, projector)
+        compiler_params=pltpu.CompilerParams(collective_id=1, has_side_effects=True),
+    )(q)
 
 
 def per_device(acts, out_grad, projector, weight, first_moment, second_moment):
     assert lax.axis_size("tensor") == 4
-    proj_hi = chip_gather(acts, projector)
+    token_proj = jnp.dot(acts, projector, preferred_element_type=jnp.float32)
+    proj_hi = chip_gather(token_proj.astype(jnp.bfloat16))
     proj_hi = proj_hi.reshape(-1, proj_hi.shape[2])
     owners = lax.axis_size("dp")
     grad_blocks = out_grad.reshape(out_grad.shape[0], owners, -1)

time: 98.4 us -> 104 us (1.057)
  matrix products: 2.38 us -> 8.3 us
  local copies, waits for them, and re-layouts: 5.81 us -> 3.62 us
  Pallas kernels: 28.9 us -> 30.3 us
    dot_general x0 -> x1, matrix products: none -> 3.56 us  [per_device(): token_proj = jnp.dot(acts, projector, preferred_element_type=jnp.float32)]
    dot_general x1, matrix products: 2.38 us -> 4.74 us  [per_device(): lax.dot_general(grad_blocks, proj_hi, dims, preferred_element_type=jnp.fl...]
    unnamed x15 -> x11, local copies, waits for them, and re-layouts: 5.81 us -> 3.62 us
    pallas_call x1, Pallas kernels: 8.69 us -> 10.2 us  [chip_gather(): pl.pallas_call(chip_gather_kernel, out_shape=jax.ShapeDtypeStruct((4,) +...]
where the time goes in v20:
time: 104 us
  blocking collectives  60.6 us (58%)
  Pallas kernels  30.3 us (29%)
  matrix products  8.3 us (8%)
  local copies, waits for them, and re-layouts  3.62 us (3%)
    all_to_all x1, blocking collectives, per_device(): lax.all_to_all(partial.astype(jnp.bfloat16), 'dp', split_axis=0, concat_a...  60.6 us
    pallas_call x1, Pallas kernels, tail(): pl.pallas_call(functools.partial(tail_kernel, n), out_shape=(jax.ShapeDty...  20.2 us
    pallas_call x1, Pallas kernels, chip_gather(): pl.pallas_call(chip_gather_kernel, out_shape=jax.ShapeDtypeStruct((4,) +...  10.2 us
    dot_general x1, matrix products, per_device(): lax.dot_general(grad_blocks, proj_hi, dims, preferred_element_type=jnp.fl...  4.74 us
    unnamed x11, local copies, waits for them, and re-layouts  3.62 us
    dot_general x1, matrix products, per_device(): token_proj = jnp.dot(acts, projector, preferred_element_type=jnp.float32)  3.56 us

profile of v20, /device:TPU:0, one launch (start us, length us, event | category | flops | bytes accessed | tf_op | source)
XLA Modules:
  0.0 103.6 jit_solution(9712761146559578617)
XLA Ops:
  0.6 0.0 copy-start
  0.6 1.2 %copy-done = bf16[128,4096]{1,0:T(8,128)(2,1)S(1)} copy-done((bf16[128,4096]{1,0:T(8,128)(2,1)S(1)}, bf16[128,4096]{1,0:T(8,128)(2,1)}, u32[]{:S(2)}) %copy-start) | copy-done | bytes 1048600
  1.9 3.6 %convolution_convert_fusion.q_ref = bf16[128,512]{1,0:T(8,128)(2,1)} fusion(bf16[128,4096]{1,0:T(8,128)(2,1)S(1)} %copy-done, bf16[4096,512]{1,0:T(8,128)(2,1)} %proj_ref.1), kind=kOutput, calls=%fused_computation.4 | convolution fusion | flops 536936448 | bytes 5373952 | tf_op jit(solution)/shard_map/dot_general | solution.py:204
  5.4 10.2 %shard_map.85 = bf16[4,128,512]{2,1,0:T(8,128)(2,1)} custom-call(bf16[128,512]{1,0:T(8,128)(2,1)} %convolution_convert_fusion.q_ref), custom_call_target="tpu_custom_call" | custom-call | tf_op jit(solution)/shard_map/pallas_call | solution.py:188
  15.6 4.7 %convert_bitcast_fusion = bf16[32,128,512]{2,1,0:T(8,128)(2,1)S(1)} fusion(bf16[512,512,1]{1,0,2:T(8,128)(2,1)} %bitcast.25, bf16[512,4096]{1,0:T(8,128)(2,1)} %param.7), kind=kOutput, calls=%fused_computation.3 | convolution fusion | flops 2149580800 | bytes 8912896 | tf_op jit(solution)/shard_map/dot_general | solution.py:210
  20.3 0.0 copy-start.1
  20.4 0.0 copy-start.2
  20.4 0.0 copy-start.3
  20.4 60.6 %all_to_all.5.blocks_ref = bf16[32,128,512]{2,1,0:T(8,128)(2,1)} all-to-all(bf16[32,128,512]{2,1,0:T(8,128)(2,1)S(1)} %convert_bitcast_fusion), channel_id=1, replica_groups=mesh['dp'=32,'tensor'=4] {'dp'}, dimensions={0} | all-to-all | bytes 8388608 | tf_op jit(solution)/shard_map/all_to_all | solution.py:211
  81.0 0.0 copy-done.1
  81.0 0.0 copy-done.2
  81.0 0.0 copy-done.3
  81.0 20.2 %shard_map.86 = (bf16[128,4096]{1,0:T(8,128)(2,1)S(1)}, f32[128,512]{1,0:T(8,128)S(1)}, f32[128,512]{1,0:T(8,128)S(1)}) custom-call(bf16[32,128,512]{2,1,0:T(8,128)(2,1)} %all_to_all.5.blocks_ref, f32[128,512]{1,0:T(8,128)S(1)} %bitcast.21, f32[128,512]{1,0:T(8,128)S(1)} %bitcast.22, bf16[4096,512]{1,0:T(8,128)(2,1)} %proj_ref.1, bf16[128,4096]{1,0:T(8,128)(2,1)S(1)} %copy-done.1), custom_call_target="tpu_custom_call" | custom-call | tf_op jit(solution)/shard_map/pallas_call | solution.py:116
  101.2 1.0 copy.25
  102.2 0.7 copy.26
  102.9 0.7 copy.27
Async XLA Ops:
  0.6 1.2 %copy-start = (bf16[128,4096]{1,0:T(8,128)(2,1)S(1)}, bf16[128,4096]{1,0:T(8,128)(2,1)}, u32[]{:S(2)}) copy-start(bf16[128,4096]{1,0:T(8,128)(2,1)} %param.6) | copy-start | bytes 3145732
  20.3 60.7 %copy-start.1 = (bf16[128,4096]{1,0:T(8,128)(2,1)S(1)}, bf16[128,4096]{1,0:T(8,128)(2,1)}, u32[]{:S(2)}) copy-start(bf16[128,4096]{1,0:T(8,128)(2,1)} %weight_ref.1) | copy-start | bytes 3145732
  20.4 60.7 %copy-start.2 = (f32[1,128,512]{2,1,0:T(8,128)S(1)}, f32[1,128,512]{2,1,0:T(8,128)}, u32[]{:S(2)}) copy-start(f32[1,128,512]{2,1,0:T(8,128)} %param.10) | copy-start | bytes 786436
  20.4 60.7 %copy-start.3 = (f32[1,128,512]{2,1,0:T(8,128)S(1)}, f32[1,128,512]{2,1,0:T(8,128)}, u32[]{:S(2)}) copy-start(f32[1,128,512]{2,1,0:T(8,128)} %param.11) | copy-start | bytes 786436

commit v21 on v19

--- a/solution.py
+++ b/solution.py
@@ -40,8 +40,8 @@
             barrier, inc=1, device_id=(lax.rem(me + k, n), col), device_id_type=MESH_ID
         )
 
-    band = 16
-    groups = 4
+    band = 32
+    groups = 8
     span = blocks_v.shape[1] // groups
     loads = []
     for g in range(groups):
@@ -128,7 +128,7 @@
             pltpu.VMEM((n, rows, hidden), jnp.bfloat16),
             pltpu.VMEM((n, rows, hidden), jnp.bfloat16),
             pltpu.VMEM((n, rows, hidden), jnp.bfloat16),
-            pltpu.SemaphoreType.DMA((4,)),
+            pltpu.SemaphoreType.DMA((8,)),
             pltpu.SemaphoreType.DMA(()),
             pltpu.SemaphoreType.DMA((n,)),
             pltpu.SemaphoreType.DMA((n,)),
@@ -156,15 +156,12 @@
     local.wait()
     pl.semaphore_wait(barrier, 2)
 
-    half = send_buf.shape[0] // 2
-
-    def send(src, slot, peer, p):
-        span = pl.ds(p * half, half)
+    def send(src, slot, peer):
         copy = pltpu.make_async_remote_copy(
-            src_ref=src.at[span],
-            dst_ref=recv.at[slot, span],
-            send_sem=send_sem.at[slot, p],
-            recv_sem=recv_sem.at[slot, p],
+            src_ref=src,
+            dst_ref=recv.at[slot],
+            send_sem=send_sem.at[slot],
+            recv_sem=recv_sem.at[slot],
             device_id={"tensor": peer},
             device_id_type=MESH_ID,
         )
@@ -174,19 +171,15 @@
     def split(slot, piece):
         hi_ref[slot] = piece
 
-    across = [send(send_buf, 1, chip_peer, p) for p in range(2)]
-    beside = [send(send_buf, 0, core_peer, p) for p in range(2)]
+    across = send(send_buf, 1, chip_peer)
+    beside = send(send_buf, 0, core_peer)
     split(me, send_buf[...])
-    forward = []
-    for p in range(2):
-        across[p].wait()
-        forward.append(send(recv.at[1], 2, core_peer, p))
+    across.wait()
+    forward = send(recv.at[1], 2, core_peer)
     split(chip_peer, recv[1])
-    for copy in beside:
-        copy.wait()
+    beside.wait()
     split(core_peer, recv[0])
-    for copy in forward:
-        copy.wait()
+    forward.wait()
     split(3 - me, recv[2])
 
 
@@ -203,8 +196,8 @@
             pltpu.VMEM(shape, jnp.bfloat16),
             pltpu.VMEM((3,) + shape, jnp.bfloat16),
             pltpu.SemaphoreType.DMA(()),
-            pltpu.SemaphoreType.DMA((3, 2)),
-            pltpu.SemaphoreType.DMA((3, 2)),
+            pltpu.SemaphoreType.DMA((3,)),
+            pltpu.SemaphoreType.DMA((3,)),
         ],
         compiler_params=pltpu.CompilerParams(
             collective_id=1, has_side_effects=True, vmem_limit_bytes=48 * 1024 * 1024

time: 98.4 us -> 98.5 us (level)
  no operation moved by 1% of the time
where the time goes in v21:
time: 98.5 us; the launch traced here: 98.2 us
  blocking collectives  60.4 us (61%)
  Pallas kernels  28.9 us (29%)
  local copies, waits for them, and re-layouts  5.81 us (6%)
  matrix products  2.38 us (2%)
    all_to_all x1, blocking collectives, per_device(): lax.all_to_all(partial.astype(jnp.bfloat16), 'dp', split_axis=0, concat_a...  60.4 us
    pallas_call x1, Pallas kernels, tail(): pl.pallas_call(functools.partial(tail_kernel, n), out_shape=(jax.ShapeDty...  20.1 us
    pallas_call x1, Pallas kernels, chip_gather(): pl.pallas_call(chip_gather_kernel, out_shape=jax.ShapeDtypeStruct((4,) +...  8.72 us
    unnamed x15, local copies, waits for them, and re-layouts  5.81 us
    dot_general x1, matrix products, per_device(): lax.dot_general(grad_blocks, proj_hi, dims, preferred_element_type=jnp.fl...  2.38 us

profile of v21, /device:TPU:0, one launch (start us, length us, event | category | flops | bytes accessed | tf_op | source)
XLA Modules:
  0.0 98.2 jit_solution(11788196595774237895)
XLA Ops:
  0.6 0.0 copy-start
  0.6 2.2 %copy-done = bf16[4096,512]{1,0:T(8,128)(2,1)S(1)} copy-done((bf16[4096,512]{1,0:T(8,128)(2,1)S(1)}, bf16[4096,512]{1,0:T(8,128)(2,1)}, u32[]{:S(2)}) %copy-start) | copy-done | bytes 4194328
  2.8 0.0 copy-start.2
  2.8 1.2 %copy-done.2 = bf16[128,4096]{1,0:T(8,128)(2,1)S(1)} copy-done((bf16[128,4096]{1,0:T(8,128)(2,1)S(1)}, bf16[128,4096]{1,0:T(8,128)(2,1)}, u32[]{:S(2)}) %copy-start.2) | copy-done | bytes 1048600
  4.0 0.0 copy-start.5
  4.0 8.7 %shard_map.85 = bf16[4,128,512]{2,1,0:T(8,128)(2,1)S(1)} custom-call(bf16[128,4096]{1,0:T(8,128)(2,1)S(1)} %copy-done.2, bf16[4096,512]{1,0:T(8,128)(2,1)S(1)} %copy-done), custom_call_target="tpu_custom_call" | custom-call | tf_op jit(solution)/shard_map/pallas_call | solution.py:189
  12.8 0.0 copy-done.5
  12.8 2.4 %convert_bitcast_fusion = bf16[32,128,512]{2,1,0:T(8,128)(2,1)S(1)} fusion(bf16[512,512,1]{1,0,2:T(8,128)(2,1)S(1)} %bitcast.19, bf16[512,4096]{1,0:T(8,128)(2,1)S(1)} %copy-done.5), kind=kOutput, calls=%fused_computation.3 | convolution fusion | flops 2149580800 | bytes 8912896 | tf_op jit(solution)/shard_map/dot_general | solution.py:215
  15.2 0.0 copy-start.1
  15.2 0.0 copy-start.3
  15.2 0.0 copy-start.4
  15.2 60.4 %all_to_all.5.blocks_ref = bf16[32,128,512]{2,1,0:T(8,128)(2,1)} all-to-all(bf16[32,128,512]{2,1,0:T(8,128)(2,1)S(1)} %convert_bitcast_fusion), channel_id=1, replica_groups=mesh['dp'=32,'tensor'=4] {'dp'}, dimensions={0} | all-to-all | bytes 8388608 | tf_op jit(solution)/shard_map/all_to_all | solution.py:216
  75.7 0.0 copy-done.1
  75.7 0.0 copy-done.3
  75.7 0.0 copy-done.4
  75.7 20.1 %shard_map.86 = (bf16[128,4096]{1,0:T(8,128)(2,1)S(1)}, f32[128,512]{1,0:T(8,128)S(1)}, f32[128,512]{1,0:T(8,128)S(1)}) custom-call(bf16[32,128,512]{2,1,0:T(8,128)(2,1)} %all_to_all.5.blocks_ref, f32[128,512]{1,0:T(8,128)S(1)} %bitcast.20, f32[128,512]{1,0:T(8,128)S(1)} %bitcast.21, bf16[4096,512]{1,0:T(8,128)(2,1)} %proj_ref.3, bf16[128,4096]{1,0:T(8,128)(2,1)S(1)} %copy-done.1), custom_call_target="tpu_custom_call" | custom-call | tf_op jit(solution)/shard_map/pallas_call | solution.py:116
  95.8 1.0 copy.25
  96.8 0.7 copy.26
  97.5 0.7 copy.27
Async XLA Ops:
  0.6 2.2 %copy-start = (bf16[4096,512]{1,0:T(8,128)(2,1)S(1)}, bf16[4096,512]{1,0:T(8,128)(2,1)}, u32[]{:S(2)}) copy-start(bf16[4096,512]{1,0:T(8,128)(2,1)} %proj_ref.3) | copy-start | bytes 12582916
  2.8 1.2 %copy-start.2 = (bf16[128,4096]{1,0:T(8,128)(2,1)S(1)}, bf16[128,4096]{1,0:T(8,128)(2,1)}, u32[]{:S(2)}) copy-start(bf16[128,4096]{1,0:T(8,128)(2,1)} %acts_ref.1) | copy-start | bytes 3145732
  4.0 8.7 %copy-start.5 = (bf16[512,4096]{1,0:T(8,128)(2,1)S(1)}, bf16[512,4096]{1,0:T(8,128)(2,1)}, u32[]{:S(2)}) copy-start(bf16[512,4096]{1,0:T(8,128)(2,1)} %param.7) | copy-start | bytes 12582916
  15.2 60.5 %copy-start.1 = (bf16[128,4096]{1,0:T(8,128)(2,1)S(1)}, bf16[128,4096]{1,0:T(8,128)(2,1)}, u32[]{:S(2)}) copy-start(bf16[128,4096]{1,0:T(8,128)(2,1)} %weight_ref.1) | copy-start | bytes 3145732
  15.2 60.5 %copy-start.3 = (f32[1,128,512]{2,1,0:T(8,128)S(1)}, f32[1,128,512]{2,1,0:T(8,128)}, u32[]{:S(2)}) copy-start(f32[1,128,512]{2,1,0:T(8,128)} %param.10) | copy-start | bytes 786436
  15.2 60.5 %copy-start.4 = (f32[1,128,512]{2,1,0:T(8,128)S(1)}, f32[1,128,512]{2,1,0:T(8,128)}, u32[]{:S(2)}) copy-start(f32[1,128,512]{2,1,0:T(8,128)} %param.11) | copy-start | bytes 786436

commit v22 on v19

--- a/solution.py
+++ b/solution.py
@@ -79,13 +79,17 @@
         .astype(jnp.bfloat16)
         .reshape(update.shape)
     )
-    local = pltpu.make_async_copy(update, sendbuf, local_sem)
-    local.start()
-    local.wait()
     pl.semaphore_wait(barrier, n - 1)
+    locals_ = []
+    for k in range(n):
+        dest = lax.rem(me + k, n)
+        local = pltpu.make_async_copy(update.at[dest], sendbuf.at[dest], local_sem.at[k])
+        local.start()
+        locals_.append(local)
     copies = []
     for k in range(1, n):
         dest = lax.rem(me + k, n)
+        locals_[k].wait()
         copy = pltpu.make_async_remote_copy(
             src_ref=sendbuf.at[dest],
             dst_ref=recv.at[k],
@@ -96,6 +100,7 @@
         )
         copy.start()
         copies.append(copy)
+    locals_[0].wait()
 
     def apply(source, block):
         cols = pl.ds(pl.multiple_of(source * width, width), width)
@@ -129,7 +134,7 @@
             pltpu.VMEM((n, rows, hidden), jnp.bfloat16),
             pltpu.VMEM((n, rows, hidden), jnp.bfloat16),
             pltpu.SemaphoreType.DMA((4,)),
-            pltpu.SemaphoreType.DMA(()),
+            pltpu.SemaphoreType.DMA((n,)),
             pltpu.SemaphoreType.DMA((n,)),
             pltpu.SemaphoreType.DMA((n,)),
         ],

time: 98.4 us -> 100 us (1.016)
  Pallas kernels: 28.9 us -> 30.5 us
    pallas_call x1, Pallas kernels: 20.2 us -> 21.8 us  [tail(): pl.pallas_call(functools.partial(tail_kernel, n), out_shape=(jax.ShapeDty...]
where the time goes in v22:
time: 100 us; the launch traced here: 99.8 us
  blocking collectives  60.4 us (60%)
  Pallas kernels  30.5 us (30%)
  local copies, waits for them, and re-layouts  5.81 us (6%)
  matrix products  2.38 us (2%)
    all_to_all x1, blocking collectives, per_device(): lax.all_to_all(partial.astype(jnp.bfloat16), 'dp', split_axis=0, concat_a...  60.4 us
    pallas_call x1, Pallas kernels, tail(): pl.pallas_call(functools.partial(tail_kernel, n), out_shape=(jax.ShapeDty...  21.8 us
    pallas_call x1, Pallas kernels, chip_gather(): pl.pallas_call(chip_gather_kernel, out_shape=jax.ShapeDtypeStruct((4,) +...  8.69 us
    unnamed x15, local copies, waits for them, and re-layouts  5.81 us
    dot_general x1, matrix products, per_device(): lax.dot_general(grad_blocks, proj_hi, dims, preferred_element_type=jnp.fl...  2.38 us

profile of v22, /device:TPU:0, one launch (start us, length us, event | category | flops | bytes accessed | tf_op | source)
XLA Modules:
  0.0 99.8 jit_solution(11516574576965113851)
XLA Ops:
  0.6 0.0 copy-start
  0.6 2.2 %copy-done = bf16[4096,512]{1,0:T(8,128)(2,1)S(1)} copy-done((bf16[4096,512]{1,0:T(8,128)(2,1)S(1)}, bf16[4096,512]{1,0:T(8,128)(2,1)}, u32[]{:S(2)}) %copy-start) | copy-done | bytes 4194328
  2.8 0.0 copy-start.2
  2.8 1.2 %copy-done.2 = bf16[128,4096]{1,0:T(8,128)(2,1)S(1)} copy-done((bf16[128,4096]{1,0:T(8,128)(2,1)S(1)}, bf16[128,4096]{1,0:T(8,128)(2,1)}, u32[]{:S(2)}) %copy-start.2) | copy-done | bytes 1048600
  4.0 0.0 copy-start.5
  4.0 8.7 %shard_map.85 = bf16[4,128,512]{2,1,0:T(8,128)(2,1)S(1)} custom-call(bf16[128,4096]{1,0:T(8,128)(2,1)S(1)} %copy-done.2, bf16[4096,512]{1,0:T(8,128)(2,1)S(1)} %copy-done), custom_call_target="tpu_custom_call" | custom-call | tf_op jit(solution)/shard_map/pallas_call | solution.py:201
  12.7 0.0 copy-done.5
  12.8 2.4 %convert_bitcast_fusion = bf16[32,128,512]{2,1,0:T(8,128)(2,1)S(1)} fusion(bf16[512,512,1]{1,0,2:T(8,128)(2,1)S(1)} %bitcast.19, bf16[512,4096]{1,0:T(8,128)(2,1)S(1)} %copy-done.5), kind=kOutput, calls=%fused_computation.3 | convolution fusion | flops 2149580800 | bytes 8912896 | tf_op jit(solution)/shard_map/dot_general | solution.py:227
  15.1 0.0 copy-start.1
  15.2 0.0 copy-start.3
  15.2 0.0 copy-start.4
  15.2 60.4 %all_to_all.5.blocks_ref = bf16[32,128,512]{2,1,0:T(8,128)(2,1)} all-to-all(bf16[32,128,512]{2,1,0:T(8,128)(2,1)S(1)} %convert_bitcast_fusion), channel_id=1, replica_groups=mesh['dp'=32,'tensor'=4] {'dp'}, dimensions={0} | all-to-all | bytes 8388608 | tf_op jit(solution)/shard_map/all_to_all | solution.py:228
  75.6 0.0 copy-done.1
  75.6 0.0 copy-done.3
  75.6 0.0 copy-done.4
  75.6 21.8 %shard_map.86 = (bf16[128,4096]{1,0:T(8,128)(2,1)S(1)}, f32[128,512]{1,0:T(8,128)S(1)}, f32[128,512]{1,0:T(8,128)S(1)}) custom-call(bf16[32,128,512]{2,1,0:T(8,128)(2,1)} %all_to_all.5.blocks_ref, f32[128,512]{1,0:T(8,128)S(1)} %bitcast.20, f32[128,512]{1,0:T(8,128)S(1)} %bitcast.21, bf16[4096,512]{1,0:T(8,128)(2,1)} %proj_ref.3, bf16[128,4096]{1,0:T(8,128)(2,1)S(1)} %copy-done.1), custom_call_target="tpu_custom_call" | custom-call | tf_op jit(solution)/shard_map/pallas_call | solution.py:121
  97.5 1.0 copy.25
  98.4 0.7 copy.26
  99.1 0.7 copy.27
Async XLA Ops:
  0.6 2.2 %copy-start = (bf16[4096,512]{1,0:T(8,128)(2,1)S(1)}, bf16[4096,512]{1,0:T(8,128)(2,1)}, u32[]{:S(2)}) copy-start(bf16[4096,512]{1,0:T(8,128)(2,1)} %proj_ref.3) | copy-start | bytes 12582916
  2.8 1.2 %copy-start.2 = (bf16[128,4096]{1,0:T(8,128)(2,1)S(1)}, bf16[128,4096]{1,0:T(8,128)(2,1)}, u32[]{:S(2)}) copy-start(bf16[128,4096]{1,0:T(8,128)(2,1)} %acts_ref.1) | copy-start | bytes 3145732
  4.0 8.7 %copy-start.5 = (bf16[512,4096]{1,0:T(8,128)(2,1)S(1)}, bf16[512,4096]{1,0:T(8,128)(2,1)}, u32[]{:S(2)}) copy-start(bf16[512,4096]{1,0:T(8,128)(2,1)} %param.7) | copy-start | bytes 12582916
  15.1 60.5 %copy-start.1 = (bf16[128,4096]{1,0:T(8,128)(2,1)S(1)}, bf16[128,4096]{1,0:T(8,128)(2,1)}, u32[]{:S(2)}) copy-start(bf16[128,4096]{1,0:T(8,128)(2,1)} %weight_ref.1) | copy-start | bytes 3145732
  15.2 60.5 %copy-start.3 = (f32[1,128,512]{2,1,0:T(8,128)S(1)}, f32[1,128,512]{2,1,0:T(8,128)}, u32[]{:S(2)}) copy-start(f32[1,128,512]{2,1,0:T(8,128)} %param.10) | copy-start | bytes 786436
  15.2 60.5 %copy-start.4 = (f32[1,128,512]{2,1,0:T(8,128)S(1)}, f32[1,128,512]{2,1,0:T(8,128)}, u32[]{:S(2)}) copy-start(f32[1,128,512]{2,1,0:T(8,128)} %param.11) | copy-start | bytes 786436

commit v23 on v19

--- a/solution.py
+++ b/solution.py
@@ -28,7 +28,7 @@
 def tail_kernel(
     n, blocks_ref, first_ref, second_ref, proj_ref, weight_ref,
     new_weight_ref, new_first_ref, new_second_ref,
-    blocks_v, direction_ref, update, sendbuf, recv, load_sem, local_sem, send_sem, recv_sem,
+    blocks_v, total, direction_ref, update, sendbuf, recv, load_sem, local_sem, send_sem, recv_sem,
 ):
     me = lax.axis_index("dp")
     col = lax.axis_index("tensor")
@@ -42,32 +42,39 @@
 
     band = 16
     groups = 4
-    span = blocks_v.shape[1] // groups
+    per = n // groups
     loads = []
     for g in range(groups):
-        rows_g = pl.ds(g * span, span)
         load = pltpu.make_async_copy(
-            blocks_ref.at[:, rows_g, :], blocks_v.at[:, rows_g, :], load_sem.at[g]
+            blocks_ref.at[pl.ds(g * per, per)], blocks_v.at[pl.ds(g * per, per)], load_sem.at[g]
         )
         load.start()
         loads.append(load)
 
-    def rows_step(r, carry):
-        rs = pl.ds(pl.multiple_of(r * band, band), band)
-        lowgrad = blocks_v[0, rs, :].astype(jnp.float32)
-        for k in range(1, n):
-            lowgrad += blocks_v[k, rs, :].astype(jnp.float32)
-        new_first, new_second, direction = adam_moments(
-            lowgrad, first_ref[rs, :], second_ref[rs, :]
-        )
-        new_first_ref[rs, :] = new_first
-        new_second_ref[rs, :] = new_second
-        direction_ref[rs, :] = direction
-        return carry
+    def group_step(g, last):
+        def rows_step(r, carry):
+            rs = pl.ds(pl.multiple_of(r * band, band), band)
+            lowgrad = blocks_v[g * per, rs, :].astype(jnp.float32)
+            for k in range(g * per + 1, (g + 1) * per):
+                lowgrad += blocks_v[k, rs, :].astype(jnp.float32)
+            if g > 0:
+                lowgrad += total[rs, :]
+            if not last:
+                total[rs, :] = lowgrad
+                return carry
+            new_first, new_second, direction = adam_moments(
+                lowgrad, first_ref[rs, :], second_ref[rs, :]
+            )
+            new_first_ref[rs, :] = new_first
+            new_second_ref[rs, :] = new_second
+            direction_ref[rs, :] = direction
+            return carry
+
+        lax.fori_loop(0, blocks_v.shape[1] // band, rows_step, 0)
 
     for g in range(groups):
         loads[g].wait()
-        lax.fori_loop(g * span // band, (g + 1) * span // band, rows_step, 0)
+        group_step(g, g == groups - 1)
 
     update[...] = (
         lax.dot_general(
@@ -124,6 +131,7 @@
         out_specs=(vmem, vmem, vmem),
         scratch_shapes=[
             pltpu.VMEM(blocks.shape, blocks.dtype),
+            pltpu.VMEM((hidden, rank), jnp.float32),
             pltpu.VMEM((hidden, rank), jnp.bfloat16),
             pltpu.VMEM((n, rows, hidden), jnp.bfloat16),
             pltpu.VMEM((n, rows, hidden), jnp.bfloat16),

time: 98.4 us -> 98.9 us (level)
  no operation moved by 1% of the time
where the time goes in v23:
time: 98.9 us; the launch traced here: 98.7 us
  blocking collectives  60.4 us (61%)
  Pallas kernels  29.3 us (30%)
  local copies, waits for them, and re-layouts  5.81 us (6%)
  matrix products  2.38 us (2%)
    all_to_all x1, blocking collectives, per_device(): lax.all_to_all(partial.astype(jnp.bfloat16), 'dp', split_axis=0, concat_a...  60.4 us
    pallas_call x1, Pallas kernels, tail(): pl.pallas_call(functools.partial(tail_kernel, n), out_shape=(jax.ShapeDty...  20.7 us
    pallas_call x1, Pallas kernels, chip_gather(): pl.pallas_call(chip_gather_kernel, out_shape=jax.ShapeDtypeStruct((4,) +...  8.69 us
    unnamed x15, local copies, waits for them, and re-layouts  5.81 us
    dot_general x1, matrix products, per_device(): lax.dot_general(grad_blocks, proj_hi, dims, preferred_element_type=jnp.fl...  2.38 us

profile of v23, /device:TPU:0, one launch (start us, length us, event | category | flops | bytes accessed | tf_op | source)
XLA Modules:
  0.0 98.7 jit_solution(11602204956585831401)
XLA Ops:
  0.6 0.0 copy-start
  0.6 2.2 %copy-done = bf16[4096,512]{1,0:T(8,128)(2,1)S(1)} copy-done((bf16[4096,512]{1,0:T(8,128)(2,1)S(1)}, bf16[4096,512]{1,0:T(8,128)(2,1)}, u32[]{:S(2)}) %copy-start) | copy-done | bytes 4194328
  2.8 0.0 copy-start.2
  2.8 1.2 %copy-done.2 = bf16[128,4096]{1,0:T(8,128)(2,1)S(1)} copy-done((bf16[128,4096]{1,0:T(8,128)(2,1)S(1)}, bf16[128,4096]{1,0:T(8,128)(2,1)}, u32[]{:S(2)}) %copy-start.2) | copy-done | bytes 1048600
  4.0 0.0 copy-start.5
  4.0 8.7 %shard_map.85 = bf16[4,128,512]{2,1,0:T(8,128)(2,1)S(1)} custom-call(bf16[128,4096]{1,0:T(8,128)(2,1)S(1)} %copy-done.2, bf16[4096,512]{1,0:T(8,128)(2,1)S(1)} %copy-done), custom_call_target="tpu_custom_call" | custom-call | tf_op jit(solution)/shard_map/pallas_call | solution.py:204
  12.7 0.0 copy-done.5
  12.8 2.4 %convert_bitcast_fusion = bf16[32,128,512]{2,1,0:T(8,128)(2,1)S(1)} fusion(bf16[512,512,1]{1,0,2:T(8,128)(2,1)S(1)} %bitcast.19, bf16[512,4096]{1,0:T(8,128)(2,1)S(1)} %copy-done.5), kind=kOutput, calls=%fused_computation.3 | convolution fusion | flops 2149580800 | bytes 8912896 | tf_op jit(solution)/shard_map/dot_general | solution.py:230
  15.1 0.0 copy-start.1
  15.2 0.0 copy-start.3
  15.2 0.0 copy-start.4
  15.2 60.4 %all_to_all.5.blocks_ref = bf16[32,128,512]{2,1,0:T(8,128)(2,1)} all-to-all(bf16[32,128,512]{2,1,0:T(8,128)(2,1)S(1)} %convert_bitcast_fusion), channel_id=1, replica_groups=mesh['dp'=32,'tensor'=4] {'dp'}, dimensions={0} | all-to-all | bytes 8388608 | tf_op jit(solution)/shard_map/all_to_all | solution.py:231
  75.6 0.0 copy-done.1
  75.6 0.0 copy-done.3
  75.6 0.0 copy-done.4
  75.6 20.7 %shard_map.86 = (bf16[128,4096]{1,0:T(8,128)(2,1)S(1)}, f32[128,512]{1,0:T(8,128)S(1)}, f32[128,512]{1,0:T(8,128)S(1)}) custom-call(bf16[32,128,512]{2,1,0:T(8,128)(2,1)} %all_to_all.5.blocks_ref, f32[128,512]{1,0:T(8,128)S(1)} %bitcast.20, f32[128,512]{1,0:T(8,128)S(1)} %bitcast.21, bf16[4096,512]{1,0:T(8,128)(2,1)} %proj_ref.3, bf16[128,4096]{1,0:T(8,128)(2,1)S(1)} %copy-done.1), custom_call_target="tpu_custom_call" | custom-call | tf_op jit(solution)/shard_map/pallas_call | solution.py:123
  96.3 1.0 copy.25
  97.3 0.7 copy.26
  98.0 0.7 copy.27
Async XLA Ops:
  0.6 2.2 %copy-start = (bf16[4096,512]{1,0:T(8,128)(2,1)S(1)}, bf16[4096,512]{1,0:T(8,128)(2,1)}, u32[]{:S(2)}) copy-start(bf16[4096,512]{1,0:T(8,128)(2,1)} %proj_ref.3) | copy-start | bytes 12582916
  2.8 1.2 %copy-start.2 = (bf16[128,4096]{1,0:T(8,128)(2,1)S(1)}, bf16[128,4096]{1,0:T(8,128)(2,1)}, u32[]{:S(2)}) copy-start(bf16[128,4096]{1,0:T(8,128)(2,1)} %acts_ref.1) | copy-start | bytes 3145732
  4.0 8.7 %copy-start.5 = (bf16[512,4096]{1,0:T(8,128)(2,1)S(1)}, bf16[512,4096]{1,0:T(8,128)(2,1)}, u32[]{:S(2)}) copy-start(bf16[512,4096]{1,0:T(8,128)(2,1)} %param.7) | copy-start | bytes 12582916
  15.1 60.5 %copy-start.1 = (bf16[128,4096]{1,0:T(8,128)(2,1)S(1)}, bf16[128,4096]{1,0:T(8,128)(2,1)}, u32[]{:S(2)}) copy-start(bf16[128,4096]{1,0:T(8,128)(2,1)} %weight_ref.1) | copy-start | bytes 3145732
  15.2 60.5 %copy-start.3 = (f32[1,128,512]{2,1,0:T(8,128)S(1)}, f32[1,128,512]{2,1,0:T(8,128)}, u32[]{:S(2)}) copy-start(f32[1,128,512]{2,1,0:T(8,128)} %param.10) | copy-start | bytes 786436
  15.2 60.5 %copy-start.4 = (f32[1,128,512]{2,1,0:T(8,128)S(1)}, f32[1,128,512]{2,1,0:T(8,128)}, u32[]{:S(2)}) copy-start(f32[1,128,512]{2,1,0:T(8,128)} %param.11) | copy-start | bytes 786436
